TPU v7x, 32 devices: a whole 2x2x4 slice. The times are simulated.
32 devices in a mesh: rows: 8 (over y, x, core), cols: 4 (over z).
Axes of the slice: x: 2, y: 2, z: 4, core: 2. Of those that a mesh axis runs over, the one named last changes fastest.
Arguments:
- field: bfloat16 [32, 512, 512], P(None, 'rows', 'cols'), may hold values from -6 to 6
- cotangent: bfloat16 [32, 512, 512], P(None, 'rows', 'cols'), may hold values from -6 to 6
- weight_real: bfloat16 [32, 32, 8192], P(None, None, ('rows', 'cols')), may hold values from -0.75 to 0.75
- weight_imag: bfloat16 [32, 32, 8192], P(None, None, ('rows', 'cols')), may hold values from -0.75 to 0.75
- kernel: bfloat16 [3, 3, 32, 32], replicated, may hold values from -0.375 to 0.375
Outputs:
- layer_out: bfloat16 [32, 512, 512], P(None, 'rows', 'cols')
- field_grad: bfloat16 [32, 512, 512], P(None, 'rows', 'cols')
- weight_grad_real: float32 [32, 32, 8192], P(None, None, ('rows', 'cols'))
- weight_grad_imag: float32 [32, 32, 8192], P(None, None, ('rows', 'cols'))
- kernel_grad: float32 [3, 3, 32, 32], replicated
All inputs are finite; a program needn't handle non-finite values.
Results may differ from a plain program's by a relative error of at most 0.0068.
Values may be sent and summed in bfloat16 or wider, within the bound.
No kernel may reach another device: no remote copies, remote signals or barrier semaphores. Data moves between devices by JAX's collectives and lax.ppermute only.
A program may use at most 128 MiB of HBM per device.

v0:
```python
import math

import jax
import jax.numpy as jnp
from jax import lax
from jax.sharding import PartitionSpec as P

M = 64


highest = lax.Precision.HIGHEST


def padded_2(x, sides, width):
    for axis, dim in sides:
        devices, length = (lax.axis_size(axis), x.shape[dim])
        up = [(i, (i + 1) % devices) for i in range(devices - 1)]
        down = [(j, i) for i, j in up]
        last = lax.slice_in_dim(x, length - width, length, axis=dim)
        initial = lax.slice_in_dim(x, 0, width, axis=dim)
        before = lax.ppermute(last, axis, up)
        after = lax.ppermute(initial, axis, down)
        x = jnp.concatenate([before, x, after], axis=dim)
    return x


def tables(count_modes, offset, local, total):
    modes = jnp.arange(count_modes, dtype=jnp.int32)
    cells = offset + jnp.arange(local, dtype=jnp.int32)
    phase = modes[:, None] * cells[None, :] % total
    angle = phase.astype(jnp.float32) * (2.0 * math.pi / total)
    return (jnp.cos(angle), jnp.sin(angle))


def row_tables(count_modes, offset, local, total):
    base = jnp.arange(count_modes, dtype=jnp.int32)
    modes = jnp.concatenate([base, total - count_modes + base])
    cells = offset + jnp.arange(local, dtype=jnp.int32)
    phase = modes[:, None] * cells[None, :] % total
    angle = phase.astype(jnp.float32) * (2.0 * math.pi / total)
    return (jnp.cos(angle), jnp.sin(angle))


def exact(form, left, right):
    return jnp.einsum(form, left, right, precision=highest, preferred_element_type=jnp.float32)


def quick(form, left, right):
    return jnp.einsum(form, left, right, preferred_element_type=jnp.float32)


def smooth(values):
    return jax.nn.gelu(values, approximate=True)


def stencil(padded, weights):
    return lax.conv_general_dilated(
        padded[None], weights, (1, 1), ((0, 0), (0, 0)), preferred_element_type=jnp.float32
    )[0]


def owner_sums(partials):
    return lax.psum_scatter(partials, ("rows", "cols"), scatter_dimension=2, tiled=True)


def spread(owned):
    return lax.all_gather(owned, ("rows", "cols"), axis=2, tiled=True)


def rims(cells):
    return padded_2(cells, (("rows", 1), ("cols", 2)), 1)


def body(field, cotangent, weight_real, weight_imag, kernel):
    channels, rows_here, cols_here = field.shape
    total_rows = rows_here * lax.axis_size("rows")
    total_cols = cols_here * lax.axis_size("cols")
    cos_rows, sin_rows = row_tables(M, lax.axis_index("rows") * rows_here, rows_here, total_rows)
    cos_cols, sin_cols = tables(M, lax.axis_index("cols") * cols_here, cols_here, total_cols)
    scale_rows = 1.0 / math.sqrt(total_rows)
    scale_cols = 1.0 / math.sqrt(total_cols)
    scale_cells = 1.0 / math.sqrt(total_rows * total_cols)
    cos_cols_half = (cos_cols * scale_cols).astype(jnp.bfloat16)
    sin_cols_half = (-(sin_cols * scale_cols)).astype(jnp.bfloat16)
    half_real = quick("cij,bj->cib", field, cos_cols_half)
    half_imag = quick("cij,bj->cib", field, sin_cols_half)
    cos_rows_scaled = cos_rows * scale_rows
    sin_rows_scaled = sin_rows * scale_rows
    part_real = exact("ai,cib->cab", cos_rows_scaled, half_real) + exact(
        "ai,cib->cab", sin_rows_scaled, half_imag
    )
    part_imag = exact("ai,cib->cab", cos_rows_scaled, half_imag) - exact(
        "ai,cib->cab", sin_rows_scaled, half_real
    )
    owned = owner_sums(jnp.stack([part_real, part_imag]).reshape(2, channels, 2 * M * M))
    coef_real = owned[0]
    coef_imag = owned[1]
    wide_real = weight_real.astype(jnp.float32)
    wide_imag = weight_imag.astype(jnp.float32)
    mixed_real = exact("cm,com->om", coef_real, wide_real) - exact(
        "cm,com->om", coef_imag, wide_imag
    )
    mixed_imag = exact("cm,com->om", coef_real, wide_imag) + exact(
        "cm,com->om", coef_imag, wide_real
    )
    mixed = jnp.stack([mixed_real, mixed_imag]).astype(jnp.bfloat16)
    spectrum = spread(mixed).reshape(2, channels, 2 * M, M)
    cos_rows_half = cos_rows.astype(jnp.bfloat16)
    sin_rows_half = sin_rows.astype(jnp.bfloat16)
    back_real = quick("ai,oab->oib", cos_rows_half, spectrum[0]) - quick(
        "ai,oab->oib", sin_rows_half, spectrum[1]
    )
    back_imag = quick("ai,oab->oib", cos_rows_half, spectrum[1]) + quick(
        "ai,oab->oib", sin_rows_half, spectrum[0]
    )
    spectral = (
        exact("oib,bj->oij", back_real, cos_cols) - exact("oib,bj->oij", back_imag, sin_cols)
    ) / M
    padded = rims(field)
    forward_weights = jnp.transpose(kernel, (3, 2, 0, 1))
    preact = spectral + stencil(padded, forward_weights)
    activated, pullback = jax.vjp(smooth, preact)
    grad_pre = pullback(cotangent.astype(jnp.float32))[0].astype(jnp.bfloat16)
    cos_cols_plain = cos_cols.astype(jnp.bfloat16)
    sin_cols_plain = sin_cols.astype(jnp.bfloat16)
    grad_back_real = quick("oij,bj->oib", grad_pre, cos_cols_plain) / M
    grad_back_imag = -quick("oij,bj->oib", grad_pre, sin_cols_plain) / M
    grad_real = exact("ai,oib->oab", cos_rows, grad_back_real) + exact(
        "ai,oib->oab", sin_rows, grad_back_imag
    )
    grad_imag = exact("ai,oib->oab", cos_rows, grad_back_imag) - exact(
        "ai,oib->oab", sin_rows, grad_back_real
    )
    owned_grad = owner_sums(jnp.stack([grad_real, grad_imag]).reshape(2, channels, 2 * M * M))
    mode_real = owned_grad[0]
    mode_imag = owned_grad[1]
    weight_scale = M * scale_cells
    out_real = (
        coef_real[:, None, :] * mode_real[None] + coef_imag[:, None, :] * mode_imag[None]
    ) * weight_scale
    out_imag = (
        coef_real[:, None, :] * mode_imag[None] - coef_imag[:, None, :] * mode_real[None]
    ) * weight_scale
    input_real = exact("com,om->cm", wide_real, mode_real) + exact(
        "com,om->cm", wide_imag, mode_imag
    )
    input_imag = exact("com,om->cm", wide_real, mode_imag) - exact(
        "com,om->cm", wide_imag, mode_real
    )
    spectrum_grad = spread(jnp.stack([input_real, input_imag]).astype(jnp.bfloat16)).reshape(
        2, channels, 2 * M, M
    )
    cos_scaled_half = cos_rows_scaled.astype(jnp.bfloat16)
    sin_scaled_half = sin_rows_scaled.astype(jnp.bfloat16)
    line_real = quick("ai,cab->cib", cos_scaled_half, spectrum_grad[0]) - quick(
        "ai,cab->cib", sin_scaled_half, spectrum_grad[1]
    )
    line_imag = quick("ai,cab->cib", sin_scaled_half, spectrum_grad[0]) + quick(
        "ai,cab->cib", cos_scaled_half, spectrum_grad[1]
    )
    field_grad = exact("cib,bj->cij", line_real, cos_cols * scale_cols) - exact(
        "cib,bj->cij", line_imag, sin_cols * scale_cols
    )
    grad_padded = rims(grad_pre)
    backward_weights = jnp.transpose(kernel[::-1, ::-1], (2, 3, 0, 1))
    field_grad = field_grad + stencil(grad_padded, backward_weights)
    kernel_terms = []
    for row_step in range(3):
        for col_step in range(3):
            window = padded[:, row_step : row_step + rows_here, col_step : col_step + cols_here]
            kernel_terms.append(quick("cij,oij->co", window, grad_pre))
    kernel_local = jnp.stack(kernel_terms).reshape(3, 3, channels, channels)
    kernel_grad = lax.psum(kernel_local, ("rows", "cols")) * scale_cells
    return (
        activated.astype(jnp.bfloat16),
        field_grad.astype(jnp.bfloat16),
        out_real,
        out_imag,
        kernel_grad,
    )


def solution(mesh):
    placed = (
        P(None, "rows", "cols"),
        P(None, "rows", "cols"),
        P(None, None, ("rows", "cols")),
        P(None, None, ("rows", "cols")),
        P(),
    )
    return jax.shard_map(
        body,
        mesh=mesh,
        in_specs=placed,
        out_specs=(
            P(None, "rows", "cols"),
            P(None, "rows", "cols"),
            P(None, None, ("rows", "cols")),
            P(None, None, ("rows", "cols")),
            P(),
        ),
        check_vma=False,
    )
```

profile of v0, /device:TPU:0, one launch (start us, length us, event | category | flops | bytes accessed | tf_op | source)
XLA Modules:
  0.0 489.5 jit_solution(7288767995015641725)
XLA Ops:
  7.3 1.7 convolution_bitcast_fusion.1
  9.0 1.7 convolution_bitcast_fusion
  10.8 1.2 fusion.98
  11.9 1.2 fusion.100
  13.1 1.2 fusion.28
  14.3 2.1 fusion.29
  16.5 1.8 copy.175
  18.3 1.6 stack.72
  20.5 1.6 stack.73
  22.2 2.8 pad_maximum_fusion
  25.1 142.7 %reduce-scatter.3.cloned.1.call-done = f32[2,32,256]{2,1,0:T(8,128)} async-done(((f32[2,32,8192]{2,1,0:T(8,128)}), f32[2,32,256]{2,1,0:T(8,128)}) %reduce-scatter.3.cloned.1.call-update) | async-done | bytes 65552 | tf_op jit(solution)/shard_map/reduce_scatter | solution.py:63
  167.8 1.4 slice_bitcast_fusion.7
  170.7 1.3 collective-permute-start
  172.0 1.3 collective-permute-start.1
  173.7 1.4 collective-permute-done.1
  176.3 1.3 collective-permute-start.2
  178.3 1.5 collective-permute-start.3
  180.8 3.1 collective-permute-done.3
  185.5 2.7 copy.303
  188.3 1.4 pad.clone
  189.7 3.3 copy.192
  193.0 1.0 slice.124
  194.1 6.9 %broadcast_select_fusion.1 = f32[64,8,17,32]{3,1,2,0:T(8,128)} fusion(pred[8,17]{0,1:T(8,128)(4,1)S(1)} %copy-done.23, bf16[3,3,32,32]{3,2,1,0:T(8,128)(2,1)S(1)} %copy-done, bf16[32,66,1,7,2]{0,3,4,1,2:T(8,128)(2,1)S(1)} %slice.124, bf16[32,66,1,8,17]{0,3,4,1,2:T(8,128)(2,1)} %copy.192), kind=kOutput, calls=%fused_computation.16 | convolution fusion | flops 162636800 | bytes 1766280 | tf_op jit(solution)/shard_map/conv_general_dilated | solution.py:57
  201.0 4.4 copy.193
  205.4 1.5 slice.125
  206.9 3.7 copy.297
  210.7 10.7 %all-gather.3.cloned.1.call-done = bf16[2,32,8192]{2,1,0:T(8,128)(2,1)} async-done(((bf16[2,32,256]{2,1,0:T(8,128)(2,1)}), bf16[2,32,8192]{2,1,0:T(8,128)(2,1)}) %all-gather.3.cloned.1.call-update) | async-done | bytes 1048592 | tf_op jit(solution)/shard_map/all_gather | solution.py:67
  221.4 1.3 fusion.304
  222.7 1.1 squeeze.37
  223.8 1.1 squeeze.36
  226.9 1.8 fusion.94
  228.8 3.3 fusion.46
  233.0 1.8 fusion.91
  234.8 2.0 fusion.89
  236.8 2.8 fusion.24
  239.7 2.8 fusion.23
  242.5 1.8 copy.200
  244.3 1.6 stack.79
  246.0 1.8 copy.197
  247.8 1.6 stack.78
  249.4 3.0 pad_maximum_fusion.1
  253.2 2.1 collective-permute-start.4
  255.3 1.3 collective-permute-start.5
  260.7 132.0 %reduce-scatter.5.cloned.1.call-done = f32[2,32,256]{2,1,0:T(8,128)} async-done(((f32[2,32,8192]{2,1,0:T(8,128)}), f32[2,32,256]{2,1,0:T(8,128)}) %reduce-scatter.5.cloned.1.call-update) | async-done | bytes 65552 | tf_op jit(solution)/shard_map/reduce_scatter | solution.py:63
  392.7 1.4 slice_bitcast_fusion.3
  395.5 1.5 fusion.35
  397.7 39.6 %psum.7 = f32[3,3,32,32]{3,2,1,0:T(8,128)S(1)} all-reduce(f32[3,3,32,32]{3,2,1,0:T(8,128)S(1)} %bitcast.249), channel_id=1, replica_groups=mesh['rows'=8,'cols'=4] {'rows','cols'}, use_global_device_ids=true, to_apply=%region_2.3 | all-reduce | flops 9216 | bytes 73728 | tf_op jit(solution)/shard_map/psum | solution.py:173
  438.5 1.3 collective-permute-start.7
  439.8 5.4 %collective-permute-start.6 = (bf16[32,66,1]{1,0,2:T(8,128)(2,1)S(1)}, bf16[32,66,1]{1,0,2:T(8,128)(2,1)S(1)}, u32[]{:S(2)}, u32[]{:S(2)}) collective-permute-start(bf16[32,66,1]{1,0,2:T(8,128)(2,1)S(1)} %copy.207), channel_id=1, source_target_pairs={{0,1},{1,2},{2,3},{4,5},{5,6},{6,7},{8,9},{9,10},{10,11},{12,13},{... | collective-permute-start | bytes 12680 | tf_op jit(solution)/shard_map/ppermute | solution.py:21
  447.0 1.7 maximum_bitcast_fusion
  448.7 1.3 copy.304
  450.3 2.7 copy.213
  453.0 5.3 %broadcast_select_fusion = f32[64,8,17,32]{3,1,2,0:T(8,128)} fusion(pred[8,17]{0,1:T(8,128)(4,1)S(1)} %copy-done.24, bf16[3,3,32,32]{3,2,1,0:T(8,128)(2,1)S(1)} %copy-done, bf16[32,66,1,7,2]{0,3,4,1,2:T(8,128)(2,1)S(1)} %slice.134, bf16[32,66,1,8,17]{0,3,4,1,2:T(8,128)(2,1)S(1)} %copy.213), kind=kOutput, calls=%fused_computation.15 | convolution fusion | flops 162636800 | bytes 1766280 | tf_op jit(solution)/shard_map/conv_general_dilated | solution.py:57
  458.3 4.0 copy.214
  462.3 1.5 slice.135
  463.8 2.7 copy.298
  466.6 1.6 subtract_multiply_fusion
  468.2 2.1 fusion.303
  470.2 1.1 squeeze.41
  471.9 1.5 fusion.164
  473.4 2.3 squeeze.42
  475.7 1.7 fusion.22
  478.1 1.8 fusion.85
  479.9 2.7 fusion.32
  (115 shorter events, 21.2 us)
Async XLA Ops:
  7.2 186.9 %copy-start = (bf16[3,3,32,32]{3,2,1,0:T(8,128)(2,1)S(1)}, bf16[3,3,32,32]{3,2,1,0:T(8,128)(2,1)}, u32[]{:S(2)}) copy-start(bf16[3,3,32,32]{3,2,1,0:T(8,128)(2,1)} %param.9) | copy-start | bytes 55300
  7.2 160.6 %reduce-scatter.3.cloned.1.call-start = ((), (), s32[]{:S(2)}) async-start(), calls=%async_computation.2 | async-start | bytes 2162688 | tf_op jit(solution)/shard_map/reduce_scatter | solution.py:63
  7.3 225.3 %copy-start.19 = (s32[128]{0:T(128)}, s32[128]{0:T(128)S(1)}, u32[]{:S(2)}) copy-start(s32[128]{0:T(128)S(1)} %iota_add_fusion.2) | copy-start | bytes 1540
  20.5 1.6 copy-start.7
  25.0 144.2 %copy-start.8 = (bf16[32,32,256]{2,1,0:T(8,128)(2,1)S(1)}, bf16[32,32,256]{2,1,0:T(8,128)(2,1)}, u32[]{:S(2)}) copy-start(bf16[32,32,256]{2,1,0:T(8,128)(2,1)} %param.7) | copy-start | bytes 1572868
  25.0 144.2 %copy-start.10 = (bf16[32,32,256]{2,1,0:T(8,128)(2,1)S(1)}, bf16[32,32,256]{2,1,0:T(8,128)(2,1)}, u32[]{:S(2)}) copy-start(bf16[32,32,256]{2,1,0:T(8,128)(2,1)} %param.8) | copy-start | bytes 1572868
  25.0 145.3 %copy-start.1 = (bf16[32,64,128]{2,1,0:T(8,128)(2,1)S(1)}, bf16[32,64,128]{2,1,0:T(8,128)(2,1)}, u32[]{:S(2)}) copy-start(bf16[32,64,128]{2,1,0:T(8,128)(2,1)} %param.5) | copy-start | bytes 1572868
  25.0 196.4 %all-gather.3.cloned.1.call-start = ((), (), s32[]{:S(2)}) async-start(), calls=%async_computation.3 | async-start | bytes 1081344 | tf_op jit(solution)/shard_map/all_gather | solution.py:67
  170.2 222.4 %reduce-scatter.5.cloned.1.call-start = ((), (), s32[]{:S(2)}) async-start(), calls=%async_computation.4 | async-start | bytes 2162688 | tf_op jit(solution)/shard_map/reduce_scatter | solution.py:63
  170.6 4.4 copy-start.13
  170.7 2.6 collective-permute-start
  172.0 3.1 collective-permute-start.1
  175.0 0.6 copy-start.21
  176.3 3.5 collective-permute-start.2
  178.3 5.6 %collective-permute-start.3 = (bf16[32,66,1]{1,0,2:T(8,128)(2,1)S(1)}, bf16[32,66,1]{1,0,2:T(8,128)(2,1)S(1)}, u32[]{:S(2)}, u32[]{:S(2)}) collective-permute-start(bf16[32,66,1]{1,0,2:T(8,128)(2,1)S(1)} %copy.187), channel_id=1, source_target_pairs={{1,0},{2,1},{3,2},{5,4},{6,5},{7,6},{9,8},{10,9},{11,10},{13,12},{... | collective-permute-start | bytes 12680 | tf_op jit(solution)/shard_map/ppermute | solution.py:22
  180.8 7.5 %copy-start.5 = (bf16[32,66,1]{2,0,1:T(8,128)(2,1)}, bf16[32,66,1]{2,0,1:T(8,128)(2,1)S(1)}, u32[]{:S(2)}) copy-start(bf16[32,66,1]{2,0,1:T(8,128)(2,1)S(1)} %copy.188) | copy-start | bytes 12676
  184.8 3.4 copy-start.3
  189.7 4.4 copy-start.23
  226.4 2.4 copy-start.12
  226.4 2.4 copy-start.22
  252.5 4.2 copy-start.6
  252.5 4.7 copy-start.14
  252.5 5.1 %copy-start.4 = (bf16[32,66,1]{2,0,1:T(8,128)(2,1)S(1)}, bf16[32,66,1]{2,0,1:T(8,128)(2,1)}, u32[]{:S(2)}) copy-start(bf16[32,66,1]{2,0,1:T(8,128)(2,1)} %copy-done.3) | copy-start | bytes 12676
  252.5 215.7 %all-gather.5.cloned.1.call-start = ((), (), s32[]{:S(2)}) async-start(), calls=%async_computation.5 | async-start | bytes 1081344 | tf_op jit(solution)/shard_map/all_gather | solution.py:67
  253.2 184.1 %collective-permute-start.4 = (bf16[32,1,128]{2,1,0:T(2,128)(2,1)}, bf16[32,1,128]{2,1,0:T(2,128)(2,1)S(1)}, u32[]{:S(2)}, u32[]{:S(2)}) collective-permute-start(bf16[32,1,128]{2,1,0:T(2,128)(2,1)} %get-tuple-element.27), channel_id=1, source_target_pairs={{0,4},{4,8},{8,12},{12,16},{16,20},{20,24},{24,28},{1,5},{5,9},{9,... | collective-permute-start | bytes 24584 | tf_op jit(solution)/shard_map/ppermute | solution.py:21
  255.3 182.0 %collective-permute-start.5 = (bf16[32,1,128]{2,1,0:T(2,128)(2,1)}, bf16[32,1,128]{2,1,0:T(2,128)(2,1)S(1)}, u32[]{:S(2)}, u32[]{:S(2)}) collective-permute-start(bf16[32,1,128]{2,1,0:T(2,128)(2,1)} %get-tuple-element.28), channel_id=1, source_target_pairs={{4,0},{8,4},{12,8},{16,12},{20,16},{24,20},{28,24},{5,1},{9,5},{13... | collective-permute-start | bytes 24584 | tf_op jit(solution)/shard_map/ppermute | solution.py:22
  257.6 1.2 copy-start.2
  259.5 134.6 %copy-start.9 = (bf16[32,32,256]{2,1,0:T(8,128)(2,1)S(1)}, bf16[32,32,256]{2,1,0:T(8,128)(2,1)}, u32[]{:S(2)}) copy-start(bf16[32,32,256]{2,1,0:T(8,128)(2,1)} %param.7) | copy-start | bytes 1572868
  259.5 134.6 %copy-start.11 = (bf16[32,32,256]{2,1,0:T(8,128)(2,1)S(1)}, bf16[32,32,256]{2,1,0:T(8,128)(2,1)}, u32[]{:S(2)}) copy-start(bf16[32,32,256]{2,1,0:T(8,128)(2,1)} %param.8) | copy-start | bytes 1572868
  437.3 1.2 copy-start.18
  438.5 8.2 %collective-permute-start.7 = (bf16[32,66,1]{1,0,2:T(8,128)(2,1)S(1)}, bf16[32,66,1]{1,0,2:T(8,128)(2,1)S(1)}, u32[]{:S(2)}, u32[]{:S(2)}) collective-permute-start(bf16[32,66,1]{1,0,2:T(8,128)(2,1)S(1)} %copy.208), channel_id=1, source_target_pairs={{1,0},{2,1},{3,2},{5,4},{6,5},{7,6},{9,8},{10,9},{11,10},{13,12},{... | collective-permute-start | bytes 12680 | tf_op jit(solution)/shard_map/ppermute | solution.py:22
  439.8 6.5 %collective-permute-start.6 = (bf16[32,66,1]{1,0,2:T(8,128)(2,1)S(1)}, bf16[32,66,1]{1,0,2:T(8,128)(2,1)S(1)}, u32[]{:S(2)}, u32[]{:S(2)}) collective-permute-start(bf16[32,66,1]{1,0,2:T(8,128)(2,1)S(1)} %copy.207), channel_id=1, source_target_pairs={{0,1},{1,2},{2,3},{4,5},{5,6},{6,7},{8,9},{9,10},{10,11},{12,13},{... | collective-permute-start | bytes 12680 | tf_op jit(solution)/shard_map/ppermute | solution.py:21
  450.2 2.8 copy-start.24
  463.8 2.7 copy-start.15
  463.8 2.7 copy-start.16
  463.8 2.7 copy-start.17
  477.4 0.7 copy-start.20
Sparse Core Ops, SparseCore 0:
  25.1 142.6 reduce-scatter.2
  171.3 50.1 all-gather.2
  252.6 140.0 reduce-scatter.4
  395.7 50.0 all-gather.4
where the time goes:
time: 498 us; the launch traced here: 490 us
  waiting for transfers between devices  290 us (58%)
  local copies, waits for them, and re-layouts  62.2 us (12%)
  matrix products  53.5 us (11%)
  blocking collectives  39.6 us (8%)
  starting transfers between devices  15.6 us (3%)
  between operations  14.9 us (3%)
  other arithmetic  13.3 us (3%)
    reduce_scatter x2, waiting for transfers between devices, owner_sums(): lax.psum_scatter(partials, ('rows', 'cols'), scatter_dimension=2, tiled=T...  275 us
    psum x1, blocking collectives, body(): kernel_grad = lax.psum(kernel_local, ('rows', 'cols')) * scale_cells  39.6 us
    dot_general x12, matrix products, exact(): jnp.einsum(form, left, right, precision=highest, preferred_element_type=j...  24.8 us
    conv_general_dilated x8, local copies, waits for them, and re-layouts, stencil(): lax.conv_general_dilated(padded[None], weights, (1, 1), ((0, 0), (0, 0)),...  18.6 us
    dot_general x21, matrix products, quick(): return jnp.einsum(form, left, right, preferred_element_type=jnp.float32)  16.5 us
    conv_general_dilated x2, matrix products, stencil(): lax.conv_general_dilated(padded[None], weights, (1, 1), ((0, 0), (0, 0)),...  12.2 us
    unnamed x57, local copies, waits for them, and re-layouts  11.8 us
    all_gather x2, waiting for transfers between devices, spread(): return lax.all_gather(owned, ('rows', 'cols'), axis=2, tiled=True)  10.7 us
  transfers between devices with their start and end apart: 12, of which 6 were waited for; matrix products, arithmetic and copies ran while one was open for 13% of the time, Pallas kernels for 0%

commit v1 on v0

v1 whole, which is shorter than its diff:
```python
import functools
import math

import jax
import jax.numpy as jnp
import numpy as np
from jax import lax
from jax.experimental import pallas as pl
from jax.experimental.pallas import tpu as pltpu
from jax.sharding import PartitionSpec as P

M = 64
BLOCK = 8
f32 = jnp.float32
bf16 = jnp.bfloat16
BOTH = ("rows", "cols")


def dot(left, right):
    return jnp.dot(left, right, preferred_element_type=f32)


def dot_nt(left, right):
    return lax.dot_general(
        left, right, (((1,), (1,)), ((), ())), preferred_element_type=f32
    )


def call(kernel, out_shape, scratch, flops, moved, *args):
    return pl.pallas_call(
        kernel,
        out_shape=out_shape,
        in_specs=[pl.BlockSpec(memory_space=pltpu.VMEM)] * len(args),
        out_specs=jax.tree.map(lambda _: pl.BlockSpec(memory_space=pltpu.VMEM), out_shape),
        scratch_shapes=scratch,
        compiler_params=pltpu.CompilerParams(vmem_limit_bytes=40 << 20),
        cost_estimate=pl.CostEstimate(flops=flops, bytes_accessed=moved, transcendentals=0),
    )(*args)


def shape(dims, dtype):
    return jax.ShapeDtypeStruct(dims, dtype)


def row_angles(total, places):
    modes = np.concatenate([np.arange(M), total - M + np.arange(M)])
    phase = modes[:, None] * np.arange(total)[None, :] % total
    angle = phase * (2.0 * np.pi / total)
    local = total // places
    cut = lambda t: t.reshape(2 * M, places, local).transpose(1, 0, 2)
    return cut(np.cos(angle)), cut(np.sin(angle))


def col_angles(total, places):
    phase = np.arange(M)[:, None] * np.arange(total)[None, :] % total
    angle = phase * (2.0 * np.pi / total)
    local = total // places
    cut = lambda t: t.reshape(M, places, local).transpose(1, 0, 2)
    return cut(np.cos(angle)), cut(np.sin(angle))


def make_tables(rows_here, cols_here):
    places_rows, places_cols = lax.axis_size("rows"), lax.axis_size("cols")
    total_rows, total_cols = rows_here * places_rows, cols_here * places_cols
    cx, sx = row_angles(total_rows, places_rows)
    cy, sy = col_angles(total_cols, places_cols)
    scale_rows, scale_cols = 1.0 / math.sqrt(total_rows), 1.0 / math.sqrt(total_cols)
    turn = lambda t: t.transpose(0, 2, 1)

    def to_modes(c, s):
        return np.concatenate([turn(c), -turn(s), -turn(s), -turn(c)], axis=2)

    def to_cells(c, s):
        return np.concatenate([c, -s, -s, -c], axis=1)

    def rows_out(c, s):
        return np.concatenate([c, s], axis=2)

    def rows_back(c, s):
        return np.concatenate([turn(c), turn(s)], axis=1)

    row_index, col_index = lax.axis_index("rows"), lax.axis_index("cols")

    def pick(table, index):
        held = jnp.asarray(table.astype(np.float32)).astype(bf16)
        return lax.dynamic_index_in_dim(held, index, 0, keepdims=False)

    return {
        "cols_forward": pick(to_modes(cy * scale_cols, sy * scale_cols), col_index),
        "rows_forward": pick(rows_out(cx * scale_rows, sx * scale_rows), row_index),
        "rows_inverse": pick(rows_back(cx, sx), row_index),
        "cols_inverse": pick(to_cells(cy, sy) / M, col_index),
        "cols_grad": pick(to_modes(cy, sy), col_index),
        "rows_grad": pick(rows_out(cx, sx) / M, row_index),
        "rows_last": pick(rows_back(cx * scale_rows, sx * scale_rows), row_index),
        "cols_last": pick(to_cells(cy * scale_cols, sy * scale_cols), col_index),
    }


def pair_to_modes(cells, cols_table, rows_table):
    height = cells.shape[0] // 2
    width = cols_table.shape[1] // 2
    lines = dot(cells, cols_table).astype(bf16)
    first = jnp.concatenate([lines[:height, :width], lines[:height, width:]], axis=0)
    second = jnp.concatenate([lines[height:, :width], lines[height:, width:]], axis=0)
    return dot(rows_table, jnp.concatenate([first, second], axis=1))


def pair_to_cells(first, second, rows_table, cols_table):
    width = first.shape[1]
    lines = dot(rows_table, jnp.concatenate([first, second], axis=1)).astype(bf16)
    height = lines.shape[0] // 2
    top = jnp.concatenate([lines[:height, :width], lines[height:, :width]], axis=1)
    low = jnp.concatenate([lines[:height, width:], lines[height:, width:]], axis=1)
    return dot(jnp.concatenate([top, low], axis=0), cols_table)


def forward_kernel(field_ref, cols_ref, rows_ref, modes_ref, turned_ref, modes_s, turned_s):
    channels, height, _ = field_ref.shape
    width = modes_ref.shape[1]
    cols_table, rows_table = cols_ref[...], rows_ref[...]
    for c in range(0, channels, 2):
        cells = jnp.concatenate([field_ref[c], field_ref[c + 1]], axis=0)
        modes = pair_to_modes(cells, cols_table, rows_table)
        wide = cells.astype(f32)
        for k in range(2):
            modes_s[pl.ds(c + k, 2 * M, stride=channels), :] = modes[:, k * width : (k + 1) * width]
            turned_s[pl.ds(c + k, height, stride=channels), :] = wide[k * height : (k + 1) * height]
    modes_ref[...] = modes_s[...].astype(bf16)
    turned_ref[...] = turned_s[...].astype(bf16)


def middle_kernel(
    modes_ref, conv_ref, cotangent_ref, rows_in_ref, cols_in_ref, cols_ref, rows_ref,
    out_ref, turned_ref, grads_ref, modes_s, grads_s, turned_s,
):
    channels, height, _ = cotangent_ref.shape
    width = modes_ref.shape[1]
    modes_s[...] = modes_ref[...].astype(f32)
    root = math.sqrt(2.0 / math.pi)
    for c in range(0, channels, 2):
        first = modes_s[pl.ds(c, 2 * M, stride=channels), :].astype(bf16)
        second = modes_s[pl.ds(c + 1, 2 * M, stride=channels), :].astype(bf16)
        cells = pair_to_cells(first, second, rows_in_ref[...], cols_in_ref[...])
        kept = []
        for k in range(2):
            pre = cells[k * height : (k + 1) * height]
            pre = pre + conv_ref[pl.ds(c + k, height, stride=channels), :]
            square = pre * pre
            turn = jnp.tanh(root * (pre + 0.044715 * (square * pre)))
            half = 0.5 * (1.0 + turn)
            out_ref[c + k] = (pre * half).astype(bf16)
            slope = half + 0.5 * pre * (1.0 - turn * turn) * (root * (1.0 + 0.134145 * square))
            grad = (cotangent_ref[c + k].astype(f32) * slope).astype(bf16)
            turned_s[pl.ds(c + k, height, stride=channels), :] = grad.astype(f32)
            kept.append(grad)
        grads = pair_to_modes(jnp.concatenate(kept, axis=0), cols_ref[...], rows_ref[...])
        for k in range(2):
            grads_s[pl.ds(c + k, 2 * M, stride=channels), :] = grads[:, k * width : (k + 1) * width]
    grads_ref[...] = grads_s[...].astype(bf16)
    turned_ref[...] = turned_s[...].astype(bf16)


def last_kernel(modes_ref, conv_ref, rows_in_ref, cols_in_ref, out_ref, modes_s):
    channels, height, _ = out_ref.shape
    modes_s[...] = modes_ref[...].astype(f32)
    for c in range(0, channels, 2):
        first = modes_s[pl.ds(c, 2 * M, stride=channels), :].astype(bf16)
        second = modes_s[pl.ds(c + 1, 2 * M, stride=channels), :].astype(bf16)
        cells = pair_to_cells(first, second, rows_in_ref[...], cols_in_ref[...])
        for k in range(2):
            total = cells[k * height : (k + 1) * height]
            total = total + conv_ref[pl.ds(c + k, height, stride=channels), :]
            out_ref[c + k] = total.astype(bf16)


def band(weights):
    outs = weights.shape[3]
    flat = jnp.transpose(weights, (3, 0, 1, 2)).reshape(outs, -1)
    step = flat.shape[1] // 3
    rows = [
        jnp.pad(flat, ((0, 0), (step * k, step * (BLOCK - 1 - k)))) for k in range(BLOCK)
    ]
    return jnp.concatenate(rows, axis=0)


def stencil_kernel(cells_ref, band_ref, out_ref):
    height, lines, width = cells_ref.shape
    rows = band_ref.shape[0]
    matrix = band_ref[...]
    for b in range(0, (height - 2) // BLOCK, 2):
        pair = [
            cells_ref[BLOCK * k : BLOCK * k + BLOCK + 2].reshape((BLOCK + 2) * lines, width)
            for k in (b, b + 1)
        ]
        both = dot(matrix, jnp.concatenate(pair, axis=1))
        for k in range(2):
            out_ref[rows * (b + k) : rows * (b + k + 1), :] = both[:, k * width : (k + 1) * width]


def stencil(cells, matrix, channels):
    height, lines, width = cells.shape
    return call(
        stencil_kernel,
        shape(((height - 2) * channels, width), f32),
        [],
        2 * matrix.size * height * width // BLOCK,
        cells.size * 2 + matrix.size * 2 + height * channels * width * 4,
        cells, matrix,
    )


def kernel_grad_kernel(cells_ref, grad_ref, out_ref):
    height, lines, width = cells_ref.shape
    channels = grad_ref.shape[1]
    taken = BLOCK * channels
    total = jnp.zeros(((BLOCK + 2) * lines, taken), f32)
    for b in range(0, (height - 2) // BLOCK, 2):
        cells = [
            cells_ref[BLOCK * k : BLOCK * k + BLOCK + 2].reshape((BLOCK + 2) * lines, width)
            for k in (b, b + 1)
        ]
        grads = [
            grad_ref[BLOCK * k : BLOCK * (k + 1)].reshape(taken, width) for k in (b, b + 1)
        ]
        total = total + dot_nt(jnp.concatenate(cells, axis=1), jnp.concatenate(grads, axis=1))
    place = lax.broadcasted_iota(jnp.int32, (3 * lines, taken), 1) // channels
    folded = jnp.zeros((3 * lines, taken), f32)
    for k in range(BLOCK):
        folded = folded + jnp.where(place == k, total[lines * k : lines * (k + 3)], 0.0)
    size = taken
    while size > 128:
        size //= 2
        folded = folded[:, :size] + folded[:, size : 2 * size]
    step = size // 2
    while step >= channels:
        folded = folded + pltpu.roll(folded, step, 1)
        step //= 2
    out_ref[...] = folded


def kernel_grad_here(cells, grad):
    height, lines, width = cells.shape
    return call(
        kernel_grad_kernel,
        shape((3 * lines, 128), f32),
        [],
        2 * cells.size * BLOCK * grad.shape[1],
        cells.size * 2 + grad.size * 2,
        cells, grad,
    )


def widened(turned):
    count_rows, count_cols = lax.axis_size("rows"), lax.axis_size("cols")
    up = [(i, i + 1) for i in range(count_rows - 1)]
    down = [(i + 1, i) for i in range(count_rows - 1)]
    before = lax.ppermute(turned[-1:], "rows", up)
    after = lax.ppermute(turned[:1], "rows", down)
    tall = jnp.concatenate([before, turned, after], axis=0)
    right = [(i, i + 1) for i in range(count_cols - 1)]
    left = [(i + 1, i) for i in range(count_cols - 1)]
    first = lax.ppermute(tall[:, :, -1], "cols", right)[:, :, None]
    final = lax.ppermute(tall[:, :, 0], "cols", left)[:, :, None]
    return jnp.concatenate(
        [
            jnp.concatenate([first, tall[:, :, :-1]], axis=2),
            tall,
            jnp.concatenate([tall[:, :, 1:], final], axis=2),
        ],
        axis=1,
    )


def total_sum(values):
    for axis in ("rows", "cols"):
        count, step = lax.axis_size(axis), 1
        while step < count:
            swap = [(i, i ^ step) for i in range(count)]
            values = values + lax.ppermute(values, axis, swap)
            step *= 2
    return values


def halves(total):
    low = lax.broadcasted_iota(jnp.int32, total[0].shape, 1) < M
    real, imag = [], []
    for t in range(0, len(total), 2):
        one, two = total[t], total[t + 1]
        real.append(jnp.where(low, one, pltpu.roll(two, M, 1)))
        imag.append(jnp.where(low, pltpu.roll(one, M, 1), two))
    return jnp.concatenate(real, axis=1), jnp.concatenate(imag, axis=1)


def unhalved(real, imag):
    low = lax.broadcasted_iota(jnp.int32, (real.shape[0], 2 * M), 1) < M
    rows = []
    for t in range(0, real.shape[1], 2 * M):
        re, im = real[:, t : t + 2 * M], imag[:, t : t + 2 * M]
        rows.append(jnp.where(low, re, pltpu.roll(im, M, 1)))
        rows.append(jnp.where(low, pltpu.roll(re, M, 1), im))
    return rows


def gathered_rows(parts_ref, channels):
    devices, lines, _ = parts_ref.shape
    total = parts_ref[0].astype(f32)
    for d in range(1, devices):
        total = total + parts_ref[d].astype(f32)
    return [total[k : k + channels] for k in range(0, lines, channels)]


def send_all(rows, out_ref, channels):
    for k, row in enumerate(rows):
        value = row.astype(bf16)
        for d in range(out_ref.shape[0]):
            out_ref[d, k * channels : (k + 1) * channels, :] = value


def mix_kernel(parts_ref, real_ref, imag_ref, out_ref, coef_real_ref, coef_imag_ref):
    channels = real_ref.shape[0]
    real, imag = halves(gathered_rows(parts_ref, channels))
    coef_real_ref[...] = real
    coef_imag_ref[...] = imag
    mixed_real = jnp.zeros(real_ref.shape[1:], f32)
    mixed_imag = jnp.zeros(real_ref.shape[1:], f32)
    for c in range(channels):
        wr, wi = real_ref[c].astype(f32), imag_ref[c].astype(f32)
        re, im = real[c : c + 1], imag[c : c + 1]
        mixed_real = mixed_real + (re * wr - im * wi)
        mixed_imag = mixed_imag + (re * wi + im * wr)
    send_all(unhalved(mixed_real, mixed_imag), out_ref, channels)


def unmix_kernel(parts_ref, real_ref, imag_ref, out_ref, mode_real_ref, mode_imag_ref, re_s, im_s):
    channels = real_ref.shape[0]
    real, imag = halves(gathered_rows(parts_ref, channels))
    mode_real_ref[...] = real
    mode_imag_ref[...] = imag
    for c in range(channels):
        wr, wi = real_ref[c].astype(f32), imag_ref[c].astype(f32)
        re_s[c : c + 1, :] = jnp.sum(wr * real + wi * imag, axis=0, keepdims=True)
        im_s[c : c + 1, :] = jnp.sum(wr * imag - wi * real, axis=0, keepdims=True)
    send_all(unhalved(re_s[...], im_s[...]), out_ref, channels)


def owner_stage(kernel, parts, real, imag, extra):
    channels, _, modes = real.shape
    return call(
        kernel,
        (shape(parts.shape, bf16), shape((channels, modes), f32), shape((channels, modes), f32)),
        [pltpu.VMEM((channels, modes), f32)] * extra,
        8 * real.size,
        parts.size * 4 + real.size * 4,
        parts, real, imag,
    )


def exact(form, left, right):
    return jnp.einsum(form, left, right, precision=lax.Precision.HIGHEST, preferred_element_type=f32)


def at_owner(partial, weight_real, weight_imag, forward):
    channels, _, modes = weight_real.shape
    devices = 2 * M * M // modes
    swap = lambda x: lax.all_to_all(x, BOTH, 0, 0, tiled=True)
    if modes % (2 * M) == 0 and M == 64:
        parts = swap(partial.reshape(devices, modes // M * channels, 2 * M))
        kernel = mix_kernel if forward else unmix_kernel
        sent, real, imag = owner_stage(kernel, parts, weight_real, weight_imag, 0 if forward else 2)
        return swap(sent).reshape(2 * M * channels, 2 * M), real, imag
    pieces = M // modes
    parts = partial.reshape(2 * M, channels, 2, pieces, modes).transpose(0, 3, 1, 2, 4)
    parts = swap(parts.reshape(devices, channels, 2, modes))
    total = jnp.sum(parts.astype(f32), axis=0)
    real, imag = total[:, 0], total[:, 1]
    wr, wi = weight_real.astype(f32), weight_imag.astype(f32)
    if forward:
        re = exact("cm,com->om", real, wr) - exact("cm,com->om", imag, wi)
        im = exact("cm,com->om", real, wi) + exact("cm,com->om", imag, wr)
    else:
        re = exact("com,om->cm", wr, real) + exact("com,om->cm", wi, imag)
        im = exact("com,om->cm", wr, imag) - exact("com,om->cm", wi, real)
    sent = jnp.stack([re, im], axis=1).astype(bf16)
    sent = swap(jnp.broadcast_to(sent, (devices,) + sent.shape))
    spread = sent.reshape(2 * M, pieces, channels, 2, modes).transpose(0, 2, 3, 1, 4)
    return spread.reshape(2 * M * channels, 2 * M), real, imag


def body(field, cotangent, weight_real, weight_imag, kernel):
    channels, rows_here, cols_here = field.shape
    total_rows = rows_here * lax.axis_size("rows")
    total_cols = cols_here * lax.axis_size("cols")
    scale_cells = 1.0 / math.sqrt(total_rows * total_cols)
    table = make_tables(rows_here, cols_here)
    cells = field.size
    lines = (2 * M * channels, 2 * M)
    turned_lines = (rows_here * channels, cols_here)
    transform = 2 * cells * 4 * M + 2 * lines[0] * lines[1] * 2 * rows_here

    partial, turned = call(
        forward_kernel,
        (shape(lines, bf16), shape(turned_lines, bf16)),
        [pltpu.VMEM(lines, f32), pltpu.VMEM(turned_lines, f32)],
        transform, cells * 4 + lines[0] * lines[1] * 2,
        field, table["cols_forward"], table["rows_forward"],
    )
    spectrum, coef_real, coef_imag = at_owner(partial, weight_real, weight_imag, True)

    wide_field = widened(turned.reshape(rows_here, channels, cols_here))
    conv = stencil(wide_field, band(kernel), channels)

    activated, grad_turned, partial_grad = call(
        middle_kernel,
        (shape(field.shape, bf16), shape(turned_lines, bf16), shape(lines, bf16)),
        [pltpu.VMEM(lines, f32), pltpu.VMEM(lines, f32), pltpu.VMEM(turned_lines, f32)],
        2 * transform, cells * 10 + lines[0] * lines[1] * 4,
        spectrum, conv, cotangent, table["rows_inverse"], table["cols_inverse"],
        table["cols_grad"], table["rows_grad"],
    )
    spectrum_grad, mode_real, mode_imag = at_owner(partial_grad, weight_real, weight_imag, False)

    grad_turned = grad_turned.reshape(rows_here, channels, cols_here)
    wide_grad = widened(grad_turned)
    backward = jnp.transpose(kernel[::-1, ::-1], (0, 1, 3, 2))
    conv_grad = stencil(wide_grad, band(backward), channels)
    local = kernel_grad_here(wide_field, grad_turned)[:, :channels]
    kernel_grad = total_sum(local).reshape(3, 3, channels, channels) * scale_cells

    weight_scale = M * scale_cells
    out_real = (
        coef_real[:, None, :] * mode_real[None] + coef_imag[:, None, :] * mode_imag[None]
    ) * weight_scale
    out_imag = (
        coef_real[:, None, :] * mode_imag[None] - coef_imag[:, None, :] * mode_real[None]
    ) * weight_scale

    field_grad = call(
        last_kernel,
        shape(field.shape, bf16),
        [pltpu.VMEM(lines, f32)],
        transform, cells * 6 + lines[0] * lines[1] * 2,
        spectrum_grad, conv_grad, table["rows_last"], table["cols_last"],
    )
    return activated, field_grad, out_real, out_imag, kernel_grad


def solution(mesh):
    placed = (
        P(None, "rows", "cols"),
        P(None, "rows", "cols"),
        P(None, None, ("rows", "cols")),
        P(None, None, ("rows", "cols")),
        P(),
    )
    return jax.shard_map(
        body, mesh=mesh, in_specs=placed, out_specs=placed, check_vma=False
    )
```

time: 498 us -> 176 us (0.35); the launches traced: 490 us -> 174 us
  waiting for transfers between devices: 290 us -> 62.6 us
  matrix products: 53.5 us -> 0 us
  blocking collectives: 39.6 us -> 0 us
  starting transfers between devices: 15.6 us -> 54.9 us
  local copies, waits for them, and re-layouts: 62.2 us -> 26.5 us
  Pallas kernels: 0 us -> 18.9 us
  between operations: 14.9 us -> 1 us
    reduce_scatter x2 -> x0, waiting for transfers between devices: 275 us -> none  [owner_sums(): lax.psum_scatter(partials, ('rows', 'cols'), scatter_dimension=2, tiled=T...]
    all_to_all x0 -> x4, waiting for transfers between devices: none -> 44.6 us  [at_owner(): swap = lambda x: lax.all_to_all(x, BOTH, 0, 0, tiled=True)]
    dot_general x33 -> x0, matrix products: 41.3 us -> none  [the longest x12 24.8 us: exact(): jnp.einsum(form, left, right, precision=highest, preferred_element_type=j...]
    psum x1 -> x0, blocking collectives: 39.6 us -> none  [body(): kernel_grad = lax.psum(kernel_local, ('rows', 'cols')) * scale_cells]
    all_to_all x0 -> x4, starting transfers between devices: none -> 26.4 us  [at_owner(): swap = lambda x: lax.all_to_all(x, BOTH, 0, 0, tiled=True)]
    pallas_call x0 -> x8, Pallas kernels: none -> 18.9 us  [call(): pl.pallas_call(kernel, out_shape=out_shape, in_specs=[pl.BlockSpec(memory...]
    conv_general_dilated x8 -> x0, local copies, waits for them, and re-layouts: 18.6 us -> none  [stencil(): lax.conv_general_dilated(padded[None], weights, (1, 1), ((0, 0), (0, 0)),...]
    ppermute x8 -> x13, starting transfers between devices: 15.4 us -> 28.5 us  [the longest x5 9.55 us: total_sum(): values = values + lax.ppermute(values, axis, swap)]
  transfers between devices with their start and end apart: 12 -> 17, of which waited for: 6 -> 8; matrix products, arithmetic and copies ran while one was open for 13% -> 15% of each run, Pallas kernels for 0% -> 2%
where the time goes in v1:
time: 176 us; the launch traced here: 174 us
  waiting for transfers between devices  62.6 us (36%)
  starting transfers between devices  54.9 us (31%)
  local copies, waits for them, and re-layouts  26.5 us (15%)
  Pallas kernels  18.9 us (11%)
  other arithmetic  10.4 us (6%)
    all_to_all x4, waiting for transfers between devices, at_owner(): swap = lambda x: lax.all_to_all(x, BOTH, 0, 0, tiled=True)  44.6 us
    all_to_all x4, starting transfers between devices, at_owner(): swap = lambda x: lax.all_to_all(x, BOTH, 0, 0, tiled=True)  26.4 us
    pallas_call x8, Pallas kernels, call(): pl.pallas_call(kernel, out_shape=out_shape, in_specs=[pl.BlockSpec(memory...  18.9 us
    ppermute x5, waiting for transfers between devices, total_sum(): values = values + lax.ppermute(values, axis, swap)  12.2 us
    unnamed x44, local copies, waits for them, and re-layouts  10.5 us
    ppermute x5, starting transfers between devices, total_sum(): values = values + lax.ppermute(values, axis, swap)  9.55 us
    ppermute x2, starting transfers between devices, widened(): first = lax.ppermute(tall[:, :, -1], 'cols', right)[:, :, None]  9.27 us
    ppermute x2, waiting for transfers between devices, widened(): first = lax.ppermute(tall[:, :, -1], 'cols', right)[:, :, None]  5.75 us
  transfers between devices with their start and end apart: 17, of which 8 were waited for; matrix products, arithmetic and copies ran while one was open for 15% of the time, Pallas kernels for 2%

profile of v1, /device:TPU:0, one launch (start us, length us, event | category | flops | bytes accessed | tf_op | source)
XLA Modules:
  0.0 174.3 jit_solution(17999059556709672332)
XLA Ops:
  0.6 0.8 dynamic-slice_bitcast_fusion.7.rows_ref
  1.4 0.8 dynamic-slice_bitcast_fusion.3.cols_ref
  2.3 1.0 copy-done.13
  3.3 2.7 %shard_map.164 = (bf16[4096,128]{1,0:T(8,128)(2,1)S(1)}, bf16[2048,128]{1,0:T(8,128)(2,1)S(1)}) custom-call(bf16[32,64,128]{2,1,0:T(8,128)(2,1)S(1)} %copy-done.13, bf16[128,256]{1,0:T(8,128)(2,1)S(1)} %dynamic-slice_bitcast_fusion.3.cols_ref, bf16[128,128]{1,0:T(8,128)(2,1)S(1)} %dynamic-slice_bitcast_fusion.7.rows_ref), custom_call_target="tpu_custom_call" | custom-call | flops 268435456 | bytes 2097152 | tf_op jit(solution)/shard_map/pallas_call | solution.py:30
  6.0 1.0 copy-done.7
  6.9 7.3 %all-to-all-start = ((bf16[32,128,128]{2,1,0:T(8,128)(2,1)}), bf16[32,128,128]{2,1,0:T(8,128)(2,1)S(1)}, u32[]{:S(2)}, u32[]{:S(2)}) async-start(bf16[32,128,128]{2,1,0:T(8,128)(2,1)} %bitcast.52), calls=%async_computation | async-start | bytes 2097152 | tf_op jit(solution)/shard_map/all_to_all | solution.py:366
  14.3 2.2 %collective-permute-start = (bf16[1,32,128]{2,1,0:T(8,128)(2,1)S(1)}, bf16[1,32,128]{2,1,0:T(8,128)(2,1)S(1)}, u32[]{:S(2)}, u32[]{:S(2)}) collective-permute-start(bf16[1,32,128]{2,1,0:T(8,128)(2,1)S(1)} %get-tuple-element.37), channel_id=1, source_target_pairs={{0,4},{4,8},{8,12},{12,16},{16,20},{20,24},{24,28},{1,5},{5,9},{9,... | collective-permute-start | bytes 24584 | tf_op jit(solution)/shard_map/ppermute | solution.py:258
  16.5 1.3 collective-permute-start.1
  17.8 0.9 dynamic-slice_bitcast_fusion.2.cols_in_ref
  18.6 20.6 %all-to-all-done.parts_ref = bf16[32,128,128]{2,1,0:T(8,128)(2,1)S(1)} async-done(((bf16[32,128,128]{2,1,0:T(8,128)(2,1)}), bf16[32,128,128]{2,1,0:T(8,128)(2,1)S(1)}, u32[]{:S(2)}, u32[]{:S(2)}) %all-to-all-start) | async-done | bytes 1048608 | tf_op jit(solution)/shard_map/all_to_all | solution.py:366
  39.2 0.7 shard_map.165
  40.0 1.0 copy-done.5
  40.9 4.7 %all-to-all-start.1 = ((bf16[32,128,128]{2,1,0:T(8,128)(2,1)}), bf16[32,128,128]{2,1,0:T(8,128)(2,1)}, u32[]{:S(2)}, u32[]{:S(2)}) async-start(bf16[32,128,128]{2,1,0:T(8,128)(2,1)} %copy-done.5), calls=%async_computation.1 | async-start | bytes 2097152 | tf_op jit(solution)/shard_map/all_to_all | solution.py:366
  45.6 0.9 dynamic-slice_bitcast_fusion.1.cols_ref
  47.1 0.8 copy-done.8
  47.9 0.8 dynamic-slice_bitcast_fusion.5
  49.0 0.7 copy.47
  49.7 0.7 copy.49
  50.4 1.3 collective-permute-start.3
  51.6 4.7 %collective-permute-start.2 = (bf16[66,32]{0,1:T(8,128)(2,1)S(1)}, bf16[66,32]{0,1:T(8,128)(2,1)S(1)}, u32[]{:S(2)}, u32[]{:S(2)}) collective-permute-start(bf16[66,32]{0,1:T(8,128)(2,1)S(1)} %bitcast.62), channel_id=1, source_target_pairs={{0,1},{1,2},{2,3},{4,5},{5,6},{6,7},{8,9},{9,10},{10,11},{12,13},{... | collective-permute-start | bytes 12680 | tf_op jit(solution)/shard_map/ppermute | solution.py:263
  56.4 1.2 fusion.3
  57.6 5.7 %collective-permute-done.2 = bf16[66,32]{0,1:T(8,128)(2,1)S(1)} collective-permute-done((bf16[66,32]{0,1:T(8,128)(2,1)S(1)}, bf16[66,32]{0,1:T(8,128)(2,1)S(1)}, u32[]{:S(2)}, u32[]{:S(2)}) %collective-permute-start.2) | collective-permute-done | bytes 4256 | tf_op jit(solution)/shard_map/ppermute | solution.py:263
  63.3 0.9 copy.48
  64.3 1.7 copy.50
  66.0 2.4 %maximum_maximum_fusion.cells_ref = bf16[66,96,128]{2,1,0:T(8,128)(2,1)S(1)} fusion(bf16[66,32,1]{2,1,0:T(8,128)(2,1)} %copy.50, bf16[66,32,127]{2,1,0:T(8,128)(2,1)} %get-tuple-element.34, bf16[1,32,128]{2,1,0:T(8,128)(2,1)S(1)} %collective-permute-done.1, bf16[64,32,128]{2,1,0:T(8,128)(2,1)S(1)} %bitcast.50, bf16[1,32,128]{2,1,0:T(8,128)(2,1)S(1)} %collective-permute-done, ...), kind=kLoop, calls=%fused_computation | loop fusion | flops 11354112 | bytes 3244032 | tf_op jit(solution)/shard_map/concatenate | solution.py:265
  68.4 0.7 shard_map.166.conv_ref
  69.1 1.4 all-to-all-done.1
  70.5 1.0 copy-done.12
  71.6 9.5 %shard_map.167 = (bf16[32,64,128]{2,1,0:T(8,128)(2,1)}, bf16[2048,128]{1,0:T(8,128)(2,1)S(1)}, bf16[4096,128]{1,0:T(8,128)(2,1)S(1)}) custom-call(bf16[4096,128]{1,0:T(8,128)(2,1)} %bitcast.3.modes_ref, f32[2048,128]{1,0:T(8,128)S(1)} %shard_map.166.conv_ref, bf16[32,64,128]{2,1,0:T(8,128)(2,1)S(1)} %copy-done.12, ...), custom_call_target="tpu_custom_call" | custom-call | flops 536870912 | bytes 4718592 | tf_op jit(solution)/shard_map/pallas_call | solution.py:30
  81.1 1.0 copy-done.6
  82.1 9.9 %all-to-all-start.2 = ((bf16[32,128,128]{2,1,0:T(8,128)(2,1)}), bf16[32,128,128]{2,1,0:T(8,128)(2,1)S(1)}, u32[]{:S(2)}, u32[]{:S(2)}) async-start(bf16[32,128,128]{2,1,0:T(8,128)(2,1)} %bitcast.51), calls=%async_computation.2 | async-start | bytes 2097152 | tf_op jit(solution)/shard_map/all_to_all | solution.py:366
  92.2 0.8 dynamic-slice_bitcast_fusion.cols_in_ref
  93.5 0.8 copy-done.10
  94.3 22.6 %all-to-all-done.2.parts_ref = bf16[32,128,128]{2,1,0:T(8,128)(2,1)S(1)} async-done(((bf16[32,128,128]{2,1,0:T(8,128)(2,1)}), bf16[32,128,128]{2,1,0:T(8,128)(2,1)S(1)}, u32[]{:S(2)}, u32[]{:S(2)}) %all-to-all-start.2) | async-done | bytes 1048608 | tf_op jit(solution)/shard_map/all_to_all | solution.py:366
  116.9 1.0 copy-done.1
  117.9 1.0 copy-done.3
  119.0 0.8 shard_map.168
  119.8 1.0 copy-done.4
  120.8 4.6 %all-to-all-start.3 = ((bf16[32,128,128]{2,1,0:T(8,128)(2,1)}), bf16[32,128,128]{2,1,0:T(8,128)(2,1)S(1)}, u32[]{:S(2)}, u32[]{:S(2)}) async-start(bf16[32,128,128]{2,1,0:T(8,128)(2,1)} %copy-done.4), calls=%async_computation.3 | async-start | bytes 2097152 | tf_op jit(solution)/shard_map/all_to_all | solution.py:366
  125.4 0.8 dynamic-slice_bitcast_fusion.4.rows_in_ref
  126.1 2.1 %collective-permute-start.4 = (bf16[1,32,128]{2,1,0:T(8,128)(2,1)S(1)}, bf16[1,32,128]{2,1,0:T(8,128)(2,1)S(1)}, u32[]{:S(2)}, u32[]{:S(2)}) collective-permute-start(bf16[1,32,128]{2,1,0:T(8,128)(2,1)S(1)} %get-tuple-element.35), channel_id=1, source_target_pairs={{0,4},{4,8},{8,12},{12,16},{16,20},{20,24},{24,28},{1,5},{5,9},{9,... | collective-permute-start | bytes 24584 | tf_op jit(solution)/shard_map/ppermute | solution.py:258
  128.3 1.5 collective-permute-start.5
  129.8 0.8 shard_map.171
  130.7 2.3 %collective-permute-start.8 = (f32[288,32]{1,0:T(8,128)S(1)}, f32[288,32]{1,0:T(8,128)S(1)}, u32[]{:S(2)}, u32[]{:S(2)}) collective-permute-start(f32[288,32]{1,0:T(8,128)S(1)} %bitcast.53), channel_id=1, source_target_pairs={{0,4},{4,0},{8,12},{12,8},{16,20},{20,16},{24,28},{28,24},{1,5},{5... | collective-permute-start | bytes 110600 | tf_op jit(solution)/shard_map/ppermute | solution.py:280
  133.1 0.9 collective-permute-done.8
  134.7 2.0 %collective-permute-start.9 = (f32[288,32]{1,0:T(8,128)}, f32[288,32]{1,0:T(8,128)}, u32[]{:S(2)}, u32[]{:S(2)}) collective-permute-start(f32[288,32]{1,0:T(8,128)} %slice_add_fusion), channel_id=1, source_target_pairs={{0,8},{4,12},{8,0},{12,4},{16,24},{20,28},{24,16},{28,20},{1,9},{5... | collective-permute-start | bytes 110600 | tf_op jit(solution)/shard_map/ppermute | solution.py:280
  136.9 0.7 copy.52
  137.5 0.7 copy.54
  138.2 1.3 collective-permute-start.7
  139.5 4.5 %collective-permute-start.6 = (bf16[66,32]{0,1:T(8,128)(2,1)S(1)}, bf16[66,32]{0,1:T(8,128)(2,1)S(1)}, u32[]{:S(2)}, u32[]{:S(2)}) collective-permute-start(bf16[66,32]{0,1:T(8,128)(2,1)S(1)} %bitcast.58), channel_id=1, source_target_pairs={{0,1},{1,2},{2,3},{4,5},{5,6},{6,7},{8,9},{9,10},{10,11},{12,13},{... | collective-permute-start | bytes 12680 | tf_op jit(solution)/shard_map/ppermute | solution.py:263
  144.1 1.7 add.69
  145.8 1.5 collective-permute-start.10
  147.4 0.9 copy.53
  148.4 1.7 copy.55
  150.1 3.2 %collective-permute-done.10 = f32[288,32]{1,0:T(8,128)} collective-permute-done((f32[288,32]{1,0:T(8,128)}, f32[288,32]{1,0:T(8,128)}, u32[]{:S(2)}, u32[]{:S(2)}) %collective-permute-start.10) | collective-permute-done | bytes 36896 | tf_op jit(solution)/shard_map/ppermute | solution.py:280
  153.3 1.0 add.70
  154.3 1.2 collective-permute-start.11
  155.5 2.2 %maximum_maximum_fusion.1.cells_ref = bf16[66,96,128]{2,1,0:T(8,128)(2,1)S(1)} fusion(bf16[66,32,1]{2,1,0:T(8,128)(2,1)} %copy.55, bf16[66,32,127]{2,1,0:T(8,128)(2,1)S(1)} %get-tuple-element.30, bf16[1,32,128]{2,1,0:T(8,128)(2,1)S(1)} %collective-permute-done.5, bf16[64,32,128]{2,1,0:T(8,128)(2,1)S(1)} %bitcast.47, ...), kind=kLoop, calls=%fused_computation.1 | loop fusion | flops 11354112 | bytes 3244032 | tf_op jit(solution)/shard_map/concatenate | solution.py:265
  157.7 2.4 %collective-permute-done.11 = f32[288,32]{1,0:T(8,128)S(1)} collective-permute-done((f32[288,32]{1,0:T(8,128)S(1)}, f32[288,32]{1,0:T(8,128)S(1)}, u32[]{:S(2)}, u32[]{:S(2)}) %collective-permute-start.11) | collective-permute-done | bytes 36896 | tf_op jit(solution)/shard_map/ppermute | solution.py:280
  160.2 2.6 %collective-permute-start.12 = (f32[288,32]{1,0:T(8,128)S(1)}, f32[288,32]{1,0:T(8,128)S(1)}, u32[]{:S(2)}, u32[]{:S(2)}) collective-permute-start(f32[288,32]{1,0:T(8,128)S(1)} %add.71), channel_id=1, source_target_pairs={{0,2},{1,3},{2,0},{3,1},{4,6},{5,7},{6,4},{7,5},{8,10},{9,11},{10,... | collective-permute-start | bytes 110600 | tf_op jit(solution)/shard_map/ppermute | solution.py:280
  162.8 0.7 shard_map.169.conv_ref
  163.5 5.7 %collective-permute-done.12 = f32[288,32]{1,0:T(8,128)S(1)} collective-permute-done((f32[288,32]{1,0:T(8,128)S(1)}, f32[288,32]{1,0:T(8,128)S(1)}, u32[]{:S(2)}, u32[]{:S(2)}) %collective-permute-start.12) | collective-permute-done | bytes 36896 | tf_op jit(solution)/shard_map/ppermute | solution.py:280
  169.8 1.6 subtract_multiply_fusion
  171.4 2.9 %shard_map.170 = bf16[32,64,128]{2,1,0:T(8,128)(2,1)} custom-call(bf16[4096,128]{1,0:T(8,128)(2,1)S(1)} %bitcast.48, f32[2048,128]{1,0:T(8,128)S(1)} %shard_map.169.conv_ref, bf16[128,128]{1,0:T(8,128)(2,1)S(1)} %dynamic-slice_bitcast_fusion.4.rows_in_ref, bf16[256,128]{1,0:T(8,128)(2,1)S(1)} %dynamic-slice_bitcast_fusion.cols_in_ref), custom_call_target="tpu_custom_call" | custom-call | flops 268435456 | bytes 2621440 | tf_op jit(solution)/shard_map/pallas_call | solution.py:30
  (59 shorter events, 3.5 us)
Async XLA Ops:
  2.2 1.0 copy-start.13
  3.3 35.9 %copy-start = (bf16[32,32,256]{2,1,0:T(8,128)(2,1)S(1)}, bf16[32,32,256]{2,1,0:T(8,128)(2,1)}, u32[]{:S(2)}) copy-start(bf16[32,32,256]{2,1,0:T(8,128)(2,1)} %real_ref.3) | copy-start | bytes 1572868
  3.3 35.9 %copy-start.2 = (bf16[32,32,256]{2,1,0:T(8,128)(2,1)S(1)}, bf16[32,32,256]{2,1,0:T(8,128)(2,1)}, u32[]{:S(2)}) copy-start(bf16[32,32,256]{2,1,0:T(8,128)(2,1)} %imag_ref.3) | copy-start | bytes 1572868
  6.0 1.0 copy-start.7
  6.9 32.3 %all-to-all-start = ((bf16[32,128,128]{2,1,0:T(8,128)(2,1)}), bf16[32,128,128]{2,1,0:T(8,128)(2,1)S(1)}, u32[]{:S(2)}, u32[]{:S(2)}) async-start(bf16[32,128,128]{2,1,0:T(8,128)(2,1)} %bitcast.52), calls=%async_computation | async-start | bytes 2097152 | tf_op jit(solution)/shard_map/all_to_all | solution.py:366
  14.3 34.4 %collective-permute-start = (bf16[1,32,128]{2,1,0:T(8,128)(2,1)S(1)}, bf16[1,32,128]{2,1,0:T(8,128)(2,1)S(1)}, u32[]{:S(2)}, u32[]{:S(2)}) collective-permute-start(bf16[1,32,128]{2,1,0:T(8,128)(2,1)S(1)} %get-tuple-element.37), channel_id=1, source_target_pairs={{0,4},{4,8},{8,12},{12,16},{16,20},{20,24},{24,28},{1,5},{5,9},{9,... | collective-permute-start | bytes 24584 | tf_op jit(solution)/shard_map/ppermute | solution.py:258
  16.5 32.2 %collective-permute-start.1 = (bf16[1,32,128]{2,1,0:T(8,128)(2,1)S(1)}, bf16[1,32,128]{2,1,0:T(8,128)(2,1)S(1)}, u32[]{:S(2)}, u32[]{:S(2)}) collective-permute-start(bf16[1,32,128]{2,1,0:T(8,128)(2,1)S(1)} %get-tuple-element.38), channel_id=1, source_target_pairs={{4,0},{8,4},{12,8},{16,12},{20,16},{24,20},{28,24},{5,1},{9,5},{13... | collective-permute-start | bytes 24584 | tf_op jit(solution)/shard_map/ppermute | solution.py:259
  40.0 1.0 copy-start.5
  40.9 5.5 %copy-start.14 = (bf16[3,3,32,32]{3,2,1,0:T(8,128)(2,1)S(1)}, bf16[3,3,32,32]{3,2,1,0:T(8,128)(2,1)}, u32[]{:S(2)}) copy-start(bf16[3,3,32,32]{3,2,1,0:T(8,128)(2,1)} %param.17) | copy-start | bytes 55300
  40.9 29.6 %all-to-all-start.1 = ((bf16[32,128,128]{2,1,0:T(8,128)(2,1)}), bf16[32,128,128]{2,1,0:T(8,128)(2,1)}, u32[]{:S(2)}, u32[]{:S(2)}) async-start(bf16[32,128,128]{2,1,0:T(8,128)(2,1)} %copy-done.5), calls=%async_computation.1 | async-start | bytes 2097152 | tf_op jit(solution)/shard_map/all_to_all | solution.py:366
  47.1 0.8 copy-start.8
  50.4 13.9 %collective-permute-start.3 = (bf16[66,32]{0,1:T(8,128)(2,1)S(1)}, bf16[66,32]{0,1:T(8,128)(2,1)S(1)}, u32[]{:S(2)}, u32[]{:S(2)}) collective-permute-start(bf16[66,32]{0,1:T(8,128)(2,1)S(1)} %bitcast.59), channel_id=1, source_target_pairs={{1,0},{2,1},{3,2},{5,4},{6,5},{7,6},{9,8},{10,9},{11,10},{13,12},{... | collective-permute-start | bytes 12680 | tf_op jit(solution)/shard_map/ppermute | solution.py:264
  51.6 11.7 %collective-permute-start.2 = (bf16[66,32]{0,1:T(8,128)(2,1)S(1)}, bf16[66,32]{0,1:T(8,128)(2,1)S(1)}, u32[]{:S(2)}, u32[]{:S(2)}) collective-permute-start(bf16[66,32]{0,1:T(8,128)(2,1)S(1)} %bitcast.62), channel_id=1, source_target_pairs={{0,1},{1,2},{2,3},{4,5},{5,6},{6,7},{8,9},{9,10},{10,11},{12,13},{... | collective-permute-start | bytes 12680 | tf_op jit(solution)/shard_map/ppermute | solution.py:263
  66.0 2.4 %copy-start.9 = (bf16[256,960]{1,0:T(8,128)(2,1)S(1)}, bf16[256,960]{1,0:T(8,128)(2,1)}, u32[]{:S(2)}) copy-start(bf16[256,960]{1,0:T(8,128)(2,1)} %copy-done.8) | copy-start | bytes 1474564
  70.5 1.0 copy-start.12
  81.1 1.0 copy-start.6
  82.1 34.8 %all-to-all-start.2 = ((bf16[32,128,128]{2,1,0:T(8,128)(2,1)}), bf16[32,128,128]{2,1,0:T(8,128)(2,1)S(1)}, u32[]{:S(2)}, u32[]{:S(2)}) async-start(bf16[32,128,128]{2,1,0:T(8,128)(2,1)} %bitcast.51), calls=%async_computation.2 | async-start | bytes 2097152 | tf_op jit(solution)/shard_map/all_to_all | solution.py:366
  93.5 0.8 copy-start.10
  116.9 1.0 copy-start.1
  117.9 1.0 copy-start.3
  119.8 1.0 copy-start.4
  120.8 50.6 %all-to-all-start.3 = ((bf16[32,128,128]{2,1,0:T(8,128)(2,1)}), bf16[32,128,128]{2,1,0:T(8,128)(2,1)S(1)}, u32[]{:S(2)}, u32[]{:S(2)}) async-start(bf16[32,128,128]{2,1,0:T(8,128)(2,1)} %copy-done.4), calls=%async_computation.3 | async-start | bytes 2097152 | tf_op jit(solution)/shard_map/all_to_all | solution.py:366
  126.1 6.9 %collective-permute-start.4 = (bf16[1,32,128]{2,1,0:T(8,128)(2,1)S(1)}, bf16[1,32,128]{2,1,0:T(8,128)(2,1)S(1)}, u32[]{:S(2)}, u32[]{:S(2)}) collective-permute-start(bf16[1,32,128]{2,1,0:T(8,128)(2,1)S(1)} %get-tuple-element.35), channel_id=1, source_target_pairs={{0,4},{4,8},{8,12},{12,16},{16,20},{20,24},{24,28},{1,5},{5,9},{9,... | collective-permute-start | bytes 24584 | tf_op jit(solution)/shard_map/ppermute | solution.py:258
  128.3 4.7 %collective-permute-start.5 = (bf16[1,32,128]{2,1,0:T(8,128)(2,1)S(1)}, bf16[1,32,128]{2,1,0:T(8,128)(2,1)S(1)}, u32[]{:S(2)}, u32[]{:S(2)}) collective-permute-start(bf16[1,32,128]{2,1,0:T(8,128)(2,1)S(1)} %get-tuple-element.36), channel_id=1, source_target_pairs={{4,0},{8,4},{12,8},{16,12},{20,16},{24,20},{28,24},{5,1},{9,5},{13... | collective-permute-start | bytes 24584 | tf_op jit(solution)/shard_map/ppermute | solution.py:259
  130.7 3.3 %collective-permute-start.8 = (f32[288,32]{1,0:T(8,128)S(1)}, f32[288,32]{1,0:T(8,128)S(1)}, u32[]{:S(2)}, u32[]{:S(2)}) collective-permute-start(f32[288,32]{1,0:T(8,128)S(1)} %bitcast.53), channel_id=1, source_target_pairs={{0,4},{4,0},{8,12},{12,8},{16,20},{20,16},{24,28},{28,24},{1,5},{5... | collective-permute-start | bytes 110600 | tf_op jit(solution)/shard_map/ppermute | solution.py:280
  134.7 9.4 %collective-permute-start.9 = (f32[288,32]{1,0:T(8,128)}, f32[288,32]{1,0:T(8,128)}, u32[]{:S(2)}, u32[]{:S(2)}) collective-permute-start(f32[288,32]{1,0:T(8,128)} %slice_add_fusion), channel_id=1, source_target_pairs={{0,8},{4,12},{8,0},{12,4},{16,24},{20,28},{24,16},{28,20},{1,9},{5... | collective-permute-start | bytes 110600 | tf_op jit(solution)/shard_map/ppermute | solution.py:280
  138.2 10.2 %collective-permute-start.7 = (bf16[66,32]{0,1:T(8,128)(2,1)S(1)}, bf16[66,32]{0,1:T(8,128)(2,1)S(1)}, u32[]{:S(2)}, u32[]{:S(2)}) collective-permute-start(bf16[66,32]{0,1:T(8,128)(2,1)S(1)} %bitcast.56), channel_id=1, source_target_pairs={{1,0},{2,1},{3,2},{5,4},{6,5},{7,6},{9,8},{10,9},{11,10},{13,12},{... | collective-permute-start | bytes 12680 | tf_op jit(solution)/shard_map/ppermute | solution.py:264
  139.5 7.9 %collective-permute-start.6 = (bf16[66,32]{0,1:T(8,128)(2,1)S(1)}, bf16[66,32]{0,1:T(8,128)(2,1)S(1)}, u32[]{:S(2)}, u32[]{:S(2)}) collective-permute-start(bf16[66,32]{0,1:T(8,128)(2,1)S(1)} %bitcast.58), channel_id=1, source_target_pairs={{0,1},{1,2},{2,3},{4,5},{5,6},{6,7},{8,9},{9,10},{10,11},{12,13},{... | collective-permute-start | bytes 12680 | tf_op jit(solution)/shard_map/ppermute | solution.py:263
  145.8 7.6 %collective-permute-start.10 = (f32[288,32]{1,0:T(8,128)}, f32[288,32]{1,0:T(8,128)}, u32[]{:S(2)}, u32[]{:S(2)}) collective-permute-start(f32[288,32]{1,0:T(8,128)} %add.69), channel_id=1, source_target_pairs={{0,16},{4,20},{8,24},{12,28},{16,0},{20,4},{24,8},{28,12},{1,17},{... | collective-permute-start | bytes 110600 | tf_op jit(solution)/shard_map/ppermute | solution.py:280
  154.3 5.8 %collective-permute-start.11 = (f32[288,32]{1,0:T(8,128)S(1)}, f32[288,32]{1,0:T(8,128)S(1)}, u32[]{:S(2)}, u32[]{:S(2)}) collective-permute-start(f32[288,32]{1,0:T(8,128)S(1)} %add.70), channel_id=1, source_target_pairs={{0,1},{1,0},{2,3},{3,2},{4,5},{5,4},{6,7},{7,6},{8,9},{9,8},{10,11... | collective-permute-start | bytes 110600 | tf_op jit(solution)/shard_map/ppermute | solution.py:280
  155.5 7.2 %copy-start.11 = (bf16[256,960]{1,0:T(8,128)(2,1)S(1)}, bf16[256,960]{1,0:T(8,128)(2,1)}, u32[]{:S(2)}) copy-start(bf16[256,960]{1,0:T(8,128)(2,1)} %copy-done.10) | copy-start | bytes 1474564
  160.2 9.0 %collective-permute-start.12 = (f32[288,32]{1,0:T(8,128)S(1)}, f32[288,32]{1,0:T(8,128)S(1)}, u32[]{:S(2)}, u32[]{:S(2)}) collective-permute-start(f32[288,32]{1,0:T(8,128)S(1)} %add.71), channel_id=1, source_target_pairs={{0,2},{1,3},{2,0},{3,1},{4,6},{5,7},{6,4},{7,5},{8,10},{9,11},{10,... | collective-permute-start | bytes 110600 | tf_op jit(solution)/shard_map/ppermute | solution.py:280

commit v2 on v1

v2 whole, which is shorter than its diff:
```python
import functools
import math

import jax
import jax.numpy as jnp
import numpy as np
from jax import lax
from jax.experimental import pallas as pl
from jax.experimental.pallas import tpu as pltpu
from jax.sharding import PartitionSpec as P

M = 64
BLOCK = 8
QUAD = 8
f32 = jnp.float32
bf16 = jnp.bfloat16
ROWS = ("chips", "core")
BOTH = ("chips", "core", "cols")


def dot(left, right):
    return jnp.dot(left, right, preferred_element_type=f32)


def dot_tn(left, right):
    return lax.dot_general(
        left, right, (((0,), (0,)), ((), ())), preferred_element_type=f32
    )


def dot_nt(left, right):
    return lax.dot_general(
        left, right, (((1,), (1,)), ((), ())), preferred_element_type=f32
    )


def call(kernel, out_shape, scratch, flops, moved, *args, far=0):
    near = [pl.BlockSpec(memory_space=pltpu.VMEM)] * (len(args) - far)
    return pl.pallas_call(
        kernel,
        out_shape=out_shape,
        in_specs=[pl.BlockSpec(memory_space=pltpu.HBM)] * far + near,
        out_specs=jax.tree.map(lambda _: pl.BlockSpec(memory_space=pltpu.VMEM), out_shape),
        scratch_shapes=scratch,
        compiler_params=pltpu.CompilerParams(vmem_limit_bytes=20 << 20),
        cost_estimate=pl.CostEstimate(flops=flops, bytes_accessed=moved, transcendentals=0),
    )(*args)


def shape(dims, dtype):
    return jax.ShapeDtypeStruct(dims, dtype)


def row_table(total, places):
    modes = np.concatenate([np.arange(M), total - M + np.arange(M)])
    phase = modes[:, None] * np.arange(total)[None, :] % total
    angle = (phase * (2.0 * np.pi / total)).reshape(2 * M, places, total // places)
    c, s = np.cos(angle).transpose(1, 0, 2), np.sin(angle).transpose(1, 0, 2)
    table = np.stack([np.concatenate([c, s], 2), np.concatenate([-s, c], 2)], axis=2)
    return table.reshape(places, 4 * M, 2 * (total // places)).astype(np.float32)


def col_table(total, places):
    phase = np.arange(total)[:, None] * np.arange(M)[None, :] % total
    angle = (phase * (2.0 * np.pi / total)).reshape(places, total // places, M)
    c, s = np.cos(angle), -np.sin(angle)
    none = np.zeros_like(c)
    even = np.concatenate([c, none, s, none], axis=2)
    odd = np.concatenate([none, c, none, s], axis=2)
    return np.concatenate([even, odd], axis=1).astype(np.float32)


def split(table):
    high = table.astype(bf16)
    return high, (table - high.astype(f32)).astype(bf16)


class Plan:
    def __init__(self, channels):
        self.chips, self.cores, self.cols = (lax.axis_size(a) for a in BOTH)
        self.devices = self.chips * self.cores * self.cols
        self.block = 4 * channels
        self.blocks = M // 2
        self.staged = M == 64 and self.devices == self.blocks

    def shapes(self, dtype):
        if not self.staged:
            return (shape((self.blocks * self.block, 2 * M), dtype),)
        return (shape((self.cols * self.block, 2 * M), dtype),) * (self.cores * self.chips)

    def places(self):
        if not self.staged:
            return [(0, k * self.block) for k in range(self.blocks)]
        return [
            (k, q * self.block) for k in range(self.cores * self.chips) for q in range(self.cols)
        ]

    def rows(self, table_ref):
        if not self.staged:
            return table_ref[...]
        chip, core, col = (lax.axis_index(a) for a in BOTH)
        found = []
        for k in range(self.cores):
            for h in range(self.chips):
                for q in range(self.cols):
                    owner = ((chip ^ h) * self.cores + (core ^ k)) * self.cols + (col ^ q)
                    found.append(table_ref[pl.ds(pl.multiple_of(owner * 8, 8), 8), :])
        return jnp.concatenate(found, axis=0)


def forward_rows(rows):
    return jnp.concatenate(split(rows), axis=1)


def quad_to_modes(plan, cells, cols_table, rows_table, pieces, at):
    height, _ = cells[0].shape
    pairs = [jnp.concatenate(cells[k : k + 2], axis=1) for k in range(0, len(cells), 2)]
    lines = dot(jnp.concatenate(pairs, axis=0), cols_table).astype(bf16)
    for t in range(0, len(pairs), 2):
        sides = []
        for p in (t, t + 1):
            part = lines[p * height : (p + 1) * height]
            sides.append(jnp.concatenate([part[:, : 2 * M], part[:, 2 * M :]], axis=0))
        right = jnp.concatenate(sides, axis=1)
        modes = dot(rows_table, jnp.concatenate([right, right], axis=0))
        for k, (piece, row) in enumerate(plan.places()):
            block = modes[8 * k : 8 * k + 8]
            block = jnp.concatenate([block[:, : 2 * M], block[:, 2 * M :]], axis=0)
            start = row + at + 8 * t
            pieces[piece][start : start + 16, :] = block.astype(bf16)


def quad_to_cells(plan, pieces, at, rows_table, cols_high, cols_low, count):
    stacked = []
    for t in range(0, count // 2, 2):
        first, second = [], []
        for piece, row in plan.places():
            block = pieces[piece][row + at + 8 * t : row + at + 8 * t + 16, :].astype(f32)
            first.append(block[:8])
            second.append(block[8:])
        modes = jnp.concatenate(
            [jnp.concatenate(first, axis=0), jnp.concatenate(second, axis=0)], axis=1
        )
        lines = dot(rows_table, modes.astype(bf16)).astype(bf16)
        height = lines.shape[0] // 2
        for p in (0, 1):
            lanes = slice(2 * M * p, 2 * M * (p + 1))
            stacked.append(jnp.concatenate([lines[:height, lanes], lines[height:, lanes]], axis=1))
    stacked = jnp.concatenate(stacked, axis=0)
    cells = dot_nt(stacked, cols_high) + dot_nt(stacked, cols_low)
    width = cells.shape[1] // 2
    return [
        cells[(k // 2) * height : (k // 2 + 1) * height, (k % 2) * width : (k % 2 + 1) * width]
        for k in range(count)
    ]


def forward_kernel(plan, scale_rows, scale_cols, field_ref, cols_all, rows_all, *refs):
    pieces, (field_s, cols_s, rows_s, sems) = refs[:-4], refs[-4:]
    channels = field_ref.shape[0]
    steps = channels // QUAD
    copies = [
        pltpu.make_async_copy(rows_all.at[lax.axis_index(ROWS)], rows_s, sems.at[0]),
        pltpu.make_async_copy(cols_all.at[lax.axis_index("cols")], cols_s, sems.at[1]),
    ]
    for k in range(steps):
        part = pl.ds(k * QUAD, QUAD)
        copies.append(pltpu.make_async_copy(field_ref.at[part], field_s.at[part], sems.at[2 + k]))
    for copy in copies:
        copy.start()
    copies[0].wait()
    rows_table = forward_rows(plan.rows(rows_s) * scale_rows)
    copies[1].wait()
    cols_table = (cols_s[...] * scale_cols).astype(bf16)
    for k in range(steps):
        copies[2 + k].wait()
        cells = [field_s[k * QUAD + c] for c in range(QUAD)]
        quad_to_modes(plan, cells, cols_table, rows_table, pieces, k * QUAD * 4)


def middle_kernel(plan, count, *refs):
    modes, refs = refs[:count], refs[count:]
    conv_ref, cotangent_ref, rows_ref, cols_ref, out_ref, grad_ref = refs[:6]
    pieces = refs[6:]
    channels = cotangent_ref.shape[0]
    rows = plan.rows(rows_ref)
    rows_in = (rows.T.astype(bf16).astype(f32) / M).astype(bf16)
    rows_out = forward_rows(rows / M)
    cols_high, cols_low = split(cols_ref[...])
    root = math.sqrt(2.0 / math.pi)
    for at in range(0, channels, QUAD):
        cells = quad_to_cells(plan, modes, at * 4, rows_in, cols_high, cols_low, QUAD)
        kept = []
        for k in range(QUAD):
            pre = cells[k] + conv_ref[at + k]
            square = pre * pre
            turn = jnp.tanh(root * (pre + 0.044715 * (square * pre)))
            half = 0.5 * (1.0 + turn)
            out_ref[at + k] = (pre * half).astype(bf16)
            slope = half + 0.5 * pre * (1.0 - turn * turn) * (root * (1.0 + 0.134145 * square))
            grad = (cotangent_ref[at + k].astype(f32) * slope).astype(bf16)
            grad_ref[at + k] = grad
            kept.append(grad)
        quad_to_modes(plan, kept, cols_high, rows_out, pieces, at * 4)


def last_kernel(plan, count, scale_rows, scale_cols, *refs):
    modes = refs[:count]
    conv_ref, rows_ref, cols_ref, out_ref = refs[count:]
    channels = out_ref.shape[0]
    rows_in = (plan.rows(rows_ref) * scale_rows).T.astype(bf16)
    cols_high, cols_low = split(cols_ref[...] * scale_cols)
    for at in range(0, channels, QUAD):
        cells = quad_to_cells(plan, modes, at * 4, rows_in, cols_high, cols_low, QUAD)
        for k in range(QUAD):
            out_ref[at + k] = (cells[k] + conv_ref[at + k]).astype(bf16)


def turn_kernel(cells_ref, turned_ref, edges_ref, turned_s):
    channels, height, width = cells_ref.shape
    for c in range(channels):
        turned_s[pl.ds(c, height, stride=channels), :] = cells_ref[c].astype(f32)
    turned = turned_s[...].astype(bf16)
    turned_ref[...] = turned
    row = lax.broadcasted_iota(jnp.int32, (16, width), 0)
    col = lax.broadcasted_iota(jnp.int32, (16, width), 1)
    chosen = ((row == 0) & (col == 0)) | ((row == 1) & (col == width - 1))
    edges_ref[...] = dot_nt(chosen.astype(f32).astype(bf16), turned).astype(bf16)


def turn(cells):
    channels, height, width = cells.shape
    lines = (height * channels, width)
    return call(
        turn_kernel,
        (shape(lines, bf16), shape((16, lines[0]), bf16)),
        [pltpu.VMEM(lines, f32)],
        2 * cells.size * 16, cells.size * 4,
        cells,
    )


def band(weights):
    outs = weights.shape[3]
    flat = jnp.transpose(weights, (3, 0, 1, 2)).reshape(outs, -1)
    step = flat.shape[1] // 3
    rows = [
        jnp.pad(flat, ((0, 0), (step * k, step * (BLOCK - 1 - k)))) for k in range(BLOCK)
    ]
    return jnp.concatenate(rows, axis=0)


def stencil_kernel(turned_ref, left_ref, right_ref, top_ref, low_ref, band_ref, out_ref, wide_ref):
    lines, width = turned_ref.shape
    channels = wide_ref.shape[1] // 3
    row = lax.broadcasted_iota(jnp.int32, (2, width), 0)
    col = lax.broadcasted_iota(jnp.int32, (2, width), 1)
    chosen = ((row == 0) & (col == 0)) | ((row == 1) & (col == width - 1))
    chosen = chosen.astype(f32).astype(bf16)
    where = lax.broadcasted_iota(jnp.int32, (channels, width), 1)

    def widen(at, cells, sides):
        count = cells.shape[0] // channels
        halo = dot_tn(sides, chosen)
        wide = cells.astype(f32)
        before, after = pltpu.roll(wide, 1, 1), pltpu.roll(wide, width - 1, 1)
        for k in range(count):
            part = slice(k * channels, (k + 1) * channels)
            wide_ref[at + k, :channels] = jnp.where(where == 0, halo[part], before[part]).astype(bf16)
            wide_ref[at + k, channels : 2 * channels] = cells[part]
            wide_ref[at + k, 2 * channels :] = jnp.where(
                where == width - 1, halo[part], after[part]
            ).astype(bf16)

    widen(0, top_ref[:channels], top_ref[channels : channels + 2, :channels])
    height = lines // channels
    widen(height + 1, low_ref[:channels], low_ref[channels : channels + 2, :channels])
    step = BLOCK * channels
    for b in range(0, lines, step):
        sides = jnp.concatenate([left_ref[:, b : b + step], right_ref[:, b : b + step]], axis=0)
        widen(b // channels + 1, turned_ref[b : b + step], sides)
    matrix = band_ref[...]
    for b in range(0, height // BLOCK, 2):
        pair = [
            wide_ref[BLOCK * k : BLOCK * k + BLOCK + 2].reshape((BLOCK + 2) * 3 * channels, width)
            for k in (b, b + 1)
        ]
        both = dot(matrix, jnp.concatenate(pair, axis=1))
        for k in range(2):
            for i in range(BLOCK):
                line = both[i * channels : (i + 1) * channels, k * width : (k + 1) * width]
                out_ref[pl.ds(BLOCK * (b + k) + i, channels, stride=height), :] = line


def shifted(value, axis, up):
    count = lax.axis_size(axis)
    pairs = [(i, i + 1) if up else (i + 1, i) for i in range(count - 1)]
    return lax.ppermute(value, axis, pairs)


def stencil(turned, edges, matrix, channels):
    lines, width = turned.shape
    height = lines // channels
    left = shifted(edges[1:2], "cols", True)
    right = shifted(edges[0:1], "cols", False)

    def with_sides(cells, at):
        sides = jnp.concatenate([left[:, at : at + channels], right[:, at : at + channels]], axis=0)
        return jnp.concatenate([cells, jnp.pad(sides, ((0, 0), (0, width - channels)))], axis=0)

    top = shifted(with_sides(turned[lines - channels :], lines - channels), ROWS, True)
    low = shifted(with_sides(turned[:channels], 0), ROWS, False)
    conv, wide = call(
        stencil_kernel,
        (shape((lines, width), f32), shape((height + 2, 3 * channels, width), bf16)),
        [],
        2 * matrix.size * height * width // BLOCK,
        lines * width * 12 + matrix.size * 2,
        turned, left, right, top, low, matrix,
    )
    return conv.reshape(channels, height, width), wide


def kernel_grad_kernel(cells_ref, grad_ref, out_ref):
    height, lines, width = cells_ref.shape
    taken = grad_ref.shape[0] * BLOCK // (height - 2)
    channels = taken // BLOCK
    total = jnp.zeros(((BLOCK + 2) * lines, taken), f32)
    for b in range(0, (height - 2) // BLOCK, 2):
        cells = [
            cells_ref[BLOCK * k : BLOCK * k + BLOCK + 2].reshape((BLOCK + 2) * lines, width)
            for k in (b, b + 1)
        ]
        grads = [grad_ref[taken * k : taken * (k + 1)] for k in (b, b + 1)]
        total = total + dot_nt(jnp.concatenate(cells, axis=1), jnp.concatenate(grads, axis=1))
    place = lax.broadcasted_iota(jnp.int32, (3 * lines, taken), 1) // channels
    folded = jnp.zeros((3 * lines, taken), f32)
    for k in range(BLOCK):
        folded = folded + jnp.where(place == k, total[lines * k : lines * (k + 3)], 0.0)
    size = taken
    while size > 128:
        size //= 2
        folded = folded[:, :size] + folded[:, size : 2 * size]
    step = size // 2
    while step >= channels:
        folded = folded + pltpu.roll(folded, step, 1)
        step //= 2
    groups = size // channels
    rows = 3 * lines // groups
    place = lax.broadcasted_iota(jnp.int32, (rows, size), 1) // channels
    packed = jnp.zeros((rows, size), f32)
    for k in range(groups):
        packed = packed + jnp.where(place == k, folded[rows * k : rows * (k + 1)], 0.0)
    out_ref[...] = packed.astype(bf16)


def kernel_grad_here(cells, grad, channels):
    _, lines, _ = cells.shape
    return call(
        kernel_grad_kernel,
        shape((3 * lines * channels // 128, 128), bf16),
        [],
        2 * cells.size * BLOCK * channels,
        cells.size * 2 + grad.size * 2,
        cells, grad,
    )


def swapped(value, axis, step):
    count = lax.axis_size(axis)
    return lax.ppermute(value, axis, [(i, i ^ step) for i in range(count)])


def tree_sum(values):
    values = [v.astype(f32) for v in values]
    while len(values) > 1:
        values = [values[k] + values[k + 1] for k in range(0, len(values), 2)]
    return values[0]


def reduce_pieces(plan, pieces):
    kept, sent = pieces[: plan.chips], pieces[plan.chips :]
    chips = []
    for h in reversed(range(plan.chips)):
        total = kept[h].astype(f32) + swapped(sent[h], "core", 1).astype(f32)
        chips.append(swapped(total.astype(bf16), "chips", h) if h else total)
    total = tree_sum(chips)
    parts = []
    for q in reversed(range(plan.cols)):
        part = total[q * plan.block : (q + 1) * plan.block].astype(bf16)
        parts.append(swapped(part, "cols", q) if q else part)
    return parts


def spread_block(plan, block, extra=None):
    def widen(value, axis, count):
        rows = value.shape[0]
        whole = value if extra is None else jnp.concatenate([value, summed.astype(bf16)], axis=0)
        got = {q: swapped(whole, axis, q) for q in reversed(range(1, count))}
        got[0] = whole
        found = [got[q] for q in range(count)]
        total = None if extra is None else tree_sum([v[rows:] for v in found])
        return [v[:rows] for v in found], total

    summed = extra
    found, summed = widen(block, "cols", plan.cols)
    here = jnp.concatenate(found, axis=0)
    pieces, summed = widen(here, "chips", plan.chips)
    pieces = pieces + [swapped(v, "core", 1) for v in pieces]
    if extra is not None:
        half = summed.astype(bf16)
        summed = tree_sum([half, swapped(half, "core", 1)])
    return pieces, summed


def to_lines(parts, total_s, re_s, im_s):
    total = parts[0][...].astype(f32)
    for part in parts[1:]:
        total = total + part[...].astype(f32)
    total_s[...] = total
    pairs = total.shape[0] // 8
    low = lax.broadcasted_iota(jnp.int32, (pairs, 2 * M), 1) < M
    for side, held in enumerate((re_s, im_s)):
        for t in range(2):
            one = total_s[pl.ds(4 * t + side, pairs, stride=8), :]
            two = total_s[pl.ds(4 * t + 2 + side, pairs, stride=8), :]
            even = jnp.where(low, one, pltpu.roll(two, M, 1))
            odd = jnp.where(low, pltpu.roll(one, M, 1), two)
            held[t, pl.ds(0, pairs, stride=2), :] = even
            held[t, pl.ds(1, pairs, stride=2), :] = odd
    return tuple(jnp.concatenate([held[0], held[1]], axis=1) for held in (re_s, im_s))


def from_lines(real, imag, total_s, re_s, out_ref):
    pairs = real.shape[0] // 2
    low = lax.broadcasted_iota(jnp.int32, (pairs, 2 * M), 1) < M
    for side, value in enumerate((real, imag)):
        for t in range(2):
            re_s[t] = value[:, 2 * M * t : 2 * M * (t + 1)]
            even = re_s[t, pl.ds(0, pairs, stride=2), :]
            odd = re_s[t, pl.ds(1, pairs, stride=2), :]
            one = jnp.where(low, even, pltpu.roll(odd, M, 1))
            two = jnp.where(low, pltpu.roll(even, M, 1), odd)
            total_s[pl.ds(4 * t + side, pairs, stride=8), :] = one
            total_s[pl.ds(4 * t + 2 + side, pairs, stride=8), :] = two
    out_ref[...] = total_s[...].astype(bf16)


def mix_kernel(*refs):
    parts, refs = refs[:-8], refs[-8:]
    real_ref, imag_ref, out_ref, coef_real_ref, coef_imag_ref, total_s, re_s, im_s = refs
    channels = real_ref.shape[0]
    real, imag = to_lines(parts, total_s, re_s, im_s)
    coef_real_ref[...] = real
    coef_imag_ref[...] = imag
    mixed_real = jnp.zeros(real_ref.shape[1:], f32)
    mixed_imag = jnp.zeros(real_ref.shape[1:], f32)
    for c in range(channels):
        wr, wi = real_ref[c].astype(f32), imag_ref[c].astype(f32)
        re, im = real[c : c + 1], imag[c : c + 1]
        mixed_real = mixed_real + (re * wr - im * wi)
        mixed_imag = mixed_imag + (re * wi + im * wr)
    from_lines(mixed_real, mixed_imag, total_s, re_s, out_ref)


def unmix_kernel(*refs):
    parts, refs = refs[:-10], refs[-10:]
    real_ref, imag_ref, out_ref, mode_real_ref, mode_imag_ref, total_s, re_s, im_s, du_re, du_im = refs
    channels = real_ref.shape[0]
    real, imag = to_lines(parts, total_s, re_s, im_s)
    mode_real_ref[...] = real
    mode_imag_ref[...] = imag
    for c in range(channels):
        wr, wi = real_ref[c].astype(f32), imag_ref[c].astype(f32)
        du_re[c : c + 1, :] = jnp.sum(wr * real + wi * imag, axis=0, keepdims=True)
        du_im[c : c + 1, :] = jnp.sum(wr * imag - wi * real, axis=0, keepdims=True)
    from_lines(du_re[...], du_im[...], total_s, re_s, out_ref)


def owner_stage(kernel, parts, real, imag, extra):
    channels, _, modes = real.shape
    return call(
        kernel,
        (shape(parts[0].shape, bf16), shape((channels, modes), f32), shape((channels, modes), f32)),
        [pltpu.VMEM((4 * channels, 2 * M), f32)]
        + [pltpu.VMEM((2, channels, 2 * M), f32)] * 2
        + [pltpu.VMEM((channels, modes), f32)] * extra,
        8 * real.size,
        parts[0].size * 10 + real.size * 4,
        *parts, real, imag,
    )


def exact(form, left, right):
    return jnp.einsum(form, left, right, precision=lax.Precision.HIGHEST, preferred_element_type=f32)


def at_owner(plan, partial, weight_real, weight_imag, forward, extra=None):
    channels, _, modes = weight_real.shape
    if plan.staged:
        parts = reduce_pieces(plan, partial)
        kernel = mix_kernel if forward else unmix_kernel
        sent, real, imag = owner_stage(kernel, parts, weight_real, weight_imag, 0 if forward else 2)
        pieces, summed = spread_block(plan, sent, extra)
        return pieces, real, imag, summed
    swap = lambda x: lax.all_to_all(x, BOTH, 0, 0, tiled=True)
    pieces = M // modes
    held = (plan.blocks, channels // 2, 4, 2, 2, pieces, modes)
    parts = partial[0].reshape(held).transpose(0, 2, 5, 1, 4, 3, 6)
    parts = swap(parts.reshape(plan.devices, channels, 2, modes))
    total = jnp.sum(parts.astype(f32), axis=0)
    real, imag = total[:, 0], total[:, 1]
    wr, wi = weight_real.astype(f32), weight_imag.astype(f32)
    if forward:
        re = exact("cm,com->om", real, wr) - exact("cm,com->om", imag, wi)
        im = exact("cm,com->om", real, wi) + exact("cm,com->om", imag, wr)
    else:
        re = exact("com,om->cm", wr, real) + exact("com,om->cm", wi, imag)
        im = exact("com,om->cm", wr, imag) - exact("com,om->cm", wi, real)
    sent = jnp.stack([re, im], axis=1).astype(bf16)
    sent = swap(jnp.broadcast_to(sent, (plan.devices,) + sent.shape))
    held = (plan.blocks, 4, pieces, channels // 2, 2, 2, modes)
    spread = sent.reshape(held).transpose(0, 3, 1, 5, 4, 2, 6)
    summed = None if extra is None else lax.psum(extra.astype(f32), BOTH)
    return [spread.reshape(2 * M * channels, 2 * M)], real, imag, summed


def layer(field, cotangent, weight_real, weight_imag, kernel):
    channels, rows_here, cols_here = field.shape
    places_rows, places_cols = lax.axis_size(ROWS), lax.axis_size("cols")
    total_rows, total_cols = rows_here * places_rows, cols_here * places_cols
    scale_rows, scale_cols = 1.0 / math.sqrt(total_rows), 1.0 / math.sqrt(total_cols)
    scale_cells = 1.0 / math.sqrt(total_rows * total_cols)
    all_rows = jnp.asarray(row_table(total_rows, places_rows))
    all_cols = jnp.asarray(col_table(total_cols, places_cols))
    plan = Plan(channels)
    cells = field.size
    modes = 4 * M * M * channels
    transform = 2 * cells * 4 * M + 4 * modes * rows_here
    pieces = plan.shapes(bf16)

    partial = call(
        functools.partial(forward_kernel, plan, scale_rows, scale_cols),
        pieces,
        [
            pltpu.VMEM(field.shape, bf16),
            pltpu.VMEM(all_cols.shape[1:], f32),
            pltpu.VMEM(all_rows.shape[1:], f32),
            pltpu.SemaphoreType.DMA((2 + channels // QUAD,)),
        ],
        transform, cells * 2 + modes * 2,
        field, all_cols, all_rows,
        far=3,
    )
    spectrum, coef_real, coef_imag, _ = at_owner(plan, partial, weight_real, weight_imag, True)
    rows = lax.dynamic_index_in_dim(all_rows, lax.axis_index(ROWS), 0, keepdims=False)
    cols = lax.dynamic_index_in_dim(all_cols, lax.axis_index("cols"), 0, keepdims=False)
    turned, edges = turn(field)
    matrix = band(kernel)
    conv, wide_field = stencil(turned, edges, matrix, channels)

    activated, grad, *partial_grad = call(
        functools.partial(middle_kernel, plan, len(spectrum)),
        (shape(field.shape, bf16), shape(field.shape, bf16)) + pieces,
        [],
        2 * transform, cells * 12 + modes * 4,
        *spectrum, conv, cotangent, rows, cols,
    )
    grad_turned, grad_edges = turn(grad)
    local = kernel_grad_here(wide_field, grad_turned, channels)
    spectrum_grad, mode_real, mode_imag, summed = at_owner(
        plan, partial_grad, weight_real, weight_imag, False, local
    )
    matrix = band(jnp.transpose(kernel[::-1, ::-1], (0, 1, 3, 2)))
    conv_grad, _ = stencil(grad_turned, grad_edges, matrix, channels)
    summed = summed.reshape(summed.shape[0], 128 // channels, channels).transpose(1, 0, 2)
    kernel_grad = summed.reshape(3, 3, channels, channels) * scale_cells

    weight_scale = M * scale_cells
    out_real = (
        coef_real[:, None, :] * mode_real[None] + coef_imag[:, None, :] * mode_imag[None]
    ) * weight_scale
    out_imag = (
        coef_real[:, None, :] * mode_imag[None] - coef_imag[:, None, :] * mode_real[None]
    ) * weight_scale

    field_grad = call(
        functools.partial(last_kernel, plan, len(spectrum_grad), scale_rows, scale_cols),
        shape(field.shape, bf16),
        [],
        transform, cells * 8 + modes * 2,
        *spectrum_grad, conv_grad, rows, cols,
    )
    return activated, field_grad, out_real, out_imag, kernel_grad


def solution(mesh):
    count_rows, count_cols = mesh.shape["rows"], mesh.shape["cols"]
    devices = mesh.devices.reshape(count_rows // 2, 2, count_cols)
    halved = jax.sharding.Mesh(devices, BOTH)
    placed = (
        P(None, ROWS, "cols"),
        P(None, ROWS, "cols"),
        P(None, None, BOTH),
        P(None, None, BOTH),
        P(),
    )
    return jax.shard_map(layer, mesh=halved, in_specs=placed, out_specs=placed, check_vma=False)
```

time: 176 us -> 125 us (0.71)
  waiting for transfers between devices: 62.6 us -> 30 us
  local copies, waits for them, and re-layouts: 26.5 us -> 18.1 us
  other arithmetic: 10.4 us -> 5.8 us
  Pallas kernels: 18.9 us -> 14.8 us
    all_to_all x4 -> x0, waiting for transfers between devices: 44.6 us -> none  [at_owner(): swap = lambda x: lax.all_to_all(x, BOTH, 0, 0, tiled=True)]
    all_to_all x4 -> x0, starting transfers between devices: 26.4 us -> none  [at_owner(): swap = lambda x: lax.all_to_all(x, BOTH, 0, 0, tiled=True)]
    ppermute x13 -> x49, starting transfers between devices: 28.5 us -> 54.1 us  [the longest x41 37.4 us: swapped(): return lax.ppermute(value, axis, [(i, i ^ step) for i in range(count)])]
    ppermute x13 -> x49, waiting for transfers between devices: 18 us -> 30 us  [the longest x41 25.3 us: swapped(): return lax.ppermute(value, axis, [(i, i ^ step) for i in range(count)])]
    broadcast_in_dim x4 -> x0, local copies, waits for them, and re-layouts: 5.28 us -> none  [the longest x2 3.39 us: widened(): final = lax.ppermute(tall[:, :, 0], 'cols', left)[:, :, None]]
    concatenate x4 -> x11, other arithmetic: 4.75 us -> 0.12 us  [the longest x4 0.05 us: with_sides(): jnp.concatenate([left[:, at:at + channels], right[:, at:at + channels]],...]
    pallas_call x8 -> x10, Pallas kernels: 18.9 us -> 14.8 us  [call(): pl.pallas_call(kernel, out_shape=out_shape, in_specs=[pl.BlockSpec(memory...]
    squeeze x7 -> x2, local copies, waits for them, and re-layouts: 5.71 us -> 1.9 us  [the longest x1 0.98 us: layer(): lax.dynamic_index_in_dim(all_cols, lax.axis_index('cols'), 0, keepdims=Fa...]
  transfers between devices with their start and end apart: 17 -> 49, of which waited for: 8 -> 18; matrix products, arithmetic and copies ran while one was open for 15% -> 16% of each run, Pallas kernels for 2% -> 5%
where the time goes in v2:
time: 125 us; the launch traced here: 124 us
  starting transfers between devices  54.1 us (43%)
  waiting for transfers between devices  30 us (24%)
  local copies, waits for them, and re-layouts  18.1 us (14%)
  Pallas kernels  14.8 us (12%)
  other arithmetic  5.8 us (5%)
    ppermute x41, starting transfers between devices, swapped(): return lax.ppermute(value, axis, [(i, i ^ step) for i in range(count)])  37.4 us
    ppermute x41, waiting for transfers between devices, swapped(): return lax.ppermute(value, axis, [(i, i ^ step) for i in range(count)])  25.3 us
    ppermute x8, starting transfers between devices, shifted(): return lax.ppermute(value, axis, pairs)  16.7 us
    pallas_call x10, Pallas kernels, call(): pl.pallas_call(kernel, out_shape=out_shape, in_specs=[pl.BlockSpec(memory...  14.8 us
    unnamed x40, local copies, waits for them, and re-layouts  10.3 us
    ppermute x8, waiting for transfers between devices, shifted(): return lax.ppermute(value, axis, pairs)  4.66 us
    convert_element_type x6, other arithmetic, reduce_pieces(): chips.append(swapped(total.astype(bf16), 'chips', h) if h else total)  2.95 us
  transfers between devices with their start and end apart: 49, of which 18 were waited for; matrix products, arithmetic and copies ran while one was open for 16% of the time, Pallas kernels for 5%

profile of v2, /device:TPU:0, one launch (start us, length us, event | category | flops | bytes accessed | tf_op | source)
XLA Modules:
  0.0 123.9 jit_solution(18115584449544120765)
XLA Ops:
  0.6 1.0 copy-done
  1.7 1.2 copy-done.3
  2.9 1.2 copy-done.4
  4.1 2.7 %shard_map.110 = (bf16[512,128]{1,0:T(8,128)(2,1)S(1)}, bf16[512,128]{1,0:T(8,128)(2,1)S(1)}, bf16[512,128]{1,0:T(8,128)(2,1)S(1)}, bf16[512,128]{1,0:T(8,128)(2...) custom-call(bf16[32,64,128]{2,1,0:T(8,128)(2,1)S(1)} %copy-done, ...), custom_call_target="tpu_custom_call" | custom-call | flops 268435456 | bytes 1572864 | tf_op jit(solution)/shard_map/pallas_call | solution.py:39
  8.0 0.8 shard_map.112
  9.4 1.3 %collective-permute-start.21 = (bf16[1,2048]{1,0:T(2,128)(2,1)}, bf16[1,2048]{1,0:T(2,128)(2,1)S(1)}, u32[]{:S(2)}, u32[]{:S(2)}) collective-permute-start(bf16[1,2048]{1,0:T(2,128)(2,1)} %get-tuple-element.90), channel_id=1, source_target_pairs={{1,0},{2,1},{3,2},{5,4},{6,5},{7,6},{9,8},{10,9},{11,10},{13,12},{... | collective-permute-start | bytes 12296 | tf_op jit(solution)/shard_map/ppermute | solution.py:298
  12.6 0.9 dynamic-slice_bitcast_fusion.1.refs_10_.refs_9_
  13.5 1.0 dynamic-slice_bitcast_fusion.refs_11_.refs_10_
  14.5 1.7 %copy.19 = bf16[32,3,3,32]{3,2,1,0:T(4,128)(2,1)} copy(bf16[32,3,3,32]{3,0,2,1:T(8,128)(2,1)} %reverse_bitcast_fusion) | data formatting | bytes 36864 | tf_op jit(solution)/shard_map/transpose;transpose | solution.py:245
  16.2 1.6 %reshape.34 = bf16[32,288]{1,0:T(8,128)(2,1)} reshape(bf16[32,3,3,32]{3,2,1,0:T(4,128)(2,1)} %copy.19) | data formatting | bytes 36864 | tf_op jit(solution)/shard_map/reshape | solution.py:245
  18.5 0.8 pad_dynamic-update-slice_fusion.6
  19.4 0.8 pad_dynamic-update-slice_fusion.5
  20.2 0.8 pad_dynamic-update-slice_fusion.4
  22.6 0.8 pad_dynamic-update-slice_fusion.1
  23.4 5.5 %collective-permute-start.20 = (bf16[1,2048]{1,0:T(2,128)(2,1)}, bf16[1,2048]{1,0:T(2,128)(2,1)S(1)}, u32[]{:S(2)}, u32[]{:S(2)}) collective-permute-start(bf16[1,2048]{1,0:T(2,128)(2,1)} %get-tuple-element.91), channel_id=1, source_target_pairs={{0,1},{1,2},{2,3},{4,5},{5,6},{6,7},{8,9},{9,10},{10,11},{12,13},{... | collective-permute-start | bytes 12296 | tf_op jit(solution)/shard_map/ppermute | solution.py:298
  29.0 0.9 add_convert_fusion.5
  29.9 2.0 %collective-permute-start.5 = (bf16[512,128]{1,0:T(8,128)(2,1)S(1)}, bf16[512,128]{1,0:T(8,128)(2,1)S(1)}, u32[]{:S(2)}, u32[]{:S(2)}) collective-permute-start(bf16[512,128]{1,0:T(8,128)(2,1)S(1)} %add_convert_fusion.5), channel_id=1, source_target_pairs={{0,8},{8,0},{16,24},{24,16},{1,9},{9,1},{17,25},{25,17},{2,10},{10... | collective-permute-start | bytes 393224 | tf_op jit(solution)/shard_map/ppermute | solution.py:371
  31.9 0.9 add_convert_fusion.6
  32.9 1.6 %collective-permute-start.3 = (bf16[512,128]{1,0:T(8,128)(2,1)S(1)}, bf16[512,128]{1,0:T(8,128)(2,1)S(1)}, u32[]{:S(2)}, u32[]{:S(2)}) collective-permute-start(bf16[512,128]{1,0:T(8,128)(2,1)S(1)} %add_convert_fusion.6), channel_id=1, source_target_pairs={{0,16},{8,24},{16,0},{24,8},{1,17},{9,25},{17,1},{25,9},{2,18},{10... | collective-permute-start | bytes 393224 | tf_op jit(solution)/shard_map/ppermute | solution.py:371
  34.5 0.9 add_convert_fusion.7
  35.6 4.2 %collective-permute-done.3 = bf16[512,128]{1,0:T(8,128)(2,1)S(1)} collective-permute-done((bf16[512,128]{1,0:T(8,128)(2,1)S(1)}, bf16[512,128]{1,0:T(8,128)(2,1)S(1)}, u32[]{:S(2)}, u32[]{:S(2)}) %collective-permute-start.3) | collective-permute-done | bytes 131104 | tf_op jit(solution)/shard_map/ppermute | solution.py:371
  39.8 1.6 %collective-permute-done.1 = bf16[512,128]{1,0:T(8,128)(2,1)S(1)} collective-permute-done((bf16[512,128]{1,0:T(8,128)(2,1)S(1)}, bf16[512,128]{1,0:T(8,128)(2,1)S(1)}, u32[]{:S(2)}, u32[]{:S(2)}) %collective-permute-start.1) | collective-permute-done | bytes 131104 | tf_op jit(solution)/shard_map/ppermute | solution.py:371
  41.3 1.0 add_convert_fusion.4
  42.4 1.5 %collective-permute-start.7 = (bf16[128,128]{1,0:T(8,128)(2,1)S(1)}, bf16[128,128]{1,0:T(8,128)(2,1)S(1)}, u32[]{:S(2)}, u32[]{:S(2)}) collective-permute-start(bf16[128,128]{1,0:T(8,128)(2,1)S(1)} %get-tuple-element.87), channel_id=1, source_target_pairs={{0,3},{1,2},{2,1},{3,0},{4,7},{5,6},{6,5},{7,4},{8,11},{9,10},{10,... | collective-permute-start | bytes 98312 | tf_op jit(solution)/shard_map/ppermute | solution.py:371
  43.8 1.6 %collective-permute-start.8 = (bf16[128,128]{1,0:T(8,128)(2,1)S(1)}, bf16[128,128]{1,0:T(8,128)(2,1)S(1)}, u32[]{:S(2)}, u32[]{:S(2)}) collective-permute-start(bf16[128,128]{1,0:T(8,128)(2,1)S(1)} %get-tuple-element.86), channel_id=1, source_target_pairs={{0,2},{1,3},{2,0},{3,1},{4,6},{5,7},{6,4},{7,5},{8,10},{9,11},{10,... | collective-permute-start | bytes 98312 | tf_op jit(solution)/shard_map/ppermute | solution.py:371
  45.5 1.3 %collective-permute-start.9 = (bf16[128,128]{1,0:T(8,128)(2,1)S(1)}, bf16[128,128]{1,0:T(8,128)(2,1)S(1)}, u32[]{:S(2)}, u32[]{:S(2)}) collective-permute-start(bf16[128,128]{1,0:T(8,128)(2,1)S(1)} %get-tuple-element.85), channel_id=1, source_target_pairs={{0,1},{1,0},{2,3},{3,2},{4,5},{5,4},{6,7},{7,6},{8,9},{9,8},{10,11... | collective-permute-start | bytes 98312 | tf_op jit(solution)/shard_map/ppermute | solution.py:371
  46.8 1.3 %collective-permute-start.22 = (bf16[34,128]{1,0:T(8,128)(2,1)S(1)}, bf16[34,128]{1,0:T(8,128)(2,1)S(1)}, u32[]{:S(2)}, u32[]{:S(2)}) collective-permute-start(bf16[34,128]{1,0:T(8,128)(2,1)S(1)} %pad_maximum_fusion.2), channel_id=1, source_target_pairs={{0,4},{4,8},{8,12},{12,16},{16,20},{20,24},{24,28},{1,5},{5,9},{9,... | collective-permute-start | bytes 26120 | tf_op jit(solution)/shard_map/ppermute | solution.py:298
  50.0 1.4 %collective-permute-start.10 = (bf16[128,128]{1,0:T(8,128)(2,1)S(1)}, bf16[128,128]{1,0:T(8,128)(2,1)S(1)}, u32[]{:S(2)}, u32[]{:S(2)}) collective-permute-start(bf16[128,128]{1,0:T(8,128)(2,1)S(1)} %get-tuple-element.44), channel_id=1, source_target_pairs={{0,1},{1,0},{2,3},{3,2},{4,5},{5,4},{6,7},{7,6},{8,9},{9,8},{10,11... | collective-permute-start | bytes 98312 | tf_op jit(solution)/shard_map/ppermute | solution.py:371
  51.4 1.7 %collective-permute-start.11 = (bf16[128,128]{1,0:T(8,128)(2,1)S(1)}, bf16[128,128]{1,0:T(8,128)(2,1)S(1)}, u32[]{:S(2)}, u32[]{:S(2)}) collective-permute-start(bf16[128,128]{1,0:T(8,128)(2,1)S(1)} %get-tuple-element.44), channel_id=1, source_target_pairs={{0,2},{1,3},{2,0},{3,1},{4,6},{5,7},{6,4},{7,5},{8,10},{9,11},{10,... | collective-permute-start | bytes 98312 | tf_op jit(solution)/shard_map/ppermute | solution.py:371
  53.1 1.4 %collective-permute-start.12 = (bf16[128,128]{1,0:T(8,128)(2,1)S(1)}, bf16[128,128]{1,0:T(8,128)(2,1)S(1)}, u32[]{:S(2)}, u32[]{:S(2)}) collective-permute-start(bf16[128,128]{1,0:T(8,128)(2,1)S(1)} %get-tuple-element.44), channel_id=1, source_target_pairs={{0,3},{1,2},{2,1},{3,0},{4,7},{5,6},{6,5},{7,4},{8,11},{9,10},{10,... | collective-permute-start | bytes 98312 | tf_op jit(solution)/shard_map/ppermute | solution.py:371
  54.4 2.5 %collective-permute-done.11 = bf16[128,128]{1,0:T(8,128)(2,1)S(1)} collective-permute-done((bf16[128,128]{1,0:T(8,128)(2,1)S(1)}, bf16[128,128]{1,0:T(8,128)(2,1)S(1)}, u32[]{:S(2)}, u32[]{:S(2)}) %collective-permute-start.11) | collective-permute-done | bytes 32800 | tf_op jit(solution)/shard_map/ppermute | solution.py:371
  56.9 1.9 %collective-permute-done.12 = bf16[128,128]{1,0:T(8,128)(2,1)S(1)} collective-permute-done((bf16[128,128]{1,0:T(8,128)(2,1)S(1)}, bf16[128,128]{1,0:T(8,128)(2,1)S(1)}, u32[]{:S(2)}, u32[]{:S(2)}) %collective-permute-start.12) | collective-permute-done | bytes 32800 | tf_op jit(solution)/shard_map/ppermute | solution.py:371
  59.3 0.9 collective-permute-start.14
  60.2 2.1 %collective-permute-start.15 = (bf16[512,128]{1,0:T(8,128)(2,1)S(1)}, bf16[512,128]{1,0:T(8,128)(2,1)S(1)}, u32[]{:S(2)}, u32[]{:S(2)}) collective-permute-start(bf16[512,128]{1,0:T(8,128)(2,1)S(1)} %constant_dynamic-update-slice_fusion.refs_0_), channel_id=1, source_target_pairs={{0,24},{8,16},{16,8},{24,0},{1,25},{9,17},{17,9},{25,1},{2,26},{10... | collective-permute-start | bytes 393224 | tf_op jit(solution)/shard_map/ppermute | solution.py:371
  62.3 1.3 %collective-permute-start.23 = (bf16[34,128]{1,0:T(8,128)(2,1)S(1)}, bf16[34,128]{1,0:T(8,128)(2,1)S(1)}, u32[]{:S(2)}, u32[]{:S(2)}) collective-permute-start(bf16[34,128]{1,0:T(8,128)(2,1)S(1)} %pad_maximum_fusion.3), channel_id=1, source_target_pairs={{4,0},{8,4},{12,8},{16,12},{20,16},{24,20},{28,24},{5,1},{9,5},{13... | collective-permute-start | bytes 26120 | tf_op jit(solution)/shard_map/ppermute | solution.py:298
  63.6 1.2 collective-permute-start.16
  66.2 1.5 %shard_map.113 = (f32[2048,128]{1,0:T(8,128)S(1)}, bf16[66,96,128]{2,1,0:T(8,128)(2,1)S(1)}) custom-call(bf16[2048,128]{1,0:T(8,128)(2,1)S(1)} %get-tuple-element.45.turned_ref, bf16[1,2048]{1,0:T(2,128)(2,1)S(1)} %collective-permute-done.20.left_ref, bf16[1,2048]{1,0:T(2,128)(2,1)S(1)} %collective-permute-done.21.right_ref, ...), custom_call_target="tpu_custom_call" | custom-call | flops 503316480 | bytes 3637248 | tf_op jit(solution)/shard_map/pallas_call | solution.py:39
  67.8 3.3 %shard_map.114 = (bf16[32,64,128]{2,1,0:T(8,128)(2,1)}, bf16[32,64,128]{2,1,0:T(8,128)(2,1)S(1)}, bf16[512,128]{1,0:T(8,128)(2,1)S(1)}, bf16[512,128]{1,0:T(8,12...) custom-call(bf16[512,128]{1,0:T(8,128)(2,1)S(1)} %constant_dynamic-u, ...), custom_call_target="tpu_custom_call" | custom-call | flops 536870912 | bytes 5242880 | tf_op jit(solution)/shard_map/pallas_call | solution.py:39
  72.1 0.8 shard_map.116
  73.0 1.3 %collective-permute-start.45 = (bf16[1,2048]{1,0:T(2,128)(2,1)S(1)}, bf16[1,2048]{1,0:T(2,128)(2,1)S(1)}, u32[]{:S(2)}, u32[]{:S(2)}) collective-permute-start(bf16[1,2048]{1,0:T(2,128)(2,1)S(1)} %get-tuple-element.88), channel_id=1, source_target_pairs={{1,0},{2,1},{3,2},{5,4},{6,5},{7,6},{9,8},{10,9},{11,10},{13,12},{... | collective-permute-start | bytes 12296 | tf_op jit(solution)/shard_map/ppermute | solution.py:298
  74.3 0.9 shard_map.117
  75.2 3.4 %collective-permute-done.45.right_ref = bf16[1,2048]{1,0:T(2,128)(2,1)S(1)} collective-permute-done((bf16[1,2048]{1,0:T(2,128)(2,1)S(1)}, bf16[1,2048]{1,0:T(2,128)(2,1)S(1)}, u32[]{:S(2)}, u32[]{:S(2)}) %collective-permute-start.45) | collective-permute-done | bytes 4128 | tf_op jit(solution)/shard_map/ppermute | solution.py:298
  78.6 3.3 %collective-permute-start.44 = (bf16[1,2048]{1,0:T(2,128)(2,1)S(1)}, bf16[1,2048]{1,0:T(2,128)(2,1)S(1)}, u32[]{:S(2)}, u32[]{:S(2)}) collective-permute-start(bf16[1,2048]{1,0:T(2,128)(2,1)S(1)} %get-tuple-element.89), channel_id=1, source_target_pairs={{0,1},{1,2},{2,3},{4,5},{5,6},{6,7},{8,9},{9,10},{10,11},{12,13},{... | collective-permute-start | bytes 12296 | tf_op jit(solution)/shard_map/ppermute | solution.py:298
  81.9 1.3 %collective-permute-done.44.left_ref = bf16[1,2048]{1,0:T(2,128)(2,1)S(1)} collective-permute-done((bf16[1,2048]{1,0:T(2,128)(2,1)S(1)}, bf16[1,2048]{1,0:T(2,128)(2,1)S(1)}, u32[]{:S(2)}, u32[]{:S(2)}) %collective-permute-start.44) | collective-permute-done | bytes 4128 | tf_op jit(solution)/shard_map/ppermute | solution.py:298
  83.3 1.3 %collective-permute-start.46 = (bf16[34,128]{1,0:T(8,128)(2,1)S(1)}, bf16[34,128]{1,0:T(8,128)(2,1)S(1)}, u32[]{:S(2)}, u32[]{:S(2)}) collective-permute-start(bf16[34,128]{1,0:T(8,128)(2,1)S(1)} %pad_maximum_fusion.4), channel_id=1, source_target_pairs={{0,4},{4,8},{8,12},{12,16},{16,20},{20,24},{24,28},{1,5},{5,9},{9,... | collective-permute-start | bytes 26120 | tf_op jit(solution)/shard_map/ppermute | solution.py:298
  84.6 1.1 collective-permute-start.29
  85.7 0.9 collective-permute-start.27
  86.7 1.7 %collective-permute-start.25 = (bf16[512,128]{1,0:T(8,128)(2,1)S(1)}, bf16[512,128]{1,0:T(8,128)(2,1)S(1)}, u32[]{:S(2)}, u32[]{:S(2)}) collective-permute-start(bf16[512,128]{1,0:T(8,128)(2,1)S(1)} %add_convert_fusion.3), channel_id=1, source_target_pairs={{0,24},{8,16},{16,8},{24,0},{1,25},{9,17},{17,9},{25,1},{2,26},{10... | collective-permute-start | bytes 393224 | tf_op jit(solution)/shard_map/ppermute | solution.py:371
  88.4 1.5 %collective-permute-start.47 = (bf16[34,128]{1,0:T(8,128)(2,1)S(1)}, bf16[34,128]{1,0:T(8,128)(2,1)S(1)}, u32[]{:S(2)}, u32[]{:S(2)}) collective-permute-start(bf16[34,128]{1,0:T(8,128)(2,1)S(1)} %pad_maximum_fusion.5), channel_id=1, source_target_pairs={{4,0},{8,4},{12,8},{16,12},{20,16},{24,20},{28,24},{5,1},{9,5},{13... | collective-permute-start | bytes 26120 | tf_op jit(solution)/shard_map/ppermute | solution.py:298
  89.9 1.0 collective-permute-done.29
  90.9 3.8 %collective-permute-done.27 = bf16[512,128]{1,0:T(8,128)(2,1)S(1)} collective-permute-done((bf16[512,128]{1,0:T(8,128)(2,1)S(1)}, bf16[512,128]{1,0:T(8,128)(2,1)S(1)}, u32[]{:S(2)}, u32[]{:S(2)}) %collective-permute-start.27) | collective-permute-done | bytes 131104 | tf_op jit(solution)/shard_map/ppermute | solution.py:371
  94.9 2.2 %collective-permute-start.31 = (bf16[128,128]{1,0:T(8,128)(2,1)S(1)}, bf16[128,128]{1,0:T(8,128)(2,1)S(1)}, u32[]{:S(2)}, u32[]{:S(2)}) collective-permute-start(bf16[128,128]{1,0:T(8,128)(2,1)S(1)} %get-tuple-element.83), channel_id=1, source_target_pairs={{0,3},{1,2},{2,1},{3,0},{4,7},{5,6},{6,5},{7,4},{8,11},{9,10},{10,... | collective-permute-start | bytes 98312 | tf_op jit(solution)/shard_map/ppermute | solution.py:371
  97.1 1.6 %collective-permute-start.32 = (bf16[128,128]{1,0:T(8,128)(2,1)S(1)}, bf16[128,128]{1,0:T(8,128)(2,1)S(1)}, u32[]{:S(2)}, u32[]{:S(2)}) collective-permute-start(bf16[128,128]{1,0:T(8,128)(2,1)S(1)} %get-tuple-element.82), channel_id=1, source_target_pairs={{0,2},{1,3},{2,0},{3,1},{4,6},{5,7},{6,4},{7,5},{8,10},{9,11},{10,... | collective-permute-start | bytes 98312 | tf_op jit(solution)/shard_map/ppermute | solution.py:371
  99.3 1.7 %shard_map.118 = (f32[2048,128]{1,0:T(8,128)S(1)}, bf16[66,96,128]{2,1,0:T(8,128)(2,1)}) custom-call(bf16[2048,128]{1,0:T(8,128)(2,1)S(1)} %get-tuple-element.60.grad_ref.turned_ref, bf16[1,2048]{1,0:T(2,128)(2,1)S(1)} %collective-permute-done.44.left_ref, bf16[1,2048]{1,0:T(2,128)(2,1)S(1)} %collective-permute-done.45.right_ref, ...), custom_call_target="tpu_custom_call" | custom-call | flops 503316480 | bytes 3637248 | tf_op jit(solution)/shard_map/pallas_call | solution.py:39
  101.1 0.9 collective-permute-done.32.refs_1_
  104.0 1.8 %collective-permute-start.35 = (bf16[200,128]{1,0:T(8,128)(2,1)S(1)}, bf16[200,128]{1,0:T(8,128)(2,1)S(1)}, u32[]{:S(2)}, u32[]{:S(2)}) collective-permute-start(bf16[200,128]{1,0:T(8,128)(2,1)S(1)} %pad_maximum_fusion.1), channel_id=1, source_target_pairs={{0,2},{1,3},{2,0},{3,1},{4,6},{5,7},{6,4},{7,5},{8,10},{9,11},{10,... | collective-permute-start | bytes 153608 | tf_op jit(solution)/shard_map/ppermute | solution.py:371
  105.9 1.9 %collective-permute-start.36 = (bf16[200,128]{1,0:T(8,128)(2,1)S(1)}, bf16[200,128]{1,0:T(8,128)(2,1)S(1)}, u32[]{:S(2)}, u32[]{:S(2)}) collective-permute-start(bf16[200,128]{1,0:T(8,128)(2,1)S(1)} %pad_maximum_fusion.1), channel_id=1, source_target_pairs={{0,3},{1,2},{2,1},{3,0},{4,7},{5,6},{6,5},{7,4},{8,11},{9,10},{10,... | collective-permute-start | bytes 153608 | tf_op jit(solution)/shard_map/ppermute | solution.py:371
  107.8 2.3 %collective-permute-done.35 = bf16[200,128]{1,0:T(8,128)(2,1)S(1)} collective-permute-done((bf16[200,128]{1,0:T(8,128)(2,1)S(1)}, bf16[200,128]{1,0:T(8,128)(2,1)S(1)}, u32[]{:S(2)}, u32[]{:S(2)}) %collective-permute-start.35) | collective-permute-done | bytes 51232 | tf_op jit(solution)/shard_map/ppermute | solution.py:371
  110.1 1.6 %collective-permute-done.36 = bf16[200,128]{1,0:T(8,128)(2,1)S(1)} collective-permute-done((bf16[200,128]{1,0:T(8,128)(2,1)S(1)}, bf16[200,128]{1,0:T(8,128)(2,1)S(1)}, u32[]{:S(2)}, u32[]{:S(2)}) %collective-permute-start.36) | collective-permute-done | bytes 51232 | tf_op jit(solution)/shard_map/ppermute | solution.py:371
  111.8 0.9 collective-permute-start.37
  113.4 2.0 %collective-permute-start.39 = (bf16[584,128]{1,0:T(8,128)(2,1)S(1)}, bf16[584,128]{1,0:T(8,128)(2,1)S(1)}, u32[]{:S(2)}, u32[]{:S(2)}) collective-permute-start(bf16[584,128]{1,0:T(8,128)(2,1)S(1)} %get-tuple-element.72), channel_id=1, source_target_pairs={{0,24},{8,16},{16,8},{24,0},{1,25},{9,17},{17,9},{25,1},{2,26},{10... | collective-permute-start | bytes 448520 | tf_op jit(solution)/shard_map/ppermute | solution.py:371
  115.4 1.6 %subtract_multiply_fusion = (f32[32,32,256]{2,1,0:T(8,128)}, f32[32,32,256]{2,1,0:T(8,128)}) fusion(f32[32,256]{1,0:T(8,128)S(1)} %get-tuple-element.66, f32[32,256]{1,0:T(8,128)S(1)} %get-tuple-element.65, f32[32,256]{1,0:T(8,128)S(1)} %get-tuple-element.64, f32[32,256]{1,0:T(8,128)S(1)} %get-tuple-element.63), kind=kLoop, calls=%fused_computation | loop fusion | flops 2097152 | bytes 2228224 | tf_op jit(solution)/shard_map/mul | solution.py:583
  117.8 1.6 %collective-permute-done.39 = bf16[584,128]{1,0:T(8,128)(2,1)S(1)} collective-permute-done((bf16[584,128]{1,0:T(8,128)(2,1)S(1)}, bf16[584,128]{1,0:T(8,128)(2,1)S(1)}, u32[]{:S(2)}, u32[]{:S(2)}) %collective-permute-start.39) | collective-permute-done | bytes 149536 | tf_op jit(solution)/shard_map/ppermute | solution.py:371
  122.2 1.6 %shard_map.119 = bf16[32,64,128]{2,1,0:T(8,128)(2,1)} custom-call(bf16[512,128]{1,0:T(8,128)(2,1)S(1)} %pad_maximum_fusion.refs_0_, bf16[512,128]{1,0:T(8,128)(2,1)S(1)} %slice.170.refs_1_, bf16[512,128]{1,0:T(8,128)(2,1)S(1)} %slice.171.refs_2_, bf16[512,128]{1,0:T(8,128)(2,1)S(1)} %slice.172.refs_3_, bf16[512,128]{1,0:T(8,128)(2,1)S(1)} %collective-permute-done.40.refs_4_, ...), custom_call_target="tpu_custom_call" | custom-call | flops 268435456 | bytes 3145728 | tf_op jit(solution)/shard_map/pallas_call | solution.py:39
  (129 shorter events, 18.6 us)
Async XLA Ops:
  0.6 1.0 copy-start
  1.7 1.2 copy-start.3
  2.9 1.2 copy-start.4
  4.1 7.2 %copy-start.7 = (bf16[3,3,32,32]{3,2,1,0:T(8,128)(2,1)S(1)}, bf16[3,3,32,32]{3,2,1,0:T(8,128)(2,1)}, u32[]{:S(2)}) copy-start(bf16[3,3,32,32]{3,2,1,0:T(8,128)(2,1)} %param.11) | copy-start | bytes 55300
  6.8 28.8 %collective-permute-start.6 = (bf16[512,128]{1,0:T(8,128)(2,1)S(1)}, bf16[512,128]{1,0:T(8,128)(2,1)}, u32[]{:S(2)}, u32[]{:S(2)}) collective-permute-start(bf16[512,128]{1,0:T(8,128)(2,1)S(1)} %get-tuple-element.43), channel_id=1, source_target_pairs={{0,4},{4,0},{1,5},{5,1},{2,6},{6,2},{3,7},{7,3},{8,12},{12,8},{9,1... | collective-permute-start | bytes 393224 | tf_op jit(solution)/shard_map/ppermute | solution.py:371
  7.4 21.6 %collective-permute-start.4 = (bf16[512,128]{1,0:T(8,128)(2,1)S(1)}, bf16[512,128]{1,0:T(8,128)(2,1)}, u32[]{:S(2)}, u32[]{:S(2)}) collective-permute-start(bf16[512,128]{1,0:T(8,128)(2,1)S(1)} %get-tuple-element.41), channel_id=1, source_target_pairs={{0,4},{4,0},{1,5},{5,1},{2,6},{6,2},{3,7},{7,3},{8,12},{12,8},{9,1... | collective-permute-start | bytes 393224 | tf_op jit(solution)/shard_map/ppermute | solution.py:371
  7.4 24.5 %collective-permute-start.2 = (bf16[512,128]{1,0:T(8,128)(2,1)S(1)}, bf16[512,128]{1,0:T(8,128)(2,1)}, u32[]{:S(2)}, u32[]{:S(2)}) collective-permute-start(bf16[512,128]{1,0:T(8,128)(2,1)S(1)} %get-tuple-element.39), channel_id=1, source_target_pairs={{0,4},{4,0},{1,5},{5,1},{2,6},{6,2},{3,7},{7,3},{8,12},{12,8},{9,1... | collective-permute-start | bytes 393224 | tf_op jit(solution)/shard_map/ppermute | solution.py:371
  7.9 26.6 %collective-permute-start = (bf16[512,128]{1,0:T(8,128)(2,1)S(1)}, bf16[512,128]{1,0:T(8,128)(2,1)}, u32[]{:S(2)}, u32[]{:S(2)}) collective-permute-start(bf16[512,128]{1,0:T(8,128)(2,1)S(1)} %get-tuple-element.37), channel_id=1, source_target_pairs={{0,4},{4,0},{1,5},{5,1},{2,6},{6,2},{3,7},{7,3},{8,12},{12,8},{9,1... | collective-permute-start | bytes 393224 | tf_op jit(solution)/shard_map/ppermute | solution.py:371
  9.4 14.0 %collective-permute-start.21 = (bf16[1,2048]{1,0:T(2,128)(2,1)}, bf16[1,2048]{1,0:T(2,128)(2,1)S(1)}, u32[]{:S(2)}, u32[]{:S(2)}) collective-permute-start(bf16[1,2048]{1,0:T(2,128)(2,1)} %get-tuple-element.90), channel_id=1, source_target_pairs={{1,0},{2,1},{3,2},{5,4},{6,5},{7,6},{9,8},{10,9},{11,10},{13,12},{... | collective-permute-start | bytes 12296 | tf_op jit(solution)/shard_map/ppermute | solution.py:298
  14.5 34.9 %copy-start.1 = (bf16[32,32,256]{2,1,0:T(8,128)(2,1)S(1)}, bf16[32,32,256]{2,1,0:T(8,128)(2,1)}, u32[]{:S(2)}) copy-start(bf16[32,32,256]{2,1,0:T(8,128)(2,1)} %refs_4_.3) | copy-start | bytes 1572868
  14.5 34.9 %copy-start.2 = (bf16[32,32,256]{2,1,0:T(8,128)(2,1)S(1)}, bf16[32,32,256]{2,1,0:T(8,128)(2,1)}, u32[]{:S(2)}) copy-start(bf16[32,32,256]{2,1,0:T(8,128)(2,1)} %refs_5_.3) | copy-start | bytes 1572868
  17.8 29.0 %copy-start.8 = (bf16[32,128]{1,0:T(8,128)(2,1)S(1)}, bf16[32,128]{1,0:T(8,128)(2,1)}, u32[]{:S(2)}) copy-start(bf16[32,128]{1,0:T(8,128)(2,1)} %get-tuple-element.77) | copy-start | bytes 24580
  23.4 12.1 %collective-permute-start.20 = (bf16[1,2048]{1,0:T(2,128)(2,1)}, bf16[1,2048]{1,0:T(2,128)(2,1)S(1)}, u32[]{:S(2)}, u32[]{:S(2)}) collective-permute-start(bf16[1,2048]{1,0:T(2,128)(2,1)} %get-tuple-element.91), channel_id=1, source_target_pairs={{0,1},{1,2},{2,3},{4,5},{5,6},{6,7},{8,9},{9,10},{10,11},{12,13},{... | collective-permute-start | bytes 12296 | tf_op jit(solution)/shard_map/ppermute | solution.py:298
  29.9 5.7 %collective-permute-start.5 = (bf16[512,128]{1,0:T(8,128)(2,1)S(1)}, bf16[512,128]{1,0:T(8,128)(2,1)S(1)}, u32[]{:S(2)}, u32[]{:S(2)}) collective-permute-start(bf16[512,128]{1,0:T(8,128)(2,1)S(1)} %add_convert_fusion.5), channel_id=1, source_target_pairs={{0,8},{8,0},{16,24},{24,16},{1,9},{9,1},{17,25},{25,17},{2,10},{10... | collective-permute-start | bytes 393224 | tf_op jit(solution)/shard_map/ppermute | solution.py:371
  31.9 34.2 %copy-start.6 = (bf16[32,288]{1,0:T(8,128)(2,1)S(1)}, bf16[32,288]{1,0:T(8,128)(2,1)}, u32[]{:S(2)}) copy-start(bf16[32,288]{1,0:T(8,128)(2,1)} %reshape.34) | copy-start | bytes 55300
  32.9 6.9 %collective-permute-start.3 = (bf16[512,128]{1,0:T(8,128)(2,1)S(1)}, bf16[512,128]{1,0:T(8,128)(2,1)S(1)}, u32[]{:S(2)}, u32[]{:S(2)}) collective-permute-start(bf16[512,128]{1,0:T(8,128)(2,1)S(1)} %add_convert_fusion.6), channel_id=1, source_target_pairs={{0,16},{8,24},{16,0},{24,8},{1,17},{9,25},{17,1},{25,9},{2,18},{10... | collective-permute-start | bytes 393224 | tf_op jit(solution)/shard_map/ppermute | solution.py:371
  35.4 5.9 %collective-permute-start.1 = (bf16[512,128]{1,0:T(8,128)(2,1)S(1)}, bf16[512,128]{1,0:T(8,128)(2,1)S(1)}, u32[]{:S(2)}, u32[]{:S(2)}) collective-permute-start(bf16[512,128]{1,0:T(8,128)(2,1)S(1)} %add_convert_fusion.7), channel_id=1, source_target_pairs={{0,24},{8,16},{16,8},{24,0},{1,25},{9,17},{17,9},{25,1},{2,26},{10... | collective-permute-start | bytes 393224 | tf_op jit(solution)/shard_map/ppermute | solution.py:371
  42.4 5.8 %collective-permute-start.7 = (bf16[128,128]{1,0:T(8,128)(2,1)S(1)}, bf16[128,128]{1,0:T(8,128)(2,1)S(1)}, u32[]{:S(2)}, u32[]{:S(2)}) collective-permute-start(bf16[128,128]{1,0:T(8,128)(2,1)S(1)} %get-tuple-element.87), channel_id=1, source_target_pairs={{0,3},{1,2},{2,1},{3,0},{4,7},{5,6},{6,5},{7,4},{8,11},{9,10},{10,... | collective-permute-start | bytes 98312 | tf_op jit(solution)/shard_map/ppermute | solution.py:371
  43.8 4.8 %collective-permute-start.8 = (bf16[128,128]{1,0:T(8,128)(2,1)S(1)}, bf16[128,128]{1,0:T(8,128)(2,1)S(1)}, u32[]{:S(2)}, u32[]{:S(2)}) collective-permute-start(bf16[128,128]{1,0:T(8,128)(2,1)S(1)} %get-tuple-element.86), channel_id=1, source_target_pairs={{0,2},{1,3},{2,0},{3,1},{4,6},{5,7},{6,4},{7,5},{8,10},{9,11},{10,... | collective-permute-start | bytes 98312 | tf_op jit(solution)/shard_map/ppermute | solution.py:371
  45.5 3.9 %collective-permute-start.9 = (bf16[128,128]{1,0:T(8,128)(2,1)S(1)}, bf16[128,128]{1,0:T(8,128)(2,1)S(1)}, u32[]{:S(2)}, u32[]{:S(2)}) collective-permute-start(bf16[128,128]{1,0:T(8,128)(2,1)S(1)} %get-tuple-element.85), channel_id=1, source_target_pairs={{0,1},{1,0},{2,3},{3,2},{4,5},{5,4},{6,7},{7,6},{8,9},{9,8},{10,11... | collective-permute-start | bytes 98312 | tf_op jit(solution)/shard_map/ppermute | solution.py:371
  46.8 16.8 %collective-permute-start.22 = (bf16[34,128]{1,0:T(8,128)(2,1)S(1)}, bf16[34,128]{1,0:T(8,128)(2,1)S(1)}, u32[]{:S(2)}, u32[]{:S(2)}) collective-permute-start(bf16[34,128]{1,0:T(8,128)(2,1)S(1)} %pad_maximum_fusion.2), channel_id=1, source_target_pairs={{0,4},{4,8},{8,12},{12,16},{16,20},{20,24},{24,28},{1,5},{5,9},{9,... | collective-permute-start | bytes 26120 | tf_op jit(solution)/shard_map/ppermute | solution.py:298
  49.4 18.4 %copy-start.5 = (bf16[32,64,128]{2,1,0:T(8,128)(2,1)S(1)}, bf16[32,64,128]{2,1,0:T(8,128)(2,1)}, u32[]{:S(2)}) copy-start(bf16[32,64,128]{2,1,0:T(8,128)(2,1)} %refs_9_.1) | copy-start | bytes 1572868
  50.0 4.4 %collective-permute-start.10 = (bf16[128,128]{1,0:T(8,128)(2,1)S(1)}, bf16[128,128]{1,0:T(8,128)(2,1)S(1)}, u32[]{:S(2)}, u32[]{:S(2)}) collective-permute-start(bf16[128,128]{1,0:T(8,128)(2,1)S(1)} %get-tuple-element.44), channel_id=1, source_target_pairs={{0,1},{1,0},{2,3},{3,2},{4,5},{5,4},{6,7},{7,6},{8,9},{9,8},{10,11... | collective-permute-start | bytes 98312 | tf_op jit(solution)/shard_map/ppermute | solution.py:371
  51.4 5.5 %collective-permute-start.11 = (bf16[128,128]{1,0:T(8,128)(2,1)S(1)}, bf16[128,128]{1,0:T(8,128)(2,1)S(1)}, u32[]{:S(2)}, u32[]{:S(2)}) collective-permute-start(bf16[128,128]{1,0:T(8,128)(2,1)S(1)} %get-tuple-element.44), channel_id=1, source_target_pairs={{0,2},{1,3},{2,0},{3,1},{4,6},{5,7},{6,4},{7,5},{8,10},{9,11},{10,... | collective-permute-start | bytes 98312 | tf_op jit(solution)/shard_map/ppermute | solution.py:371
  53.1 5.7 %collective-permute-start.12 = (bf16[128,128]{1,0:T(8,128)(2,1)S(1)}, bf16[128,128]{1,0:T(8,128)(2,1)S(1)}, u32[]{:S(2)}, u32[]{:S(2)}) collective-permute-start(bf16[128,128]{1,0:T(8,128)(2,1)S(1)} %get-tuple-element.44), channel_id=1, source_target_pairs={{0,3},{1,2},{2,1},{3,0},{4,7},{5,6},{6,5},{7,4},{8,11},{9,10},{10,... | collective-permute-start | bytes 98312 | tf_op jit(solution)/shard_map/ppermute | solution.py:371
  58.8 6.0 %collective-permute-start.13 = (bf16[512,128]{1,0:T(8,128)(2,1)S(1)}, bf16[512,128]{1,0:T(8,128)(2,1)S(1)}, u32[]{:S(2)}, u32[]{:S(2)}) collective-permute-start(bf16[512,128]{1,0:T(8,128)(2,1)S(1)} %constant_dynamic-update-slice_fusion.refs_0_), channel_id=1, source_target_pairs={{0,8},{8,0},{16,24},{24,16},{1,9},{9,1},{17,25},{25,17},{2,10},{10... | collective-permute-start | bytes 393224 | tf_op jit(solution)/shard_map/ppermute | solution.py:371
  59.3 5.6 %collective-permute-start.14 = (bf16[512,128]{1,0:T(8,128)(2,1)S(1)}, bf16[512,128]{1,0:T(8,128)(2,1)S(1)}, u32[]{:S(2)}, u32[]{:S(2)}) collective-permute-start(bf16[512,128]{1,0:T(8,128)(2,1)S(1)} %constant_dynamic-update-slice_fusion.refs_0_), channel_id=1, source_target_pairs={{0,16},{8,24},{16,0},{24,8},{1,17},{9,25},{17,1},{25,9},{2,18},{10... | collective-permute-start | bytes 393224 | tf_op jit(solution)/shard_map/ppermute | solution.py:371
  60.2 5.9 %collective-permute-start.15 = (bf16[512,128]{1,0:T(8,128)(2,1)S(1)}, bf16[512,128]{1,0:T(8,128)(2,1)S(1)}, u32[]{:S(2)}, u32[]{:S(2)}) collective-permute-start(bf16[512,128]{1,0:T(8,128)(2,1)S(1)} %constant_dynamic-update-slice_fusion.refs_0_), channel_id=1, source_target_pairs={{0,24},{8,16},{16,8},{24,0},{1,25},{9,17},{17,9},{25,1},{2,26},{10... | collective-permute-start | bytes 393224 | tf_op jit(solution)/shard_map/ppermute | solution.py:371
  62.3 3.9 %collective-permute-start.23 = (bf16[34,128]{1,0:T(8,128)(2,1)S(1)}, bf16[34,128]{1,0:T(8,128)(2,1)S(1)}, u32[]{:S(2)}, u32[]{:S(2)}) collective-permute-start(bf16[34,128]{1,0:T(8,128)(2,1)S(1)} %pad_maximum_fusion.3), channel_id=1, source_target_pairs={{4,0},{8,4},{12,8},{16,12},{20,16},{24,20},{28,24},{5,1},{9,5},{13... | collective-permute-start | bytes 26120 | tf_op jit(solution)/shard_map/ppermute | solution.py:298
  63.6 4.1 %collective-permute-start.16 = (bf16[512,128]{1,0:T(8,128)(2,1)S(1)}, bf16[512,128]{1,0:T(8,128)(2,1)S(1)}, u32[]{:S(2)}, u32[]{:S(2)}) collective-permute-start(bf16[512,128]{1,0:T(8,128)(2,1)S(1)} %constant_dynamic-update-slice_fusion.refs_0_), channel_id=1, source_target_pairs={{0,4},{4,0},{1,5},{5,1},{2,6},{6,2},{3,7},{7,3},{8,12},{12,8},{9,1... | collective-permute-start | bytes 393224 | tf_op jit(solution)/shard_map/ppermute | solution.py:371
  64.8 2.9 %collective-permute-start.17 = (bf16[512,128]{1,0:T(8,128)(2,1)S(1)}, bf16[512,128]{1,0:T(8,128)(2,1)S(1)}, u32[]{:S(2)}, u32[]{:S(2)}) collective-permute-start(bf16[512,128]{1,0:T(8,128)(2,1)S(1)} %collective-permute-done.13.refs_1_), channel_id=1, source_target_pairs={{0,4},{4,0},{1,5},{5,1},{2,6},{6,2},{3,7},{7,3},{8,12},{12,8},{9,1... | collective-permute-start | bytes 393224 | tf_op jit(solution)/shard_map/ppermute | solution.py:371
  64.9 2.8 %collective-permute-start.18 = (bf16[512,128]{1,0:T(8,128)(2,1)S(1)}, bf16[512,128]{1,0:T(8,128)(2,1)S(1)}, u32[]{:S(2)}, u32[]{:S(2)}) collective-permute-start(bf16[512,128]{1,0:T(8,128)(2,1)S(1)} %collective-permute-done.14.refs_2_), channel_id=1, source_target_pairs={{0,4},{4,0},{1,5},{5,1},{2,6},{6,2},{3,7},{7,3},{8,12},{12,8},{9,1... | collective-permute-start | bytes 393224 | tf_op jit(solution)/shard_map/ppermute | solution.py:371
  66.1 1.7 %collective-permute-start.19 = (bf16[512,128]{1,0:T(8,128)(2,1)S(1)}, bf16[512,128]{1,0:T(8,128)(2,1)S(1)}, u32[]{:S(2)}, u32[]{:S(2)}) collective-permute-start(bf16[512,128]{1,0:T(8,128)(2,1)S(1)} %collective-permute-done.15.refs_3_), channel_id=1, source_target_pairs={{0,4},{4,0},{1,5},{5,1},{2,6},{6,2},{3,7},{7,3},{8,12},{12,8},{9,1... | collective-permute-start | bytes 393224 | tf_op jit(solution)/shard_map/ppermute | solution.py:371
  71.1 17.3 %collective-permute-start.30 = (bf16[512,128]{1,0:T(8,128)(2,1)S(1)}, bf16[512,128]{1,0:T(8,128)(2,1)S(1)}, u32[]{:S(2)}, u32[]{:S(2)}) collective-permute-start(bf16[512,128]{1,0:T(8,128)(2,1)S(1)} %get-tuple-element.56), channel_id=1, source_target_pairs={{0,4},{4,0},{1,5},{5,1},{2,6},{6,2},{3,7},{7,3},{8,12},{12,8},{9,1... | collective-permute-start | bytes 393224 | tf_op jit(solution)/shard_map/ppermute | solution.py:371
  71.6 13.0 %collective-permute-start.28 = (bf16[512,128]{1,0:T(8,128)(2,1)S(1)}, bf16[512,128]{1,0:T(8,128)(2,1)S(1)}, u32[]{:S(2)}, u32[]{:S(2)}) collective-permute-start(bf16[512,128]{1,0:T(8,128)(2,1)S(1)} %get-tuple-element.54), channel_id=1, source_target_pairs={{0,4},{4,0},{1,5},{5,1},{2,6},{6,2},{3,7},{7,3},{8,12},{12,8},{9,1... | collective-permute-start | bytes 393224 | tf_op jit(solution)/shard_map/ppermute | solution.py:371
  71.6 14.1 %collective-permute-start.26 = (bf16[512,128]{1,0:T(8,128)(2,1)S(1)}, bf16[512,128]{1,0:T(8,128)(2,1)S(1)}, u32[]{:S(2)}, u32[]{:S(2)}) collective-permute-start(bf16[512,128]{1,0:T(8,128)(2,1)S(1)} %get-tuple-element.52), channel_id=1, source_target_pairs={{0,4},{4,0},{1,5},{5,1},{2,6},{6,2},{3,7},{7,3},{8,12},{12,8},{9,1... | collective-permute-start | bytes 393224 | tf_op jit(solution)/shard_map/ppermute | solution.py:371
  72.1 14.6 %collective-permute-start.24 = (bf16[512,128]{1,0:T(8,128)(2,1)S(1)}, bf16[512,128]{1,0:T(8,128)(2,1)S(1)}, u32[]{:S(2)}, u32[]{:S(2)}) collective-permute-start(bf16[512,128]{1,0:T(8,128)(2,1)S(1)} %get-tuple-element.50), channel_id=1, source_target_pairs={{0,4},{4,0},{1,5},{5,1},{2,6},{6,2},{3,7},{7,3},{8,12},{12,8},{9,1... | collective-permute-start | bytes 393224 | tf_op jit(solution)/shard_map/ppermute | solution.py:371
  73.0 5.5 %collective-permute-start.45 = (bf16[1,2048]{1,0:T(2,128)(2,1)S(1)}, bf16[1,2048]{1,0:T(2,128)(2,1)S(1)}, u32[]{:S(2)}, u32[]{:S(2)}) collective-permute-start(bf16[1,2048]{1,0:T(2,128)(2,1)S(1)} %get-tuple-element.88), channel_id=1, source_target_pairs={{1,0},{2,1},{3,2},{5,4},{6,5},{7,6},{9,8},{10,9},{11,10},{13,12},{... | collective-permute-start | bytes 12296 | tf_op jit(solution)/shard_map/ppermute | solution.py:298
  78.6 4.6 %collective-permute-start.44 = (bf16[1,2048]{1,0:T(2,128)(2,1)S(1)}, bf16[1,2048]{1,0:T(2,128)(2,1)S(1)}, u32[]{:S(2)}, u32[]{:S(2)}) collective-permute-start(bf16[1,2048]{1,0:T(2,128)(2,1)S(1)} %get-tuple-element.89), channel_id=1, source_target_pairs={{0,1},{1,2},{2,3},{4,5},{5,6},{6,7},{8,9},{9,10},{10,11},{12,13},{... | collective-permute-start | bytes 12296 | tf_op jit(solution)/shard_map/ppermute | solution.py:298
  83.3 16.0 %collective-permute-start.46 = (bf16[34,128]{1,0:T(8,128)(2,1)S(1)}, bf16[34,128]{1,0:T(8,128)(2,1)S(1)}, u32[]{:S(2)}, u32[]{:S(2)}) collective-permute-start(bf16[34,128]{1,0:T(8,128)(2,1)S(1)} %pad_maximum_fusion.4), channel_id=1, source_target_pairs={{0,4},{4,8},{8,12},{12,16},{16,20},{20,24},{24,28},{1,5},{5,9},{9,... | collective-permute-start | bytes 26120 | tf_op jit(solution)/shard_map/ppermute | solution.py:298
  84.6 6.3 %collective-permute-start.29 = (bf16[512,128]{1,0:T(8,128)(2,1)S(1)}, bf16[512,128]{1,0:T(8,128)(2,1)S(1)}, u32[]{:S(2)}, u32[]{:S(2)}) collective-permute-start(bf16[512,128]{1,0:T(8,128)(2,1)S(1)} %add_convert_fusion.1), channel_id=1, source_target_pairs={{0,8},{8,0},{16,24},{24,16},{1,9},{9,1},{17,25},{25,17},{2,10},{10... | collective-permute-start | bytes 393224 | tf_op jit(solution)/shard_map/ppermute | solution.py:371
  85.7 9.0 %collective-permute-start.27 = (bf16[512,128]{1,0:T(8,128)(2,1)S(1)}, bf16[512,128]{1,0:T(8,128)(2,1)S(1)}, u32[]{:S(2)}, u32[]{:S(2)}) collective-permute-start(bf16[512,128]{1,0:T(8,128)(2,1)S(1)} %add_convert_fusion.2), channel_id=1, source_target_pairs={{0,16},{8,24},{16,0},{24,8},{1,17},{9,25},{17,1},{25,9},{2,18},{10... | collective-permute-start | bytes 393224 | tf_op jit(solution)/shard_map/ppermute | solution.py:371
  86.7 8.0 %collective-permute-start.25 = (bf16[512,128]{1,0:T(8,128)(2,1)S(1)}, bf16[512,128]{1,0:T(8,128)(2,1)S(1)}, u32[]{:S(2)}, u32[]{:S(2)}) collective-permute-start(bf16[512,128]{1,0:T(8,128)(2,1)S(1)} %add_convert_fusion.3), channel_id=1, source_target_pairs={{0,24},{8,16},{16,8},{24,0},{1,25},{9,17},{17,9},{25,1},{2,26},{10... | collective-permute-start | bytes 393224 | tf_op jit(solution)/shard_map/ppermute | solution.py:371
  88.4 10.9 %collective-permute-start.47 = (bf16[34,128]{1,0:T(8,128)(2,1)S(1)}, bf16[34,128]{1,0:T(8,128)(2,1)S(1)}, u32[]{:S(2)}, u32[]{:S(2)}) collective-permute-start(bf16[34,128]{1,0:T(8,128)(2,1)S(1)} %pad_maximum_fusion.5), channel_id=1, source_target_pairs={{4,0},{8,4},{12,8},{16,12},{20,16},{24,20},{28,24},{5,1},{9,5},{13... | collective-permute-start | bytes 26120 | tf_op jit(solution)/shard_map/ppermute | solution.py:298
  94.9 6.2 %collective-permute-start.31 = (bf16[128,128]{1,0:T(8,128)(2,1)S(1)}, bf16[128,128]{1,0:T(8,128)(2,1)S(1)}, u32[]{:S(2)}, u32[]{:S(2)}) collective-permute-start(bf16[128,128]{1,0:T(8,128)(2,1)S(1)} %get-tuple-element.83), channel_id=1, source_target_pairs={{0,3},{1,2},{2,1},{3,0},{4,7},{5,6},{6,5},{7,4},{8,11},{9,10},{10,... | collective-permute-start | bytes 98312 | tf_op jit(solution)/shard_map/ppermute | solution.py:371
  97.1 4.9 %collective-permute-start.32 = (bf16[128,128]{1,0:T(8,128)(2,1)S(1)}, bf16[128,128]{1,0:T(8,128)(2,1)S(1)}, u32[]{:S(2)}, u32[]{:S(2)}) collective-permute-start(bf16[128,128]{1,0:T(8,128)(2,1)S(1)} %get-tuple-element.82), channel_id=1, source_target_pairs={{0,2},{1,3},{2,0},{3,1},{4,6},{5,7},{6,4},{7,5},{8,10},{9,11},{10,... | collective-permute-start | bytes 98312 | tf_op jit(solution)/shard_map/ppermute | solution.py:371
  98.7 3.9 %collective-permute-start.33 = (bf16[128,128]{1,0:T(8,128)(2,1)S(1)}, bf16[128,128]{1,0:T(8,128)(2,1)S(1)}, u32[]{:S(2)}, u32[]{:S(2)}) collective-permute-start(bf16[128,128]{1,0:T(8,128)(2,1)S(1)} %get-tuple-element.81), channel_id=1, source_target_pairs={{0,1},{1,0},{2,3},{3,2},{4,5},{5,4},{6,7},{7,6},{8,9},{9,8},{10,11... | collective-permute-start | bytes 98312 | tf_op jit(solution)/shard_map/ppermute | solution.py:371
  103.3 4.5 %collective-permute-start.34 = (bf16[200,128]{1,0:T(8,128)(2,1)S(1)}, bf16[200,128]{1,0:T(8,128)(2,1)S(1)}, u32[]{:S(2)}, u32[]{:S(2)}) collective-permute-start(bf16[200,128]{1,0:T(8,128)(2,1)S(1)} %pad_maximum_fusion.1), channel_id=1, source_target_pairs={{0,1},{1,0},{2,3},{3,2},{4,5},{5,4},{6,7},{7,6},{8,9},{9,8},{10,11... | collective-permute-start | bytes 153608 | tf_op jit(solution)/shard_map/ppermute | solution.py:371
  104.0 6.1 %collective-permute-start.35 = (bf16[200,128]{1,0:T(8,128)(2,1)S(1)}, bf16[200,128]{1,0:T(8,128)(2,1)S(1)}, u32[]{:S(2)}, u32[]{:S(2)}) collective-permute-start(bf16[200,128]{1,0:T(8,128)(2,1)S(1)} %pad_maximum_fusion.1), channel_id=1, source_target_pairs={{0,2},{1,3},{2,0},{3,1},{4,6},{5,7},{6,4},{7,5},{8,10},{9,11},{10,... | collective-permute-start | bytes 153608 | tf_op jit(solution)/shard_map/ppermute | solution.py:371
  105.9 5.9 %collective-permute-start.36 = (bf16[200,128]{1,0:T(8,128)(2,1)S(1)}, bf16[200,128]{1,0:T(8,128)(2,1)S(1)}, u32[]{:S(2)}, u32[]{:S(2)}) collective-permute-start(bf16[200,128]{1,0:T(8,128)(2,1)S(1)} %pad_maximum_fusion.1), channel_id=1, source_target_pairs={{0,3},{1,2},{2,1},{3,0},{4,7},{5,6},{6,5},{7,4},{8,11},{9,10},{10,... | collective-permute-start | bytes 153608 | tf_op jit(solution)/shard_map/ppermute | solution.py:371
  111.8 5.2 %collective-permute-start.37 = (bf16[584,128]{1,0:T(8,128)(2,1)S(1)}, bf16[584,128]{1,0:T(8,128)(2,1)S(1)}, u32[]{:S(2)}, u32[]{:S(2)}) collective-permute-start(bf16[584,128]{1,0:T(8,128)(2,1)S(1)} %get-tuple-element.72), channel_id=1, source_target_pairs={{0,8},{8,0},{16,24},{24,16},{1,9},{9,1},{17,25},{25,17},{2,10},{10... | collective-permute-start | bytes 448520 | tf_op jit(solution)/shard_map/ppermute | solution.py:371
  112.7 5.2 %collective-permute-start.38 = (bf16[584,128]{1,0:T(8,128)(2,1)S(1)}, bf16[584,128]{1,0:T(8,128)(2,1)S(1)}, u32[]{:S(2)}, u32[]{:S(2)}) collective-permute-start(bf16[584,128]{1,0:T(8,128)(2,1)S(1)} %get-tuple-element.72), channel_id=1, source_target_pairs={{0,16},{8,24},{16,0},{24,8},{1,17},{9,25},{17,1},{25,9},{2,18},{10... | collective-permute-start | bytes 448520 | tf_op jit(solution)/shard_map/ppermute | solution.py:371
  113.4 6.1 %collective-permute-start.39 = (bf16[584,128]{1,0:T(8,128)(2,1)S(1)}, bf16[584,128]{1,0:T(8,128)(2,1)S(1)}, u32[]{:S(2)}, u32[]{:S(2)}) collective-permute-start(bf16[584,128]{1,0:T(8,128)(2,1)S(1)} %get-tuple-element.72), channel_id=1, source_target_pairs={{0,24},{8,16},{16,8},{24,0},{1,25},{9,17},{17,9},{25,1},{2,26},{10... | collective-permute-start | bytes 448520 | tf_op jit(solution)/shard_map/ppermute | solution.py:371
  119.5 1.4 %collective-permute-start.48 = (bf16[72,128]{1,0:T(8,128)(2,1)S(1)}, bf16[72,128]{1,0:T(8,128)(2,1)S(1)}, u32[]{:S(2)}, u32[]{:S(2)}) collective-permute-start(bf16[72,128]{1,0:T(8,128)(2,1)S(1)} %add_convert_fusion.8), channel_id=1, source_target_pairs={{0,4},{4,0},{1,5},{5,1},{2,6},{6,2},{3,7},{7,3},{8,12},{12,8},{9,1... | collective-permute-start | bytes 55304 | tf_op jit(solution)/shard_map/ppermute | solution.py:371
  119.6 2.2 %collective-permute-start.40 = (bf16[512,128]{1,0:T(8,128)(2,1)S(1)}, bf16[512,128]{1,0:T(8,128)(2,1)S(1)}, u32[]{:S(2)}, u32[]{:S(2)}) collective-permute-start(bf16[512,128]{1,0:T(8,128)(2,1)S(1)} %pad_maximum_fusion.refs_0_), channel_id=1, source_target_pairs={{0,4},{4,0},{1,5},{5,1},{2,6},{6,2},{3,7},{7,3},{8,12},{12,8},{9,1... | collective-permute-start | bytes 393224 | tf_op jit(solution)/shard_map/ppermute | solution.py:371
  120.2 1.6 %collective-permute-start.41 = (bf16[512,128]{1,0:T(8,128)(2,1)S(1)}, bf16[512,128]{1,0:T(8,128)(2,1)S(1)}, u32[]{:S(2)}, u32[]{:S(2)}) collective-permute-start(bf16[512,128]{1,0:T(8,128)(2,1)S(1)} %slice.170.refs_1_), channel_id=1, source_target_pairs={{0,4},{4,0},{1,5},{5,1},{2,6},{6,2},{3,7},{7,3},{8,12},{12,8},{9,1... | collective-permute-start | bytes 393224 | tf_op jit(solution)/shard_map/ppermute | solution.py:371
  120.3 1.6 %collective-permute-start.42 = (bf16[512,128]{1,0:T(8,128)(2,1)S(1)}, bf16[512,128]{1,0:T(8,128)(2,1)S(1)}, u32[]{:S(2)}, u32[]{:S(2)}) collective-permute-start(bf16[512,128]{1,0:T(8,128)(2,1)S(1)} %slice.171.refs_2_), channel_id=1, source_target_pairs={{0,4},{4,0},{1,5},{5,1},{2,6},{6,2},{3,7},{7,3},{8,12},{12,8},{9,1... | collective-permute-start | bytes 393224 | tf_op jit(solution)/shard_map/ppermute | solution.py:371
  120.8 1.4 %collective-permute-start.43 = (bf16[512,128]{1,0:T(8,128)(2,1)S(1)}, bf16[512,128]{1,0:T(8,128)(2,1)S(1)}, u32[]{:S(2)}, u32[]{:S(2)}) collective-permute-start(bf16[512,128]{1,0:T(8,128)(2,1)S(1)} %slice.172.refs_3_), channel_id=1, source_target_pairs={{0,4},{4,0},{1,5},{5,1},{2,6},{6,2},{3,7},{7,3},{8,12},{12,8},{9,1... | collective-permute-start | bytes 393224 | tf_op jit(solution)/shard_map/ppermute | solution.py:371

commit v3 on v2

--- a/solution.py
+++ b/solution.py
@@ -216,7 +216,7 @@
             out_ref[at + k] = (cells[k] + conv_ref[at + k]).astype(bf16)
 
 
-def turn_kernel(cells_ref, turned_ref, edges_ref, turned_s):
+def turn_kernel(cells_ref, turned_ref, edges_ref, turned_s, edges_s):
     channels, height, width = cells_ref.shape
     for c in range(channels):
         turned_s[pl.ds(c, height, stride=channels), :] = cells_ref[c].astype(f32)
@@ -225,7 +225,14 @@
     row = lax.broadcasted_iota(jnp.int32, (16, width), 0)
     col = lax.broadcasted_iota(jnp.int32, (16, width), 1)
     chosen = ((row == 0) & (col == 0)) | ((row == 1) & (col == width - 1))
-    edges_ref[...] = dot_nt(chosen.astype(f32).astype(bf16), turned).astype(bf16)
+    edges = dot_nt(chosen.astype(f32).astype(bf16), turned)
+    half = edges_s.shape[0] // 2
+    for k in range(half):
+        for side in range(2):
+            edges_s[side * half + k : side * half + k + 1, :] = edges[
+                side : side + 1, k * 128 : (k + 1) * 128
+            ]
+    edges_ref[...] = edges_s[...].astype(bf16)
 
 
 def turn(cells):
@@ -233,8 +240,8 @@
     lines = (height * channels, width)
     return call(
         turn_kernel,
-        (shape(lines, bf16), shape((16, lines[0]), bf16)),
-        [pltpu.VMEM(lines, f32)],
+        (shape(lines, bf16), shape((lines[0] // 64, 128), bf16)),
+        [pltpu.VMEM(lines, f32), pltpu.VMEM((lines[0] // 64, 128), f32)],
         2 * cells.size * 16, cells.size * 4,
         cells,
     )
@@ -276,8 +283,11 @@
     height = lines // channels
     widen(height + 1, low_ref[:channels], low_ref[channels : channels + 2, :channels])
     step = BLOCK * channels
+    left, right = left_ref[...].astype(f32), right_ref[...].astype(f32)
     for b in range(0, lines, step):
-        sides = jnp.concatenate([left_ref[:, b : b + step], right_ref[:, b : b + step]], axis=0)
+        rows = range(b // 128, (b + step) // 128)
+        sides = [jnp.concatenate([v[k : k + 1] for k in rows], axis=1) for v in (left, right)]
+        sides = jnp.concatenate(sides, axis=0).astype(bf16)
         widen(b // channels + 1, turned_ref[b : b + step], sides)
     matrix = band_ref[...]
     for b in range(0, height // BLOCK, 2):
@@ -298,14 +308,20 @@
     return lax.ppermute(value, axis, pairs)
 
 
-def stencil(turned, edges, matrix, channels):
+def stencil(turned, edges, sides, matrix, channels):
     lines, width = turned.shape
     height = lines // channels
-    left = shifted(edges[1:2], "cols", True)
-    right = shifted(edges[0:1], "cols", False)
+    if sides is None:
+        half = edges.shape[0] // 2
+        left = shifted(edges[half:], "cols", True)
+        right = shifted(edges[:half], "cols", False)
+    else:
+        left, right = sides
 
     def with_sides(cells, at):
-        sides = jnp.concatenate([left[:, at : at + channels], right[:, at : at + channels]], axis=0)
+        row, lane = at // 128, at % 128
+        sides = [v[row : row + 1, lane : lane + channels] for v in (left, right)]
+        sides = jnp.concatenate(sides, axis=0)
         return jnp.concatenate([cells, jnp.pad(sides, ((0, 0), (0, width - channels)))], axis=0)
 
     top = shifted(with_sides(turned[lines - channels :], lines - channels), ROWS, True)
@@ -392,25 +408,30 @@
     return parts
 
 
-def spread_block(plan, block, extra=None):
-    def widen(value, axis, count):
-        rows = value.shape[0]
-        whole = value if extra is None else jnp.concatenate([value, summed.astype(bf16)], axis=0)
+def spread_block(plan, block, edges, extra=None):
+    def widen(parts, axis, count):
+        whole = parts[0] if len(parts) == 1 else jnp.concatenate(parts, axis=0)
         got = {q: swapped(whole, axis, q) for q in reversed(range(1, count))}
         got[0] = whole
-        found = [got[q] for q in range(count)]
-        total = None if extra is None else tree_sum([v[rows:] for v in found])
-        return [v[:rows] for v in found], total
-
-    summed = extra
-    found, summed = widen(block, "cols", plan.cols)
-    here = jnp.concatenate(found, axis=0)
-    pieces, summed = widen(here, "chips", plan.chips)
+        found, at = [], 0
+        for part in parts:
+            found.append([got[q][at : at + part.shape[0]] for q in range(count)])
+            at += part.shape[0]
+        return found
+
+    more = [] if extra is None else [extra]
+    blocks, around, *more = widen([block, edges] + more, "cols", plan.cols)
+    more = [tree_sum(v).astype(bf16) for v in more]
+    col, half = lax.axis_index("cols"), edges.shape[0] // 2
+    left = right = jnp.zeros((half, edges.shape[1]), bf16)
+    for q in range(1, plan.cols):
+        left = jnp.where((col ^ q) == col - 1, around[q][half:], left)
+        right = jnp.where((col ^ q) == col + 1, around[q][:half], right)
+    pieces, *more = widen([jnp.concatenate(blocks, axis=0)] + more, "chips", plan.chips)
+    more = [tree_sum(v).astype(bf16) for v in more]
+    more = [tree_sum([v, swapped(v, "core", 1)]) for v in more]
     pieces = pieces + [swapped(v, "core", 1) for v in pieces]
-    if extra is not None:
-        half = summed.astype(bf16)
-        summed = tree_sum([half, swapped(half, "core", 1)])
-    return pieces, summed
+    return pieces, (left, right), more[0] if more else None
 
 
 def to_lines(parts, total_s, re_s, im_s):
@@ -495,14 +516,14 @@
     return jnp.einsum(form, left, right, precision=lax.Precision.HIGHEST, preferred_element_type=f32)
 
 
-def at_owner(plan, partial, weight_real, weight_imag, forward, extra=None):
+def at_owner(plan, partial, weight_real, weight_imag, forward, edges, extra=None):
     channels, _, modes = weight_real.shape
     if plan.staged:
         parts = reduce_pieces(plan, partial)
         kernel = mix_kernel if forward else unmix_kernel
         sent, real, imag = owner_stage(kernel, parts, weight_real, weight_imag, 0 if forward else 2)
-        pieces, summed = spread_block(plan, sent, extra)
-        return pieces, real, imag, summed
+        pieces, sides, summed = spread_block(plan, sent, edges, extra)
+        return pieces, real, imag, sides, summed
     swap = lambda x: lax.all_to_all(x, BOTH, 0, 0, tiled=True)
     pieces = M // modes
     held = (plan.blocks, channels // 2, 4, 2, 2, pieces, modes)
@@ -522,7 +543,7 @@
     held = (plan.blocks, 4, pieces, channels // 2, 2, 2, modes)
     spread = sent.reshape(held).transpose(0, 3, 1, 5, 4, 2, 6)
     summed = None if extra is None else lax.psum(extra.astype(f32), BOTH)
-    return [spread.reshape(2 * M * channels, 2 * M)], real, imag, summed
+    return [spread.reshape(2 * M * channels, 2 * M)], real, imag, None, summed
 
 
 def layer(field, cotangent, weight_real, weight_imag, kernel):
@@ -549,15 +570,17 @@
             pltpu.SemaphoreType.DMA((2 + channels // QUAD,)),
         ],
         transform, cells * 2 + modes * 2,
-        field, all_cols, all_rows,
+        *(pltpu.with_memory_space_constraint(v, pltpu.HBM) for v in (field, all_cols, all_rows)),
         far=3,
     )
-    spectrum, coef_real, coef_imag, _ = at_owner(plan, partial, weight_real, weight_imag, True)
     rows = lax.dynamic_index_in_dim(all_rows, lax.axis_index(ROWS), 0, keepdims=False)
     cols = lax.dynamic_index_in_dim(all_cols, lax.axis_index("cols"), 0, keepdims=False)
     turned, edges = turn(field)
+    spectrum, coef_real, coef_imag, sides, _ = at_owner(
+        plan, partial, weight_real, weight_imag, True, edges
+    )
     matrix = band(kernel)
-    conv, wide_field = stencil(turned, edges, matrix, channels)
+    conv, wide_field = stencil(turned, edges, sides, matrix, channels)
 
     activated, grad, *partial_grad = call(
         functools.partial(middle_kernel, plan, len(spectrum)),
@@ -568,11 +591,11 @@
     )
     grad_turned, grad_edges = turn(grad)
     local = kernel_grad_here(wide_field, grad_turned, channels)
-    spectrum_grad, mode_real, mode_imag, summed = at_owner(
-        plan, partial_grad, weight_real, weight_imag, False, local
+    spectrum_grad, mode_real, mode_imag, sides, summed = at_owner(
+        plan, partial_grad, weight_real, weight_imag, False, grad_edges, local
     )
     matrix = band(jnp.transpose(kernel[::-1, ::-1], (0, 1, 3, 2)))
-    conv_grad, _ = stencil(grad_turned, grad_edges, matrix, channels)
+    conv_grad, _ = stencil(grad_turned, grad_edges, sides, matrix, channels)
     summed = summed.reshape(summed.shape[0], 128 // channels, channels).transpose(1, 0, 2)
     kernel_grad = summed.reshape(3, 3, channels, channels) * scale_cells
 

time: 125 us -> 104 us (0.83)
  local copies, waits for them, and re-layouts: 18.1 us -> 6.29 us
  waiting for transfers between devices: 30 us -> 24.6 us
  starting transfers between devices: 54.1 us -> 51.5 us
    ppermute x8 -> x4, starting transfers between devices: 16.7 us -> 7.55 us  [shifted(): return lax.ppermute(value, axis, pairs)]
    unnamed x40 -> x34, local copies, waits for them, and re-layouts: 10.3 us -> 3.51 us
    ppermute x41, starting transfers between devices: 37.4 us -> 44 us  [swapped(): return lax.ppermute(value, axis, [(i, i ^ step) for i in range(count)])]
    ppermute x8 -> x4, waiting for transfers between devices: 4.66 us -> 1.32 us  [shifted(): return lax.ppermute(value, axis, pairs)]
    another operation x2, local copies, waits for them, and re-layouts: 2.3 us -> 0.06 us  [band(): flat = jnp.transpose(weights, (3, 0, 1, 2)).reshape(outs, -1)]
    ppermute x41, waiting for transfers between devices: 25.3 us -> 23.2 us  [swapped(): return lax.ppermute(value, axis, [(i, i ^ step) for i in range(count)])]
    reshape x2, local copies, waits for them, and re-layouts: 1.7 us -> 0.2 us  [band(): flat = jnp.transpose(weights, (3, 0, 1, 2)).reshape(outs, -1)]
  transfers between devices with their start and end apart: 49 -> 45, of which waited for: 18 -> 16; matrix products, arithmetic and copies ran while one was open for 16% -> 8% of each run, Pallas kernels for 5% -> 6%
where the time goes in v3:
time: 104 us; the launch traced here: 103 us
  starting transfers between devices  51.5 us (50%)
  waiting for transfers between devices  24.6 us (24%)
  Pallas kernels  15 us (14%)
  local copies, waits for them, and re-layouts  6.29 us (6%)
  other arithmetic  5.01 us (5%)
  between operations  1.1 us (1%)
    ppermute x41, starting transfers between devices, swapped(): return lax.ppermute(value, axis, [(i, i ^ step) for i in range(count)])  44 us
    ppermute x41, waiting for transfers between devices, swapped(): return lax.ppermute(value, axis, [(i, i ^ step) for i in range(count)])  23.2 us
    pallas_call x10, Pallas kernels, call(): pl.pallas_call(kernel, out_shape=out_shape, in_specs=[pl.BlockSpec(memory...  15 us
    ppermute x4, starting transfers between devices, shifted(): return lax.ppermute(value, axis, pairs)  7.55 us
    unnamed x34, local copies, waits for them, and re-layouts  3.51 us
  transfers between devices with their start and end apart: 45, of which 16 were waited for; matrix products, arithmetic and copies ran while one was open for 8% of the time, Pallas kernels for 6%

profile of v3, /device:TPU:0, one launch (start us, length us, event | category | flops | bytes accessed | tf_op | source)
XLA Modules:
  0.0 103.5 jit_solution(9647649640033994632)
XLA Ops:
  0.7 2.9 %shard_map.110 = (bf16[512,128]{1,0:T(8,128)(2,1)S(1)}, bf16[512,128]{1,0:T(8,128)(2,1)S(1)}, bf16[512,128]{1,0:T(8,128)(2,1)S(1)}, bf16[512,128]{1,0:T(8,128)(2...) custom-call(bf16[32,64,128]{2,1,0:T(8,128)(2,1)} %cells_ref.1, ...), custom_call_target="tpu_custom_call" | custom-call | flops 268435456 | bytes 1572864 | tf_op jit(solution)/shard_map/pallas_call | solution.py:39
  3.5 0.6 collective-permute-start.6
  4.2 0.4 collective-permute-start.2
  4.7 0.8 shard_map.112
  5.6 0.8 copy-done.4
  7.3 1.0 dynamic-slice_bitcast_fusion.1.refs_10_.refs_9_
  8.3 0.9 add_convert_fusion.5
  9.2 3.0 %collective-permute-start.5 = (bf16[512,128]{1,0:T(8,128)(2,1)S(1)}, bf16[512,128]{1,0:T(8,128)(2,1)S(1)}, u32[]{:S(2)}, u32[]{:S(2)}) collective-permute-start(bf16[512,128]{1,0:T(8,128)(2,1)S(1)} %add_convert_fusion.5), channel_id=1, source_target_pairs={{0,8},{8,0},{16,24},{24,16},{1,9},{9,1},{17,25},{25,17},{2,10},{10... | collective-permute-start | bytes 393224 | tf_op jit(solution)/shard_map/ppermute | solution.py:387
  12.2 0.9 add_convert_fusion.6
  13.1 1.6 %collective-permute-start.3 = (bf16[512,128]{1,0:T(8,128)(2,1)S(1)}, bf16[512,128]{1,0:T(8,128)(2,1)}, u32[]{:S(2)}, u32[]{:S(2)}) collective-permute-start(bf16[512,128]{1,0:T(8,128)(2,1)S(1)} %add_convert_fusion.6), channel_id=1, source_target_pairs={{0,16},{8,24},{16,0},{24,8},{1,17},{9,25},{17,1},{25,9},{2,18},{10... | collective-permute-start | bytes 393224 | tf_op jit(solution)/shard_map/ppermute | solution.py:387
  14.9 1.0 dynamic-slice_bitcast_fusion.refs_11_.refs_10_
  15.9 5.4 %collective-permute-done.3 = bf16[512,128]{1,0:T(8,128)(2,1)} collective-permute-done((bf16[512,128]{1,0:T(8,128)(2,1)S(1)}, bf16[512,128]{1,0:T(8,128)(2,1)}, u32[]{:S(2)}, u32[]{:S(2)}) %collective-permute-start.3) | collective-permute-done | bytes 131104 | tf_op jit(solution)/shard_map/ppermute | solution.py:387
  21.3 1.1 %add_convert_fusion.4 = bf16[512,128]{1,0:T(8,128)(2,1)S(1)} fusion(bf16[512,128]{1,0:T(8,128)(2,1)} %collective-permute-done.6, bf16[512,128]{1,0:T(8,128)(2,1)S(1)} %get-tuple-element.42, bf16[512,128]{1,0:T(8,128)(2,1)S(1)} %collective-permute-done.5, bf16[512,128]{1,0:T(8,128)(2,1)} %collective-permute-done.3, bf16[512,128]{1,0:T(8,128)(2,1)S(1)} %collective-permute-done.1), kind=kLoop, calls=%fused_computation.7 | loop fusion | flops 655360 | bytes 786432 | tf_op jit(solution)/shard_map/convert.7
  22.4 3.7 %collective-permute-start.7 = (bf16[128,128]{1,0:T(8,128)(2,1)S(1)}, bf16[128,128]{1,0:T(8,128)(2,1)S(1)}, u32[]{:S(2)}, u32[]{:S(2)}) collective-permute-start(bf16[128,128]{1,0:T(8,128)(2,1)S(1)} %get-tuple-element.89), channel_id=1, source_target_pairs={{0,3},{1,2},{2,1},{3,0},{4,7},{5,6},{6,5},{7,4},{8,11},{9,10},{10,... | collective-permute-start | bytes 98312 | tf_op jit(solution)/shard_map/ppermute | solution.py:387
  26.1 0.8 collective-permute-start.9
  26.9 1.2 %collective-permute-done.7.refs_0_ = bf16[128,128]{1,0:T(8,128)(2,1)S(1)} collective-permute-done((bf16[128,128]{1,0:T(8,128)(2,1)S(1)}, bf16[128,128]{1,0:T(8,128)(2,1)S(1)}, u32[]{:S(2)}, u32[]{:S(2)}) %collective-permute-start.7) | collective-permute-done | bytes 32800 | tf_op jit(solution)/shard_map/ppermute | solution.py:387
  28.2 2.9 %collective-permute-done.8.refs_1_ = bf16[128,128]{1,0:T(8,128)(2,1)S(1)} collective-permute-done((bf16[128,128]{1,0:T(8,128)(2,1)S(1)}, bf16[128,128]{1,0:T(8,128)(2,1)S(1)}, u32[]{:S(2)}, u32[]{:S(2)}) %collective-permute-start.8) | collective-permute-done | bytes 32800 | tf_op jit(solution)/shard_map/ppermute | solution.py:387
  31.1 0.6 shard_map.111
  31.8 1.3 %collective-permute-start.12 = (bf16[160,128]{1,0:T(8,128)(2,1)S(1)}, bf16[160,128]{1,0:T(8,128)(2,1)S(1)}, u32[]{:S(2)}, u32[]{:S(2)}) collective-permute-start(bf16[160,128]{1,0:T(8,128)(2,1)S(1)} %constant_dynamic-update-slice_fusion), channel_id=1, source_target_pairs={{0,3},{1,2},{2,1},{3,0},{4,7},{5,6},{6,5},{7,4},{8,11},{9,10},{10,... | collective-permute-start | bytes 122888 | tf_op jit(solution)/shard_map/ppermute | solution.py:387
  33.1 0.6 collective-permute-start.11
  33.7 2.5 %collective-permute-start.10 = (bf16[160,128]{1,0:T(8,128)(2,1)S(1)}, bf16[160,128]{1,0:T(8,128)(2,1)S(1)}, u32[]{:S(2)}, u32[]{:S(2)}) collective-permute-start(bf16[160,128]{1,0:T(8,128)(2,1)S(1)} %constant_dynamic-update-slice_fusion), channel_id=1, source_target_pairs={{0,1},{1,0},{2,3},{3,2},{4,5},{5,4},{6,7},{7,6},{8,9},{9,8},{10,11... | collective-permute-start | bytes 122888 | tf_op jit(solution)/shard_map/ppermute | solution.py:387
  36.2 1.4 %collective-permute-done.12 = bf16[160,128]{1,0:T(8,128)(2,1)S(1)} collective-permute-done((bf16[160,128]{1,0:T(8,128)(2,1)S(1)}, bf16[160,128]{1,0:T(8,128)(2,1)S(1)}, u32[]{:S(2)}, u32[]{:S(2)}) %collective-permute-start.12) | collective-permute-done | bytes 40992 | tf_op jit(solution)/shard_map/ppermute | solution.py:387
  37.6 0.5 collective-permute-done.11
  38.5 0.5 collective-permute-start.13
  39.0 1.5 %collective-permute-start.14 = (bf16[512,128]{1,0:T(8,128)(2,1)S(1)}, bf16[512,128]{1,0:T(8,128)(2,1)S(1)}, u32[]{:S(2)}, u32[]{:S(2)}) collective-permute-start(bf16[512,128]{1,0:T(8,128)(2,1)S(1)} %pad_maximum_fusion.refs_0_), channel_id=1, source_target_pairs={{0,16},{8,24},{16,0},{24,8},{1,17},{9,25},{17,1},{25,9},{2,18},{10... | collective-permute-start | bytes 393224 | tf_op jit(solution)/shard_map/ppermute | solution.py:387
  40.5 1.5 %collective-permute-start.15 = (bf16[512,128]{1,0:T(8,128)(2,1)S(1)}, bf16[512,128]{1,0:T(8,128)(2,1)S(1)}, u32[]{:S(2)}, u32[]{:S(2)}) collective-permute-start(bf16[512,128]{1,0:T(8,128)(2,1)S(1)} %pad_maximum_fusion.refs_0_), channel_id=1, source_target_pairs={{0,24},{8,16},{16,8},{24,0},{1,25},{9,17},{17,9},{25,1},{2,26},{10... | collective-permute-start | bytes 393224 | tf_op jit(solution)/shard_map/ppermute | solution.py:387
  42.2 2.4 %collective-permute-start.20 = (bf16[34,128]{1,0:T(8,128)(2,1)S(1)}, bf16[34,128]{1,0:T(8,128)(2,1)S(1)}, u32[]{:S(2)}, u32[]{:S(2)}) collective-permute-start(bf16[34,128]{1,0:T(8,128)(2,1)S(1)} %pad_maximum_fusion.3), channel_id=1, source_target_pairs={{0,4},{4,8},{8,12},{12,16},{16,20},{20,24},{24,28},{1,5},{5,9},{9,... | collective-permute-start | bytes 26120 | tf_op jit(solution)/shard_map/ppermute | solution.py:308
  44.6 0.8 collective-permute-done.20.top_ref
  45.4 1.5 %collective-permute-start.21 = (bf16[34,128]{1,0:T(8,128)(2,1)S(1)}, bf16[34,128]{1,0:T(8,128)(2,1)S(1)}, u32[]{:S(2)}, u32[]{:S(2)}) collective-permute-start(bf16[34,128]{1,0:T(8,128)(2,1)S(1)} %pad_maximum_fusion.4), channel_id=1, source_target_pairs={{4,0},{8,4},{12,8},{16,12},{20,16},{24,20},{28,24},{5,1},{9,5},{13... | collective-permute-start | bytes 26120 | tf_op jit(solution)/shard_map/ppermute | solution.py:308
  46.9 1.2 %collective-permute-start.17 = (bf16[512,128]{1,0:T(8,128)(2,1)S(1)}, bf16[512,128]{1,0:T(8,128)(2,1)S(1)}, u32[]{:S(2)}, u32[]{:S(2)}) collective-permute-start(bf16[512,128]{1,0:T(8,128)(2,1)S(1)} %collective-permute-done.13.refs_1_), channel_id=1, source_target_pairs={{0,4},{4,0},{1,5},{5,1},{2,6},{6,2},{3,7},{7,3},{8,12},{12,8},{9,1... | collective-permute-start | bytes 393224 | tf_op jit(solution)/shard_map/ppermute | solution.py:387
  48.7 1.0 copy-done.5
  49.8 1.5 %shard_map.113 = (f32[2048,128]{1,0:T(8,128)S(1)}, bf16[66,96,128]{2,1,0:T(8,128)(2,1)S(1)}) custom-call(bf16[2048,128]{1,0:T(8,128)(2,1)S(1)} %copy-done.5, bf16[16,128]{1,0:T(8,128)(2,1)S(1)} %get-tuple-element.91.left_ref, bf16[16,128]{1,0:T(8,128)(2,1)S(1)} %get-tuple-element.90.right_ref, bf16[34,128]{1,0:T(8,128)(2,1)S(1)} %collective-permute-done.20.top_ref, ...), custom_call_target="tpu_custom_call" | custom-call | flops 503316480 | bytes 3637248 | tf_op jit(solution)/shard_map/pallas_call | solution.py:39
  51.3 3.3 %shard_map.114 = (bf16[32,64,128]{2,1,0:T(8,128)(2,1)}, bf16[32,64,128]{2,1,0:T(8,128)(2,1)S(1)}, bf16[512,128]{1,0:T(8,128)(2,1)S(1)}, bf16[512,128]{1,0:T(8,12...) custom-call(bf16[512,128]{1,0:T(8,128)(2,1)S(1)} %pad_maximum_fusion, ...), custom_call_target="tpu_custom_call" | custom-call | flops 536870912 | bytes 5242880 | tf_op jit(solution)/shard_map/pallas_call | solution.py:39
  54.7 2.3 %collective-permute-start.26 = (bf16[512,128]{1,0:T(8,128)(2,1)S(1)}, bf16[512,128]{1,0:T(8,128)(2,1)S(1)}, u32[]{:S(2)}, u32[]{:S(2)}) collective-permute-start(bf16[512,128]{1,0:T(8,128)(2,1)S(1)} %get-tuple-element.54), channel_id=1, source_target_pairs={{0,4},{4,0},{1,5},{5,1},{2,6},{6,2},{3,7},{7,3},{8,12},{12,8},{9,1... | collective-permute-start | bytes 393224 | tf_op jit(solution)/shard_map/ppermute | solution.py:387
  57.1 0.5 collective-permute-start.24
  57.7 0.8 shard_map.116
  58.6 3.4 %collective-permute-start.27 = (bf16[512,128]{1,0:T(8,128)(2,1)S(1)}, bf16[512,128]{1,0:T(8,128)(2,1)S(1)}, u32[]{:S(2)}, u32[]{:S(2)}) collective-permute-start(bf16[512,128]{1,0:T(8,128)(2,1)S(1)} %add_convert_fusion.1), channel_id=1, source_target_pairs={{0,8},{8,0},{16,24},{24,16},{1,9},{9,1},{17,25},{25,17},{2,10},{10... | collective-permute-start | bytes 393224 | tf_op jit(solution)/shard_map/ppermute | solution.py:387
  62.2 1.5 %collective-permute-start.23 = (bf16[512,128]{1,0:T(8,128)(2,1)S(1)}, bf16[512,128]{1,0:T(8,128)(2,1)S(1)}, u32[]{:S(2)}, u32[]{:S(2)}) collective-permute-start(bf16[512,128]{1,0:T(8,128)(2,1)S(1)} %add_convert_fusion.3), channel_id=1, source_target_pairs={{0,24},{8,16},{16,8},{24,0},{1,25},{9,17},{17,9},{25,1},{2,26},{10... | collective-permute-start | bytes 393224 | tf_op jit(solution)/shard_map/ppermute | solution.py:387
  63.7 2.4 %collective-permute-done.27 = bf16[512,128]{1,0:T(8,128)(2,1)S(1)} collective-permute-done((bf16[512,128]{1,0:T(8,128)(2,1)S(1)}, bf16[512,128]{1,0:T(8,128)(2,1)S(1)}, u32[]{:S(2)}, u32[]{:S(2)}) %collective-permute-start.27) | collective-permute-done | bytes 131104 | tf_op jit(solution)/shard_map/ppermute | solution.py:387
  66.1 4.4 %collective-permute-done.25 = bf16[512,128]{1,0:T(8,128)(2,1)S(1)} collective-permute-done((bf16[512,128]{1,0:T(8,128)(2,1)S(1)}, bf16[512,128]{1,0:T(8,128)(2,1)S(1)}, u32[]{:S(2)}, u32[]{:S(2)}) %collective-permute-start.25) | collective-permute-done | bytes 131104 | tf_op jit(solution)/shard_map/ppermute | solution.py:387
  70.6 2.4 %collective-permute-start.29 = (bf16[128,128]{1,0:T(8,128)(2,1)S(1)}, bf16[128,128]{1,0:T(8,128)(2,1)S(1)}, u32[]{:S(2)}, u32[]{:S(2)}) collective-permute-start(bf16[128,128]{1,0:T(8,128)(2,1)S(1)} %get-tuple-element.85), channel_id=1, source_target_pairs={{0,3},{1,2},{2,1},{3,0},{4,7},{5,6},{6,5},{7,4},{8,11},{9,10},{10,... | collective-permute-start | bytes 98312 | tf_op jit(solution)/shard_map/ppermute | solution.py:387
  73.0 0.7 collective-permute-start.30
  73.7 1.3 %collective-permute-start.31 = (bf16[128,128]{1,0:T(8,128)(2,1)S(1)}, bf16[128,128]{1,0:T(8,128)(2,1)S(1)}, u32[]{:S(2)}, u32[]{:S(2)}) collective-permute-start(bf16[128,128]{1,0:T(8,128)(2,1)S(1)} %get-tuple-element.83), channel_id=1, source_target_pairs={{0,1},{1,0},{2,3},{3,2},{4,5},{5,4},{6,7},{7,6},{8,9},{9,8},{10,11... | collective-permute-start | bytes 98312 | tf_op jit(solution)/shard_map/ppermute | solution.py:387
  75.0 0.8 shard_map.117
  75.9 0.5 collective-permute-done.29.refs_0_
  76.4 1.6 %collective-permute-done.30.refs_1_ = bf16[128,128]{1,0:T(8,128)(2,1)S(1)} collective-permute-done((bf16[128,128]{1,0:T(8,128)(2,1)S(1)}, bf16[128,128]{1,0:T(8,128)(2,1)S(1)}, u32[]{:S(2)}, u32[]{:S(2)}) %collective-permute-start.30) | collective-permute-done | bytes 32800 | tf_op jit(solution)/shard_map/ppermute | solution.py:387
  78.0 0.7 shard_map.115
  78.7 1.0 %collective-permute-start.32 = (bf16[232,128]{1,0:T(8,128)(2,1)S(1)}, bf16[232,128]{1,0:T(8,128)(2,1)S(1)}, u32[]{:S(2)}, u32[]{:S(2)}) collective-permute-start(bf16[232,128]{1,0:T(8,128)(2,1)S(1)} %pad_maximum_fusion.2), channel_id=1, source_target_pairs={{0,1},{1,0},{2,3},{3,2},{4,5},{5,4},{6,7},{7,6},{8,9},{9,8},{10,11... | collective-permute-start | bytes 178184 | tf_op jit(solution)/shard_map/ppermute | solution.py:387
  79.8 1.3 %collective-permute-start.33 = (bf16[232,128]{1,0:T(8,128)(2,1)S(1)}, bf16[232,128]{1,0:T(8,128)(2,1)S(1)}, u32[]{:S(2)}, u32[]{:S(2)}) collective-permute-start(bf16[232,128]{1,0:T(8,128)(2,1)S(1)} %pad_maximum_fusion.2), channel_id=1, source_target_pairs={{0,2},{1,3},{2,0},{3,1},{4,6},{5,7},{6,4},{7,5},{8,10},{9,11},{10,... | collective-permute-start | bytes 178184 | tf_op jit(solution)/shard_map/ppermute | solution.py:387
  81.0 2.2 %collective-permute-start.34 = (bf16[232,128]{1,0:T(8,128)(2,1)S(1)}, bf16[232,128]{1,0:T(8,128)(2,1)S(1)}, u32[]{:S(2)}, u32[]{:S(2)}) collective-permute-start(bf16[232,128]{1,0:T(8,128)(2,1)S(1)} %pad_maximum_fusion.2), channel_id=1, source_target_pairs={{0,3},{1,2},{2,1},{3,0},{4,7},{5,6},{6,5},{7,4},{8,11},{9,10},{10,... | collective-permute-start | bytes 178184 | tf_op jit(solution)/shard_map/ppermute | solution.py:387
  83.2 1.6 %subtract_multiply_fusion = (f32[32,32,256]{2,1,0:T(8,128)}, f32[32,32,256]{2,1,0:T(8,128)}) fusion(f32[32,256]{1,0:T(8,128)S(1)} %get-tuple-element.66, f32[32,256]{1,0:T(8,128)S(1)} %get-tuple-element.65, f32[32,256]{1,0:T(8,128)S(1)} %get-tuple-element.64, f32[32,256]{1,0:T(8,128)S(1)} %get-tuple-element.63), kind=kLoop, calls=%fused_computation | loop fusion | flops 2097152 | bytes 2228224 | tf_op jit(solution)/shard_map/mul | solution.py:606
  84.8 0.7 collective-permute-done.33
  85.5 1.5 %collective-permute-done.34 = bf16[232,128]{1,0:T(8,128)(2,1)S(1)} collective-permute-done((bf16[232,128]{1,0:T(8,128)(2,1)S(1)}, bf16[232,128]{1,0:T(8,128)(2,1)S(1)}, u32[]{:S(2)}, u32[]{:S(2)}) %collective-permute-start.34) | collective-permute-done | bytes 59424 | tf_op jit(solution)/shard_map/ppermute | solution.py:387
  87.5 1.3 %collective-permute-start.36 = (bf16[584,128]{1,0:T(8,128)(2,1)S(1)}, bf16[584,128]{1,0:T(8,128)(2,1)S(1)}, u32[]{:S(2)}, u32[]{:S(2)}) collective-permute-start(bf16[584,128]{1,0:T(8,128)(2,1)S(1)} %get-tuple-element.72), channel_id=1, source_target_pairs={{0,16},{8,24},{16,0},{24,8},{1,17},{9,25},{17,1},{25,9},{2,18},{10... | collective-permute-start | bytes 448520 | tf_op jit(solution)/shard_map/ppermute | solution.py:387
  88.8 1.8 %collective-permute-start.37 = (bf16[584,128]{1,0:T(8,128)(2,1)S(1)}, bf16[584,128]{1,0:T(8,128)(2,1)S(1)}, u32[]{:S(2)}, u32[]{:S(2)}) collective-permute-start(bf16[584,128]{1,0:T(8,128)(2,1)S(1)} %get-tuple-element.72), channel_id=1, source_target_pairs={{0,24},{8,16},{16,8},{24,0},{1,25},{9,17},{17,9},{25,1},{2,26},{10... | collective-permute-start | bytes 448520 | tf_op jit(solution)/shard_map/ppermute | solution.py:387
  90.9 2.4 %collective-permute-start.42 = (bf16[34,128]{1,0:T(8,128)(2,1)S(1)}, bf16[34,128]{1,0:T(8,128)(2,1)S(1)}, u32[]{:S(2)}, u32[]{:S(2)}) collective-permute-start(bf16[34,128]{1,0:T(8,128)(2,1)S(1)} %pad_maximum_fusion.5), channel_id=1, source_target_pairs={{0,4},{4,8},{8,12},{12,16},{16,20},{20,24},{24,28},{1,5},{5,9},{9,... | collective-permute-start | bytes 26120 | tf_op jit(solution)/shard_map/ppermute | solution.py:308
  93.3 1.3 %collective-permute-start.43 = (bf16[34,128]{1,0:T(8,128)(2,1)S(1)}, bf16[34,128]{1,0:T(8,128)(2,1)S(1)}, u32[]{:S(2)}, u32[]{:S(2)}) collective-permute-start(bf16[34,128]{1,0:T(8,128)(2,1)S(1)} %pad_maximum_fusion.6), channel_id=1, source_target_pairs={{4,0},{8,4},{12,8},{16,12},{20,16},{24,20},{28,24},{5,1},{9,5},{13... | collective-permute-start | bytes 26120 | tf_op jit(solution)/shard_map/ppermute | solution.py:308
  94.9 1.0 collective-permute-start.44
  95.9 0.5 collective-permute-done.43.low_ref
  96.4 1.8 %shard_map.118 = (f32[2048,128]{1,0:T(8,128)S(1)}, bf16[66,96,128]{2,1,0:T(8,128)(2,1)}) custom-call(bf16[2048,128]{1,0:T(8,128)(2,1)S(1)} %get-tuple-element.61.grad_ref.turned_ref, bf16[16,128]{1,0:T(8,128)(2,1)S(1)} %get-tuple-element.79.left_ref, bf16[16,128]{1,0:T(8,128)(2,1)S(1)} %get-tuple-element.78.right_ref, ...), custom_call_target="tpu_custom_call" | custom-call | flops 503316480 | bytes 3637248 | tf_op jit(solution)/shard_map/pallas_call | solution.py:39
  98.2 2.0 %collective-permute-start.39 = (bf16[512,128]{1,0:T(8,128)(2,1)S(1)}, bf16[512,128]{1,0:T(8,128)(2,1)S(1)}, u32[]{:S(2)}, u32[]{:S(2)}) collective-permute-start(bf16[512,128]{1,0:T(8,128)(2,1)S(1)} %slice.241.refs_1_), channel_id=1, source_target_pairs={{0,4},{4,0},{1,5},{5,1},{2,6},{6,2},{3,7},{7,3},{8,12},{12,8},{9,1... | collective-permute-start | bytes 393224 | tf_op jit(solution)/shard_map/ppermute | solution.py:387
  100.3 0.6 collective-permute-start.41
  101.0 0.8 copy.24
  101.8 1.6 %shard_map.119 = bf16[32,64,128]{2,1,0:T(8,128)(2,1)} custom-call(bf16[512,128]{1,0:T(8,128)(2,1)S(1)} %pad_maximum_fusion.1.refs_0_, bf16[512,128]{1,0:T(8,128)(2,1)S(1)} %slice.241.refs_1_, bf16[512,128]{1,0:T(8,128)(2,1)S(1)} %slice.242.refs_2_, bf16[512,128]{1,0:T(8,128)(2,1)S(1)} %slice.243.refs_3_, ...), custom_call_target="tpu_custom_call" | custom-call | flops 268435456 | bytes 3145728 | tf_op jit(solution)/shard_map/pallas_call | solution.py:39
  (118 shorter events, 4.5 us)
Async XLA Ops:
  0.6 4.1 %copy-start = (bf16[32,64,128]{2,1,0:T(8,128)(2,1)S(1)}, bf16[32,64,128]{2,1,0:T(8,128)(2,1)}, u32[]{:S(2)}) copy-start(bf16[32,64,128]{2,1,0:T(8,128)(2,1)} %cells_ref.1) | copy-start | bytes 1572868
  0.6 5.7 %copy-start.6 = (bf16[3,3,32,32]{3,2,1,0:T(8,128)(2,1)S(1)}, bf16[3,3,32,32]{3,2,1,0:T(8,128)(2,1)}, u32[]{:S(2)}) copy-start(bf16[3,3,32,32]{3,2,1,0:T(8,128)(2,1)} %param.11) | copy-start | bytes 55300
  3.5 12.4 %collective-permute-start.6 = (bf16[512,128]{1,0:T(8,128)(2,1)S(1)}, bf16[512,128]{1,0:T(8,128)(2,1)}, u32[]{:S(2)}, u32[]{:S(2)}) collective-permute-start(bf16[512,128]{1,0:T(8,128)(2,1)S(1)} %get-tuple-element.43), channel_id=1, source_target_pairs={{0,4},{4,0},{1,5},{5,1},{2,6},{6,2},{3,7},{7,3},{8,12},{12,8},{9,1... | collective-permute-start | bytes 393224 | tf_op jit(solution)/shard_map/ppermute | solution.py:387
  4.1 4.2 %collective-permute-start.4 = (bf16[512,128]{1,0:T(8,128)(2,1)S(1)}, bf16[512,128]{1,0:T(8,128)(2,1)}, u32[]{:S(2)}, u32[]{:S(2)}) collective-permute-start(bf16[512,128]{1,0:T(8,128)(2,1)S(1)} %get-tuple-element.41), channel_id=1, source_target_pairs={{0,4},{4,0},{1,5},{5,1},{2,6},{6,2},{3,7},{7,3},{8,12},{12,8},{9,1... | collective-permute-start | bytes 393224 | tf_op jit(solution)/shard_map/ppermute | solution.py:387
  4.2 8.0 %collective-permute-start.2 = (bf16[512,128]{1,0:T(8,128)(2,1)S(1)}, bf16[512,128]{1,0:T(8,128)(2,1)}, u32[]{:S(2)}, u32[]{:S(2)}) collective-permute-start(bf16[512,128]{1,0:T(8,128)(2,1)S(1)} %get-tuple-element.39), channel_id=1, source_target_pairs={{0,4},{4,0},{1,5},{5,1},{2,6},{6,2},{3,7},{7,3},{8,12},{12,8},{9,1... | collective-permute-start | bytes 393224 | tf_op jit(solution)/shard_map/ppermute | solution.py:387
  4.6 10.1 %collective-permute-start = (bf16[512,128]{1,0:T(8,128)(2,1)S(1)}, bf16[512,128]{1,0:T(8,128)(2,1)S(1)}, u32[]{:S(2)}, u32[]{:S(2)}) collective-permute-start(bf16[512,128]{1,0:T(8,128)(2,1)S(1)} %get-tuple-element.37), channel_id=1, source_target_pairs={{0,4},{4,0},{1,5},{5,1},{2,6},{6,2},{3,7},{7,3},{8,12},{12,8},{9,1... | collective-permute-start | bytes 393224 | tf_op jit(solution)/shard_map/ppermute | solution.py:387
  5.5 0.8 copy-start.4
  7.2 23.9 %copy-start.1 = (bf16[32,32,256]{2,1,0:T(8,128)(2,1)S(1)}, bf16[32,32,256]{2,1,0:T(8,128)(2,1)}, u32[]{:S(2)}) copy-start(bf16[32,32,256]{2,1,0:T(8,128)(2,1)} %refs_4_.3) | copy-start | bytes 1572868
  7.2 23.9 %copy-start.2 = (bf16[32,32,256]{2,1,0:T(8,128)(2,1)S(1)}, bf16[32,32,256]{2,1,0:T(8,128)(2,1)}, u32[]{:S(2)}) copy-start(bf16[32,32,256]{2,1,0:T(8,128)(2,1)} %refs_5_.3) | copy-start | bytes 1572868
  9.2 6.7 %collective-permute-start.5 = (bf16[512,128]{1,0:T(8,128)(2,1)S(1)}, bf16[512,128]{1,0:T(8,128)(2,1)S(1)}, u32[]{:S(2)}, u32[]{:S(2)}) collective-permute-start(bf16[512,128]{1,0:T(8,128)(2,1)S(1)} %add_convert_fusion.5), channel_id=1, source_target_pairs={{0,8},{8,0},{16,24},{24,16},{1,9},{9,1},{17,25},{25,17},{2,10},{10... | collective-permute-start | bytes 393224 | tf_op jit(solution)/shard_map/ppermute | solution.py:387
  13.1 8.2 %collective-permute-start.3 = (bf16[512,128]{1,0:T(8,128)(2,1)S(1)}, bf16[512,128]{1,0:T(8,128)(2,1)}, u32[]{:S(2)}, u32[]{:S(2)}) collective-permute-start(bf16[512,128]{1,0:T(8,128)(2,1)S(1)} %add_convert_fusion.6), channel_id=1, source_target_pairs={{0,16},{8,24},{16,0},{24,8},{1,17},{9,25},{17,1},{25,9},{2,18},{10... | collective-permute-start | bytes 393224 | tf_op jit(solution)/shard_map/ppermute | solution.py:387
  14.8 6.6 %collective-permute-start.1 = (bf16[512,128]{1,0:T(8,128)(2,1)S(1)}, bf16[512,128]{1,0:T(8,128)(2,1)S(1)}, u32[]{:S(2)}, u32[]{:S(2)}) collective-permute-start(bf16[512,128]{1,0:T(8,128)(2,1)S(1)} %add_convert_fusion.7), channel_id=1, source_target_pairs={{0,24},{8,16},{16,8},{24,0},{1,25},{9,17},{17,9},{25,1},{2,26},{10... | collective-permute-start | bytes 393224 | tf_op jit(solution)/shard_map/ppermute | solution.py:387
  22.4 5.8 %collective-permute-start.7 = (bf16[128,128]{1,0:T(8,128)(2,1)S(1)}, bf16[128,128]{1,0:T(8,128)(2,1)S(1)}, u32[]{:S(2)}, u32[]{:S(2)}) collective-permute-start(bf16[128,128]{1,0:T(8,128)(2,1)S(1)} %get-tuple-element.89), channel_id=1, source_target_pairs={{0,3},{1,2},{2,1},{3,0},{4,7},{5,6},{6,5},{7,4},{8,11},{9,10},{10,... | collective-permute-start | bytes 98312 | tf_op jit(solution)/shard_map/ppermute | solution.py:387
  26.1 5.0 %collective-permute-start.8 = (bf16[128,128]{1,0:T(8,128)(2,1)S(1)}, bf16[128,128]{1,0:T(8,128)(2,1)S(1)}, u32[]{:S(2)}, u32[]{:S(2)}) collective-permute-start(bf16[128,128]{1,0:T(8,128)(2,1)S(1)} %get-tuple-element.88), channel_id=1, source_target_pairs={{0,2},{1,3},{2,0},{3,1},{4,6},{5,7},{6,4},{7,5},{8,10},{9,11},{10,... | collective-permute-start | bytes 98312 | tf_op jit(solution)/shard_map/ppermute | solution.py:387
  26.1 5.0 %collective-permute-start.9 = (bf16[128,128]{1,0:T(8,128)(2,1)S(1)}, bf16[128,128]{1,0:T(8,128)(2,1)S(1)}, u32[]{:S(2)}, u32[]{:S(2)}) collective-permute-start(bf16[128,128]{1,0:T(8,128)(2,1)S(1)} %get-tuple-element.87), channel_id=1, source_target_pairs={{0,1},{1,0},{2,3},{3,2},{4,5},{5,4},{6,7},{7,6},{8,9},{9,8},{10,11... | collective-permute-start | bytes 98312 | tf_op jit(solution)/shard_map/ppermute | solution.py:387
  31.7 19.6 %copy-start.3 = (bf16[32,64,128]{2,1,0:T(8,128)(2,1)S(1)}, bf16[32,64,128]{2,1,0:T(8,128)(2,1)}, u32[]{:S(2)}) copy-start(bf16[32,64,128]{2,1,0:T(8,128)(2,1)} %refs_9_.1) | copy-start | bytes 1572868
  31.8 5.9 %collective-permute-start.12 = (bf16[160,128]{1,0:T(8,128)(2,1)S(1)}, bf16[160,128]{1,0:T(8,128)(2,1)S(1)}, u32[]{:S(2)}, u32[]{:S(2)}) collective-permute-start(bf16[160,128]{1,0:T(8,128)(2,1)S(1)} %constant_dynamic-update-slice_fusion), channel_id=1, source_target_pairs={{0,3},{1,2},{2,1},{3,0},{4,7},{5,6},{6,5},{7,4},{8,11},{9,10},{10,... | collective-permute-start | bytes 122888 | tf_op jit(solution)/shard_map/ppermute | solution.py:387
  33.1 5.0 %collective-permute-start.11 = (bf16[160,128]{1,0:T(8,128)(2,1)S(1)}, bf16[160,128]{1,0:T(8,128)(2,1)S(1)}, u32[]{:S(2)}, u32[]{:S(2)}) collective-permute-start(bf16[160,128]{1,0:T(8,128)(2,1)S(1)} %constant_dynamic-update-slice_fusion), channel_id=1, source_target_pairs={{0,2},{1,3},{2,0},{3,1},{4,6},{5,7},{6,4},{7,5},{8,10},{9,11},{10,... | collective-permute-start | bytes 122888 | tf_op jit(solution)/shard_map/ppermute | solution.py:387
  33.7 4.8 %collective-permute-start.10 = (bf16[160,128]{1,0:T(8,128)(2,1)S(1)}, bf16[160,128]{1,0:T(8,128)(2,1)S(1)}, u32[]{:S(2)}, u32[]{:S(2)}) collective-permute-start(bf16[160,128]{1,0:T(8,128)(2,1)S(1)} %constant_dynamic-update-slice_fusion), channel_id=1, source_target_pairs={{0,1},{1,0},{2,3},{3,2},{4,5},{5,4},{6,7},{7,6},{8,9},{9,8},{10,11... | collective-permute-start | bytes 122888 | tf_op jit(solution)/shard_map/ppermute | solution.py:387
  38.5 8.4 %collective-permute-start.13 = (bf16[512,128]{1,0:T(8,128)(2,1)S(1)}, bf16[512,128]{1,0:T(8,128)(2,1)S(1)}, u32[]{:S(2)}, u32[]{:S(2)}) collective-permute-start(bf16[512,128]{1,0:T(8,128)(2,1)S(1)} %pad_maximum_fusion.refs_0_), channel_id=1, source_target_pairs={{0,8},{8,0},{16,24},{24,16},{1,9},{9,1},{17,25},{25,17},{2,10},{10... | collective-permute-start | bytes 393224 | tf_op jit(solution)/shard_map/ppermute | solution.py:387
  39.0 9.1 %collective-permute-start.14 = (bf16[512,128]{1,0:T(8,128)(2,1)S(1)}, bf16[512,128]{1,0:T(8,128)(2,1)S(1)}, u32[]{:S(2)}, u32[]{:S(2)}) collective-permute-start(bf16[512,128]{1,0:T(8,128)(2,1)S(1)} %pad_maximum_fusion.refs_0_), channel_id=1, source_target_pairs={{0,16},{8,24},{16,0},{24,8},{1,17},{9,25},{17,1},{25,9},{2,18},{10... | collective-permute-start | bytes 393224 | tf_op jit(solution)/shard_map/ppermute | solution.py:387
  40.5 7.7 %collective-permute-start.15 = (bf16[512,128]{1,0:T(8,128)(2,1)S(1)}, bf16[512,128]{1,0:T(8,128)(2,1)S(1)}, u32[]{:S(2)}, u32[]{:S(2)}) collective-permute-start(bf16[512,128]{1,0:T(8,128)(2,1)S(1)} %pad_maximum_fusion.refs_0_), channel_id=1, source_target_pairs={{0,24},{8,16},{16,8},{24,0},{1,25},{9,17},{17,9},{25,1},{2,26},{10... | collective-permute-start | bytes 393224 | tf_op jit(solution)/shard_map/ppermute | solution.py:387
  42.1 9.2 %collective-permute-start.16 = (bf16[512,128]{1,0:T(8,128)(2,1)S(1)}, bf16[512,128]{1,0:T(8,128)(2,1)S(1)}, u32[]{:S(2)}, u32[]{:S(2)}) collective-permute-start(bf16[512,128]{1,0:T(8,128)(2,1)S(1)} %pad_maximum_fusion.refs_0_), channel_id=1, source_target_pairs={{0,4},{4,0},{1,5},{5,1},{2,6},{6,2},{3,7},{7,3},{8,12},{12,8},{9,1... | collective-permute-start | bytes 393224 | tf_op jit(solution)/shard_map/ppermute | solution.py:387
  42.2 3.2 %collective-permute-start.20 = (bf16[34,128]{1,0:T(8,128)(2,1)S(1)}, bf16[34,128]{1,0:T(8,128)(2,1)S(1)}, u32[]{:S(2)}, u32[]{:S(2)}) collective-permute-start(bf16[34,128]{1,0:T(8,128)(2,1)S(1)} %pad_maximum_fusion.3), channel_id=1, source_target_pairs={{0,4},{4,8},{8,12},{12,16},{16,20},{20,24},{24,28},{1,5},{5,9},{9,... | collective-permute-start | bytes 26120 | tf_op jit(solution)/shard_map/ppermute | solution.py:308
  45.4 3.3 %collective-permute-start.21 = (bf16[34,128]{1,0:T(8,128)(2,1)S(1)}, bf16[34,128]{1,0:T(8,128)(2,1)S(1)}, u32[]{:S(2)}, u32[]{:S(2)}) collective-permute-start(bf16[34,128]{1,0:T(8,128)(2,1)S(1)} %pad_maximum_fusion.4), channel_id=1, source_target_pairs={{4,0},{8,4},{12,8},{16,12},{20,16},{24,20},{28,24},{5,1},{9,5},{13... | collective-permute-start | bytes 26120 | tf_op jit(solution)/shard_map/ppermute | solution.py:308
  46.9 4.4 %collective-permute-start.17 = (bf16[512,128]{1,0:T(8,128)(2,1)S(1)}, bf16[512,128]{1,0:T(8,128)(2,1)S(1)}, u32[]{:S(2)}, u32[]{:S(2)}) collective-permute-start(bf16[512,128]{1,0:T(8,128)(2,1)S(1)} %collective-permute-done.13.refs_1_), channel_id=1, source_target_pairs={{0,4},{4,0},{1,5},{5,1},{2,6},{6,2},{3,7},{7,3},{8,12},{12,8},{9,1... | collective-permute-start | bytes 393224 | tf_op jit(solution)/shard_map/ppermute | solution.py:387
  48.1 3.2 %collective-permute-start.18 = (bf16[512,128]{1,0:T(8,128)(2,1)S(1)}, bf16[512,128]{1,0:T(8,128)(2,1)S(1)}, u32[]{:S(2)}, u32[]{:S(2)}) collective-permute-start(bf16[512,128]{1,0:T(8,128)(2,1)S(1)} %collective-permute-done.14.refs_2_), channel_id=1, source_target_pairs={{0,4},{4,0},{1,5},{5,1},{2,6},{6,2},{3,7},{7,3},{8,12},{12,8},{9,1... | collective-permute-start | bytes 393224 | tf_op jit(solution)/shard_map/ppermute | solution.py:387
  48.2 3.1 %collective-permute-start.19 = (bf16[512,128]{1,0:T(8,128)(2,1)S(1)}, bf16[512,128]{1,0:T(8,128)(2,1)S(1)}, u32[]{:S(2)}, u32[]{:S(2)}) collective-permute-start(bf16[512,128]{1,0:T(8,128)(2,1)S(1)} %collective-permute-done.15.refs_3_), channel_id=1, source_target_pairs={{0,4},{4,0},{1,5},{5,1},{2,6},{6,2},{3,7},{7,3},{8,12},{12,8},{9,1... | collective-permute-start | bytes 393224 | tf_op jit(solution)/shard_map/ppermute | solution.py:387
  48.7 1.0 %copy-start.5 = (bf16[2048,128]{1,0:T(8,128)(2,1)S(1)}, bf16[2048,128]{1,0:T(8,128)(2,1)}, u32[]{:S(2)}) copy-start(bf16[2048,128]{1,0:T(8,128)(2,1)} %copy-done.4) | copy-start | bytes 1572868
  54.7 3.9 %collective-permute-start.26 = (bf16[512,128]{1,0:T(8,128)(2,1)S(1)}, bf16[512,128]{1,0:T(8,128)(2,1)S(1)}, u32[]{:S(2)}, u32[]{:S(2)}) collective-permute-start(bf16[512,128]{1,0:T(8,128)(2,1)S(1)} %get-tuple-element.54), channel_id=1, source_target_pairs={{0,4},{4,0},{1,5},{5,1},{2,6},{6,2},{3,7},{7,3},{8,12},{12,8},{9,1... | collective-permute-start | bytes 393224 | tf_op jit(solution)/shard_map/ppermute | solution.py:387
  57.1 6.6 %collective-permute-start.28 = (bf16[512,128]{1,0:T(8,128)(2,1)S(1)}, bf16[512,128]{1,0:T(8,128)(2,1)S(1)}, u32[]{:S(2)}, u32[]{:S(2)}) collective-permute-start(bf16[512,128]{1,0:T(8,128)(2,1)S(1)} %get-tuple-element.56), channel_id=1, source_target_pairs={{0,4},{4,0},{1,5},{5,1},{2,6},{6,2},{3,7},{7,3},{8,12},{12,8},{9,1... | collective-permute-start | bytes 393224 | tf_op jit(solution)/shard_map/ppermute | solution.py:387
  57.1 4.9 %collective-permute-start.24 = (bf16[512,128]{1,0:T(8,128)(2,1)S(1)}, bf16[512,128]{1,0:T(8,128)(2,1)S(1)}, u32[]{:S(2)}, u32[]{:S(2)}) collective-permute-start(bf16[512,128]{1,0:T(8,128)(2,1)S(1)} %get-tuple-element.52), channel_id=1, source_target_pairs={{0,4},{4,0},{1,5},{5,1},{2,6},{6,2},{3,7},{7,3},{8,12},{12,8},{9,1... | collective-permute-start | bytes 393224 | tf_op jit(solution)/shard_map/ppermute | solution.py:387
  57.6 4.5 %collective-permute-start.22 = (bf16[512,128]{1,0:T(8,128)(2,1)S(1)}, bf16[512,128]{1,0:T(8,128)(2,1)S(1)}, u32[]{:S(2)}, u32[]{:S(2)}) collective-permute-start(bf16[512,128]{1,0:T(8,128)(2,1)S(1)} %get-tuple-element.50), channel_id=1, source_target_pairs={{0,4},{4,0},{1,5},{5,1},{2,6},{6,2},{3,7},{7,3},{8,12},{12,8},{9,1... | collective-permute-start | bytes 393224 | tf_op jit(solution)/shard_map/ppermute | solution.py:387
  58.6 7.5 %collective-permute-start.27 = (bf16[512,128]{1,0:T(8,128)(2,1)S(1)}, bf16[512,128]{1,0:T(8,128)(2,1)S(1)}, u32[]{:S(2)}, u32[]{:S(2)}) collective-permute-start(bf16[512,128]{1,0:T(8,128)(2,1)S(1)} %add_convert_fusion.1), channel_id=1, source_target_pairs={{0,8},{8,0},{16,24},{24,16},{1,9},{9,1},{17,25},{25,17},{2,10},{10... | collective-permute-start | bytes 393224 | tf_op jit(solution)/shard_map/ppermute | solution.py:387
  62.0 8.4 %collective-permute-start.25 = (bf16[512,128]{1,0:T(8,128)(2,1)S(1)}, bf16[512,128]{1,0:T(8,128)(2,1)S(1)}, u32[]{:S(2)}, u32[]{:S(2)}) collective-permute-start(bf16[512,128]{1,0:T(8,128)(2,1)S(1)} %add_convert_fusion.2), channel_id=1, source_target_pairs={{0,16},{8,24},{16,0},{24,8},{1,17},{9,25},{17,1},{25,9},{2,18},{10... | collective-permute-start | bytes 393224 | tf_op jit(solution)/shard_map/ppermute | solution.py:387
  62.2 8.3 %collective-permute-start.23 = (bf16[512,128]{1,0:T(8,128)(2,1)S(1)}, bf16[512,128]{1,0:T(8,128)(2,1)S(1)}, u32[]{:S(2)}, u32[]{:S(2)}) collective-permute-start(bf16[512,128]{1,0:T(8,128)(2,1)S(1)} %add_convert_fusion.3), channel_id=1, source_target_pairs={{0,24},{8,16},{16,8},{24,0},{1,25},{9,17},{17,9},{25,1},{2,26},{10... | collective-permute-start | bytes 393224 | tf_op jit(solution)/shard_map/ppermute | solution.py:387
  70.6 5.8 %collective-permute-start.29 = (bf16[128,128]{1,0:T(8,128)(2,1)S(1)}, bf16[128,128]{1,0:T(8,128)(2,1)S(1)}, u32[]{:S(2)}, u32[]{:S(2)}) collective-permute-start(bf16[128,128]{1,0:T(8,128)(2,1)S(1)} %get-tuple-element.85), channel_id=1, source_target_pairs={{0,3},{1,2},{2,1},{3,0},{4,7},{5,6},{6,5},{7,4},{8,11},{9,10},{10,... | collective-permute-start | bytes 98312 | tf_op jit(solution)/shard_map/ppermute | solution.py:387
  73.0 4.9 %collective-permute-start.30 = (bf16[128,128]{1,0:T(8,128)(2,1)S(1)}, bf16[128,128]{1,0:T(8,128)(2,1)S(1)}, u32[]{:S(2)}, u32[]{:S(2)}) collective-permute-start(bf16[128,128]{1,0:T(8,128)(2,1)S(1)} %get-tuple-element.84), channel_id=1, source_target_pairs={{0,2},{1,3},{2,0},{3,1},{4,6},{5,7},{6,4},{7,5},{8,10},{9,11},{10,... | collective-permute-start | bytes 98312 | tf_op jit(solution)/shard_map/ppermute | solution.py:387
  73.7 4.3 %collective-permute-start.31 = (bf16[128,128]{1,0:T(8,128)(2,1)S(1)}, bf16[128,128]{1,0:T(8,128)(2,1)S(1)}, u32[]{:S(2)}, u32[]{:S(2)}) collective-permute-start(bf16[128,128]{1,0:T(8,128)(2,1)S(1)} %get-tuple-element.83), channel_id=1, source_target_pairs={{0,1},{1,0},{2,3},{3,2},{4,5},{5,4},{6,7},{7,6},{8,9},{9,8},{10,11... | collective-permute-start | bytes 98312 | tf_op jit(solution)/shard_map/ppermute | solution.py:387
  78.7 6.1 %collective-permute-start.32 = (bf16[232,128]{1,0:T(8,128)(2,1)S(1)}, bf16[232,128]{1,0:T(8,128)(2,1)S(1)}, u32[]{:S(2)}, u32[]{:S(2)}) collective-permute-start(bf16[232,128]{1,0:T(8,128)(2,1)S(1)} %pad_maximum_fusion.2), channel_id=1, source_target_pairs={{0,1},{1,0},{2,3},{3,2},{4,5},{5,4},{6,7},{7,6},{8,9},{9,8},{10,11... | collective-permute-start | bytes 178184 | tf_op jit(solution)/shard_map/ppermute | solution.py:387
  79.8 5.7 %collective-permute-start.33 = (bf16[232,128]{1,0:T(8,128)(2,1)S(1)}, bf16[232,128]{1,0:T(8,128)(2,1)S(1)}, u32[]{:S(2)}, u32[]{:S(2)}) collective-permute-start(bf16[232,128]{1,0:T(8,128)(2,1)S(1)} %pad_maximum_fusion.2), channel_id=1, source_target_pairs={{0,2},{1,3},{2,0},{3,1},{4,6},{5,7},{6,4},{7,5},{8,10},{9,11},{10,... | collective-permute-start | bytes 178184 | tf_op jit(solution)/shard_map/ppermute | solution.py:387
  81.0 6.0 %collective-permute-start.34 = (bf16[232,128]{1,0:T(8,128)(2,1)S(1)}, bf16[232,128]{1,0:T(8,128)(2,1)S(1)}, u32[]{:S(2)}, u32[]{:S(2)}) collective-permute-start(bf16[232,128]{1,0:T(8,128)(2,1)S(1)} %pad_maximum_fusion.2), channel_id=1, source_target_pairs={{0,3},{1,2},{2,1},{3,0},{4,7},{5,6},{6,5},{7,4},{8,11},{9,10},{10,... | collective-permute-start | bytes 178184 | tf_op jit(solution)/shard_map/ppermute | solution.py:387
  87.0 6.3 %collective-permute-start.35 = (bf16[584,128]{1,0:T(8,128)(2,1)S(1)}, bf16[584,128]{1,0:T(8,128)(2,1)S(1)}, u32[]{:S(2)}, u32[]{:S(2)}) collective-permute-start(bf16[584,128]{1,0:T(8,128)(2,1)S(1)} %get-tuple-element.72), channel_id=1, source_target_pairs={{0,8},{8,0},{16,24},{24,16},{1,9},{9,1},{17,25},{25,17},{2,10},{10... | collective-permute-start | bytes 448520 | tf_op jit(solution)/shard_map/ppermute | solution.py:387
  87.5 7.2 %collective-permute-start.36 = (bf16[584,128]{1,0:T(8,128)(2,1)S(1)}, bf16[584,128]{1,0:T(8,128)(2,1)S(1)}, u32[]{:S(2)}, u32[]{:S(2)}) collective-permute-start(bf16[584,128]{1,0:T(8,128)(2,1)S(1)} %get-tuple-element.72), channel_id=1, source_target_pairs={{0,16},{8,24},{16,0},{24,8},{1,17},{9,25},{17,1},{25,9},{2,18},{10... | collective-permute-start | bytes 448520 | tf_op jit(solution)/shard_map/ppermute | solution.py:387
  88.8 6.1 %collective-permute-start.37 = (bf16[584,128]{1,0:T(8,128)(2,1)S(1)}, bf16[584,128]{1,0:T(8,128)(2,1)S(1)}, u32[]{:S(2)}, u32[]{:S(2)}) collective-permute-start(bf16[584,128]{1,0:T(8,128)(2,1)S(1)} %get-tuple-element.72), channel_id=1, source_target_pairs={{0,24},{8,16},{16,8},{24,0},{1,25},{9,17},{17,9},{25,1},{2,26},{10... | collective-permute-start | bytes 448520 | tf_op jit(solution)/shard_map/ppermute | solution.py:387
  90.6 11.1 %collective-permute-start.38 = (bf16[512,128]{1,0:T(8,128)(2,1)S(1)}, bf16[512,128]{1,0:T(8,128)(2,1)S(1)}, u32[]{:S(2)}, u32[]{:S(2)}) collective-permute-start(bf16[512,128]{1,0:T(8,128)(2,1)S(1)} %pad_maximum_fusion.1.refs_0_), channel_id=1, source_target_pairs={{0,4},{4,0},{1,5},{5,1},{2,6},{6,2},{3,7},{7,3},{8,12},{12,8},{9,1... | collective-permute-start | bytes 393224 | tf_op jit(solution)/shard_map/ppermute | solution.py:387
  90.9 5.0 %collective-permute-start.42 = (bf16[34,128]{1,0:T(8,128)(2,1)S(1)}, bf16[34,128]{1,0:T(8,128)(2,1)S(1)}, u32[]{:S(2)}, u32[]{:S(2)}) collective-permute-start(bf16[34,128]{1,0:T(8,128)(2,1)S(1)} %pad_maximum_fusion.5), channel_id=1, source_target_pairs={{0,4},{4,8},{8,12},{12,16},{16,20},{20,24},{24,28},{1,5},{5,9},{9,... | collective-permute-start | bytes 26120 | tf_op jit(solution)/shard_map/ppermute | solution.py:308
  93.3 3.1 %collective-permute-start.43 = (bf16[34,128]{1,0:T(8,128)(2,1)S(1)}, bf16[34,128]{1,0:T(8,128)(2,1)S(1)}, u32[]{:S(2)}, u32[]{:S(2)}) collective-permute-start(bf16[34,128]{1,0:T(8,128)(2,1)S(1)} %pad_maximum_fusion.6), channel_id=1, source_target_pairs={{4,0},{8,4},{12,8},{16,12},{20,16},{24,20},{28,24},{5,1},{9,5},{13... | collective-permute-start | bytes 26120 | tf_op jit(solution)/shard_map/ppermute | solution.py:308
  94.9 6.0 %collective-permute-start.44 = (bf16[72,128]{1,0:T(8,128)(2,1)S(1)}, bf16[72,128]{1,0:T(8,128)(2,1)S(1)}, u32[]{:S(2)}, u32[]{:S(2)}) collective-permute-start(bf16[72,128]{1,0:T(8,128)(2,1)S(1)} %add_convert_fusion.8), channel_id=1, source_target_pairs={{0,4},{4,0},{1,5},{5,1},{2,6},{6,2},{3,7},{7,3},{8,12},{12,8},{9,1... | collective-permute-start | bytes 55304 | tf_op jit(solution)/shard_map/ppermute | solution.py:387
  98.2 3.6 %collective-permute-start.39 = (bf16[512,128]{1,0:T(8,128)(2,1)S(1)}, bf16[512,128]{1,0:T(8,128)(2,1)S(1)}, u32[]{:S(2)}, u32[]{:S(2)}) collective-permute-start(bf16[512,128]{1,0:T(8,128)(2,1)S(1)} %slice.241.refs_1_), channel_id=1, source_target_pairs={{0,4},{4,0},{1,5},{5,1},{2,6},{6,2},{3,7},{7,3},{8,12},{12,8},{9,1... | collective-permute-start | bytes 393224 | tf_op jit(solution)/shard_map/ppermute | solution.py:387
  100.2 1.5 %collective-permute-start.40 = (bf16[512,128]{1,0:T(8,128)(2,1)S(1)}, bf16[512,128]{1,0:T(8,128)(2,1)S(1)}, u32[]{:S(2)}, u32[]{:S(2)}) collective-permute-start(bf16[512,128]{1,0:T(8,128)(2,1)S(1)} %slice.242.refs_2_), channel_id=1, source_target_pairs={{0,4},{4,0},{1,5},{5,1},{2,6},{6,2},{3,7},{7,3},{8,12},{12,8},{9,1... | collective-permute-start | bytes 393224 | tf_op jit(solution)/shard_map/ppermute | solution.py:387
  100.3 1.5 %collective-permute-start.41 = (bf16[512,128]{1,0:T(8,128)(2,1)S(1)}, bf16[512,128]{1,0:T(8,128)(2,1)S(1)}, u32[]{:S(2)}, u32[]{:S(2)}) collective-permute-start(bf16[512,128]{1,0:T(8,128)(2,1)S(1)} %slice.243.refs_3_), channel_id=1, source_target_pairs={{0,4},{4,0},{1,5},{5,1},{2,6},{6,2},{3,7},{7,3},{8,12},{12,8},{9,1... | collective-permute-start | bytes 393224 | tf_op jit(solution)/shard_map/ppermute | solution.py:387
